TPU v7x, 32 devices: a whole 2x2x4 slice. The times are simulated.
32 devices in a mesh: seq: 8 (over z, core), wide: 4 (over y, x).
Axes of the slice: x: 2, y: 2, z: 4, core: 2. Of those that a mesh axis runs over, the one named last changes fastest.
Arguments:
- inputs: bfloat16 [16, 1024, 768], P('wide', 'seq'), may hold values from -6 to 6
- routes: int32 [16, 1024, 1], P('wide', 'seq'), may hold values from 0 to 7
- bucket_ids: int32 [2047], replicated, may hold values from 0 to 31
- gain_attn: bfloat16 [768], replicated, may hold values from 0.5 to 1.5
- w_query: bfloat16 [768, 768], replicated, may hold values from -0.02734375 to 0.02734375
- w_key: bfloat16 [768, 768], replicated, may hold values from -0.21875 to 0.21875
- w_value: bfloat16 [768, 768], replicated, may hold values from -0.21875 to 0.21875
- w_output: bfloat16 [768, 768], replicated, may hold values from -3.5 to 3.5
- rel_table: bfloat16 [32, 12], replicated, may hold values from -6 to 6
- gain_ffn: bfloat16 [768], replicated, may hold values from 0.5 to 1.5
- w_router: bfloat16 [768, 8], replicated, may hold values from -0.109375 to 0.109375
- w_in: bfloat16 [8, 768, 3072], P('wide'), may hold values from -0.21875 to 0.21875
- w_out: bfloat16 [8, 3072, 768], P('wide'), may hold values from -1.5 to 1.5
- cotangent: bfloat16 [16, 1024, 768], P('wide', 'seq'), may hold values from -6 to 6
Outputs:
- output: bfloat16 [16, 1024, 768], P('wide', 'seq')
- grad_inputs: float32 [16, 1024, 768], P('wide', 'seq')
- grad_gain_attn: float32 [768], P('seq')
- grad_w_query: float32 [768, 768], P('seq')
- grad_w_key: float32 [768, 768], P('seq')
- grad_w_value: float32 [768, 768], P('seq')
- grad_w_output: float32 [768, 768], P('seq')
- grad_rel_table: float32 [32, 12], P('seq')
- grad_gain_ffn: float32 [768], P('seq')
- grad_w_router: float32 [768, 8], P('seq')
- grad_w_in: float32 [8, 768, 3072], P('wide', None, 'seq')
- grad_w_out: float32 [8, 3072, 768], P('wide', 'seq')
Inputs may be any that keep to these rules, and one draw needn't show every extreme that they name: `routes`: each token names one expert.
All inputs are finite; a program needn't handle non-finite values.
Results may differ from a plain program's by a relative error of at most 0.025.
Values may be sent and summed in bfloat16 or wider, within the bound.
A program may use at most 320 MiB of HBM per device.

v0:
```python
import jax
import jax.numpy as jnp
from jax import lax
from jax.sharding import PartitionSpec as P

EPSILON = 1e-06


def norm_forward(source, gain_vec):
    inv_rms = lax.rsqrt(jnp.mean(source * source, axis=-1, keepdims=True) + EPSILON)
    return (source * inv_rms * gain_vec, inv_rms)


def norm_backward(source, inv_rms, gain_vec, upstream):
    scaled = upstream * gain_vec
    gain_grad = jnp.sum(upstream * source * inv_rms, axis=0)
    mean_inner = jnp.mean(source * scaled, axis=-1, keepdims=True)
    return (inv_rms * scaled - source * (inv_rms * inv_rms * inv_rms) * mean_inner, gain_grad)


def smooth_act(values):
    return jax.nn.gelu(values, approximate=True)


def per_device(
    inputs,
    routes,
    bucket_ids,
    gain_attn,
    w_query,
    w_key,
    w_value,
    w_output,
    rel_table,
    gain_ffn,
    w_router,
    w_in,
    w_out,
    cotangent,
):
    seqs_dev, local_len, width = inputs.shape
    bucket_count, head_count = rel_table.shape
    head_size = width // head_count
    full_len = local_len * lax.axis_size("seq")
    experts = w_router.shape[1]
    tok_dev = seqs_dev * local_len
    capacity = (5 * tok_dev + 4 * experts - 1) // (4 * experts)
    slot_count = experts * capacity
    flat_in = inputs.reshape(tok_dev, width).astype(jnp.float32)
    gain_one = gain_attn.astype(jnp.float32)
    normed_pre, scale_one = norm_forward(flat_in, gain_one)
    first_normed_input = normed_pre.astype(jnp.bfloat16)
    projected_query_rows = (
        jnp.dot(first_normed_input, w_query, preferred_element_type=jnp.float32)
        .astype(jnp.bfloat16)
        .reshape(seqs_dev, local_len, width)
    )
    projected_key_rows = (
        jnp.dot(first_normed_input, w_key, preferred_element_type=jnp.float32)
        .astype(jnp.bfloat16)
        .reshape(seqs_dev, local_len, width)
    )
    projected_value_rows = (
        jnp.dot(first_normed_input, w_value, preferred_element_type=jnp.float32)
        .astype(jnp.bfloat16)
        .reshape(seqs_dev, local_len, width)
    )
    all_keys, all_values = (
        lax.all_gather(projected_key_rows, "seq", axis=1, tiled=True),
        lax.all_gather(projected_value_rows, "seq", axis=1, tiled=True),
    )
    first_row = lax.axis_index("seq") * local_len
    local_pos = first_row + jnp.arange(local_len, dtype=jnp.int32)
    every_pos = jnp.arange(full_len, dtype=jnp.int32)
    offsets = every_pos[None, :] - local_pos[:, None] + full_len - 1
    bucket_map = jnp.take(bucket_ids, offsets)
    bucket_hot = (
        bucket_map[None, :, :] == jnp.arange(bucket_count, dtype=jnp.int32)[:, None, None]
    ).astype(jnp.bfloat16)
    rel_bias = jnp.einsum("baj,bh->haj", bucket_hot, rel_table, preferred_element_type=jnp.float32)

    def attend(blocks):
        query_s, keys_s, values_s = blocks
        scores = (
            jnp.einsum(
                "ahd,jhd->haj",
                query_s.reshape(local_len, head_count, head_size),
                keys_s.reshape(full_len, head_count, head_size),
                preferred_element_type=jnp.float32,
            )
            + rel_bias
        )
        row_max = jnp.max(scores, axis=-1, keepdims=True)
        shifted = jnp.exp(scores - row_max)
        row_sum = jnp.sum(shifted, axis=-1, keepdims=True)
        probs_low = (shifted / row_sum).astype(jnp.bfloat16)
        mixed_heads = jnp.einsum(
            "haj,jhd->ahd",
            probs_low,
            values_s.reshape(full_len, head_count, head_size),
            preferred_element_type=jnp.float32,
        )
        return (
            mixed_heads.astype(jnp.bfloat16).reshape(local_len, width),
            (row_max + jnp.log(row_sum))[:, :, 0],
        )

    attention_output, log_total = lax.map(attend, (projected_query_rows, all_keys, all_values))
    flat_att = attention_output.reshape(tok_dev, width)
    middle = flat_in + jnp.dot(flat_att, w_output, preferred_element_type=jnp.float32)
    gain_two = gain_ffn.astype(jnp.float32)
    normed_pre_two, scale_two = norm_forward(middle, gain_two)
    second_normed_input = normed_pre_two.astype(jnp.bfloat16)
    router_probs = jax.nn.softmax(
        jnp.dot(second_normed_input, w_router, preferred_element_type=jnp.float32), axis=-1
    )
    chosen = routes.reshape(tok_dev)
    picked = (chosen[:, None] == jnp.arange(experts, dtype=jnp.int32)[None, :]).astype(jnp.int32)
    earlier = jnp.cumsum(picked, axis=0) - picked
    rank_in = jnp.sum(earlier * picked, axis=1)
    slot_of = jnp.where(rank_in < capacity, chosen * capacity + rank_in, slot_count)
    slot_hot = (slot_of[:, None] == jnp.arange(slot_count, dtype=jnp.int32)[None, :]).astype(
        jnp.bfloat16
    )
    picked_float = picked.astype(jnp.float32)
    gate_prob = jnp.sum(router_probs * picked_float, axis=1)
    packed = (
        jnp.einsum("ts,td->sd", slot_hot, second_normed_input, preferred_element_type=jnp.float32)
        .astype(jnp.bfloat16)
        .reshape(experts, capacity, width)
    )
    received = lax.all_to_all(packed, "wide", split_axis=0, concat_axis=1, tiled=True)
    pre_act = jnp.einsum("erd,edf->erf", received, w_in, preferred_element_type=jnp.float32)
    hidden = smooth_act(pre_act).astype(jnp.bfloat16)
    expert_out = jnp.einsum(
        "erf,efd->erd", hidden, w_out, preferred_element_type=jnp.float32
    ).astype(jnp.bfloat16)
    returned = lax.all_to_all(expert_out, "wide", split_axis=1, concat_axis=0, tiled=True).reshape(
        slot_count, width
    )
    selected = jnp.dot(slot_hot, returned, preferred_element_type=jnp.float32)
    result = middle + gate_prob[:, None] * selected
    output = result.astype(jnp.bfloat16).reshape(inputs.shape)
    upstream = cotangent.reshape(tok_dev, width).astype(jnp.float32)
    grad_gate = jnp.sum(upstream * selected, axis=1)
    weighted = (gate_prob[:, None] * upstream).astype(jnp.bfloat16)
    grad_slot = (
        jnp.einsum("ts,td->sd", slot_hot, weighted, preferred_element_type=jnp.float32)
        .astype(jnp.bfloat16)
        .reshape(experts, capacity, width)
    )
    grad_expert_out = lax.all_to_all(grad_slot, "wide", split_axis=0, concat_axis=1, tiled=True)
    grad_hidden = jnp.einsum(
        "erd,efd->erf", grad_expert_out, w_out, preferred_element_type=jnp.float32
    ).astype(jnp.bfloat16)
    act_pullback = jax.vjp(smooth_act, pre_act)[1]
    grad_pre = act_pullback(grad_hidden.astype(jnp.float32))[0].astype(jnp.bfloat16)
    grad_received = jnp.einsum(
        "erf,edf->erd", grad_pre, w_in, preferred_element_type=jnp.float32
    ).astype(jnp.bfloat16)
    grad_packed = lax.all_to_all(
        grad_received, "wide", split_axis=1, concat_axis=0, tiled=True
    ).reshape(slot_count, width)
    part_in = jnp.einsum("erd,erf->edf", received, grad_pre, preferred_element_type=jnp.float32)
    part_out = jnp.einsum(
        "erf,erd->efd", hidden, grad_expert_out, preferred_element_type=jnp.float32
    )
    grad_w_in, grad_w_out = (
        lax.psum_scatter(
            part_in.astype(jnp.bfloat16), "seq", scatter_dimension=2, tiled=True
        ).astype(jnp.float32),
        lax.psum_scatter(
            part_out.astype(jnp.bfloat16), "seq", scatter_dimension=1, tiled=True
        ).astype(jnp.float32),
    )
    grad_logits = grad_gate[:, None] * router_probs * (picked_float - gate_prob[:, None])
    grad_logits_low = grad_logits.astype(jnp.bfloat16)
    grad_router = jnp.einsum(
        "td,te->de", second_normed_input, grad_logits_low, preferred_element_type=jnp.float32
    )
    grad_normed_two = jnp.dot(
        slot_hot, grad_packed, preferred_element_type=jnp.float32
    ) + jnp.einsum("te,de->td", grad_logits_low, w_router, preferred_element_type=jnp.float32)
    grad_mid_norm, grad_gain_two = norm_backward(middle, scale_two, gain_two, grad_normed_two)
    grad_middle = upstream + grad_mid_norm
    grad_branch = grad_middle.astype(jnp.bfloat16)
    grad_att = jnp.einsum(
        "te,de->td", grad_branch, w_output, preferred_element_type=jnp.float32
    ).astype(jnp.bfloat16)
    grad_w_output = jnp.einsum(
        "td,te->de", flat_att, grad_branch, preferred_element_type=jnp.float32
    )
    keys_back, values_back = (all_keys, all_values)
    grad_att_seq = grad_att.reshape(seqs_dev, local_len, width)

    def attend_back(table_sum, blocks):
        query_s, keys_s, values_s, grad_s, total_s = blocks
        query_h = query_s.reshape(local_len, head_count, head_size)
        keys_h = keys_s.reshape(full_len, head_count, head_size)
        values_h = values_s.reshape(full_len, head_count, head_size)
        grad_h = grad_s.reshape(local_len, head_count, head_size)
        scores = (
            jnp.einsum("ahd,jhd->haj", query_h, keys_h, preferred_element_type=jnp.float32)
            + rel_bias
        )
        attn_probs = jnp.exp(scores - total_s[:, :, None])
        grad_probs = jnp.einsum(
            "ahd,jhd->haj", grad_h, values_h, preferred_element_type=jnp.float32
        )
        row_inner = jnp.sum(attn_probs * grad_probs, axis=-1, keepdims=True)
        grad_scores = (attn_probs * (grad_probs - row_inner)).astype(jnp.bfloat16)
        grad_query = jnp.einsum(
            "haj,jhd->ahd", grad_scores, keys_h, preferred_element_type=jnp.float32
        ).astype(jnp.bfloat16)
        table_sum = table_sum + jnp.einsum(
            "haj,baj->bh", grad_scores, bucket_hot, preferred_element_type=jnp.float32
        )
        return (
            table_sum,
            (
                grad_query.reshape(local_len, width),
                attn_probs,
                grad_scores,
                grad_h,
                query_h,
                row_inner[:, :, 0],
            ),
        )

    table_init = jnp.zeros((bucket_count, head_count), jnp.float32)

    def attend_back_all(table_sum, blocks):
        table_sum, (grad_query, attn_probs, grad_scores, grad_h, query_h, row_inner) = attend_back(
            table_sum, blocks
        )
        grad_values = jnp.einsum(
            "haj,ahd->jhd",
            attn_probs.astype(jnp.bfloat16),
            grad_h,
            preferred_element_type=jnp.float32,
        )
        grad_keys = jnp.einsum(
            "haj,ahd->jhd", grad_scores, query_h, preferred_element_type=jnp.float32
        )
        return (
            table_sum,
            (grad_query, grad_keys.reshape(full_len, width), grad_values.reshape(full_len, width)),
        )

    grad_table, (grad_queries, grad_keys_all, grad_values_all) = lax.scan(
        attend_back_all,
        table_init,
        (projected_query_rows, keys_back, values_back, grad_att_seq, log_total),
    )
    grad_keys_loc, grad_values_loc = (
        lax.psum_scatter(
            grad_keys_all.astype(jnp.bfloat16), "seq", scatter_dimension=1, tiled=True
        ).astype(jnp.float32),
        lax.psum_scatter(
            grad_values_all.astype(jnp.bfloat16), "seq", scatter_dimension=1, tiled=True
        ).astype(jnp.float32),
    )
    grad_q_flat = grad_queries.reshape(tok_dev, width)
    grad_k_flat = grad_keys_loc.astype(jnp.bfloat16).reshape(tok_dev, width)
    grad_v_flat = grad_values_loc.astype(jnp.bfloat16).reshape(tok_dev, width)
    grad_w_query = jnp.einsum(
        "td,te->de", first_normed_input, grad_q_flat, preferred_element_type=jnp.float32
    )
    grad_w_key = jnp.einsum(
        "td,te->de", first_normed_input, grad_k_flat, preferred_element_type=jnp.float32
    )
    grad_w_value = jnp.einsum(
        "td,te->de", first_normed_input, grad_v_flat, preferred_element_type=jnp.float32
    )
    grad_normed_one = jnp.einsum(
        "te,de->td", grad_q_flat, w_query, preferred_element_type=jnp.float32
    )
    grad_normed_one = grad_normed_one + jnp.einsum(
        "te,de->td", grad_k_flat, w_key, preferred_element_type=jnp.float32
    )
    grad_normed_one = grad_normed_one + jnp.einsum(
        "te,de->td", grad_v_flat, w_value, preferred_element_type=jnp.float32
    )
    grad_in_norm, grad_gain_one = norm_backward(flat_in, scale_one, gain_one, grad_normed_one)
    grad_inputs = (grad_middle + grad_in_norm).reshape(inputs.shape)
    (
        shard_query,
        shard_key,
        shard_value,
        shard_output,
        shard_gain_one,
        shard_gain_two,
        shard_table,
        shard_router,
    ) = (
        lax.psum_scatter(
            grad_w_query.astype(jnp.bfloat16), "seq", scatter_dimension=0, tiled=True
        ).astype(jnp.float32),
        lax.psum_scatter(
            grad_w_key.astype(jnp.bfloat16), "seq", scatter_dimension=0, tiled=True
        ).astype(jnp.float32),
        lax.psum_scatter(
            grad_w_value.astype(jnp.bfloat16), "seq", scatter_dimension=0, tiled=True
        ).astype(jnp.float32),
        lax.psum_scatter(
            grad_w_output.astype(jnp.bfloat16), "seq", scatter_dimension=0, tiled=True
        ).astype(jnp.float32),
        lax.psum_scatter(
            grad_gain_one.astype(jnp.bfloat16), "seq", scatter_dimension=0, tiled=True
        ).astype(jnp.float32),
        lax.psum_scatter(
            grad_gain_two.astype(jnp.bfloat16), "seq", scatter_dimension=0, tiled=True
        ).astype(jnp.float32),
        lax.psum_scatter(
            grad_table.astype(jnp.bfloat16), "seq", scatter_dimension=0, tiled=True
        ).astype(jnp.float32),
        lax.psum_scatter(
            grad_router.astype(jnp.bfloat16), "seq", scatter_dimension=0, tiled=True
        ).astype(jnp.float32),
    )
    (
        total_query,
        total_key,
        total_value,
        total_output,
        total_gain_one,
        total_gain_two,
        total_table,
        total_router,
    ) = lax.psum(
        (
            shard_query,
            shard_key,
            shard_value,
            shard_output,
            shard_gain_one,
            shard_gain_two,
            shard_table,
            shard_router,
        ),
        "wide",
    )
    return (
        output,
        grad_inputs,
        total_gain_one,
        total_query,
        total_key,
        total_value,
        total_output,
        total_table,
        total_gain_two,
        total_router,
        grad_w_in,
        grad_w_out,
    )


def solution(mesh):
    in_specs = (
        P("wide", "seq", None),
        P("wide", "seq", None),
        P(),
        P(),
        P(),
        P(),
        P(),
        P(),
        P(),
        P(),
        P(),
        P("wide", None, None),
        P("wide", None, None),
        P("wide", "seq", None),
    )
    out_specs = (
        P("wide", "seq", None),
        P("wide", "seq", None),
        P("seq"),
        P("seq", None),
        P("seq", None),
        P("seq", None),
        P("seq", None),
        P("seq", None),
        P("seq"),
        P("seq", None),
        P("wide", None, "seq"),
        P("wide", "seq", None),
    )
    return jax.shard_map(
        per_device, mesh=mesh, in_specs=in_specs, out_specs=out_specs, check_vma=False
    )
```

profile of v0, /device:TPU:0, one launch (start us, length us, event | category | flops | bytes accessed | tf_op | source)
XLA Modules:
  0.0 1544.4 jit_solution(651951745820064336)
XLA Ops:
  18.5 724.9 %gather_fusion = s32[131072]{0:T(1024)S(1)} fusion(s32[2047]{0:T(1024)S(1)} %copy-done.1, s32[131072]{0:T(1024)S(1)} %broadcast_clamp_fusion), kind=kCustom, calls=%fused_computation | custom fusion | bytes 1572864 | tf_op jit(solution)/shard_map/jit(_take)/gather | solution.py:76
  751.6 6.2 copy.114
  758.6 38.7 %while.29 = (s32[]{:T(128)}, bf16[4,128,768]{2,1,0:T(8,128)(2,1)S(1)}, f32[4,12,128]{2,1,0:T(8,128)}, bf16[4,1024,768]{1,2,0:T(8,128)(2,1)}, bf16[4,128,768]{1,2...) while((s32[]{:T(128)}, bf16[4,128,768]{2,1,0:T(8,128)(2,1)S(1)}, ...), condition=%wide.region_4.5_spmd, body=%wide.region_1.4_spmd.sunk | while | flops 413760000 | bytes 61393032 | solution.py:108
  804.3 5.2 all-to-all-start.2
  811.9 11.1 all-to-all-done.2
  829.5 10.4 all-to-all-done
  841.2 6.2 fusion.84
  847.4 10.3 convolution_convert_fusion.8
  864.4 10.6 fusion.26
  875.0 8.7 convolution_convert_fusion.7
  895.6 6.7 all-to-all-done.3
  908.9 118.7 %while.30 = (s32[]{:T(128)}, f32[32,12]{0,1:T(8,128)S(1)}, bf16[4,128,768]{1,2,0:T(8,128)(2,1)}, bf16[4,1024,768]{2,1,0:T(8,128)(2,1)}, bf16[4,1024,768]{2,1,0:T...) while((s32[]{:T(128)}, f32[32,12]{0,1:T(8,128)S(1)}, ...), condition=%wide.region_16.17_spmd.clone, body=%wide.region_14.16_spmd.clone.sunk | while | flops 1128365312 | bytes 143099232 | solution.py:250
  1038.8 59.1 %reduce-scatter.14.cloned.1.call-done = bf16[4,128,768]{2,1,0:T(8,128)(2,1)} async-done(((bf16[4,1024,768]{2,1,0:T(8,128)(2,1)}), bf16[4,128,768]{2,1,0:T(8,128)(2,1)}) %reduce-scatter.14.cloned.1.call-update) | async-done | bytes 786448 | tf_op jit(solution)/shard_map/reduce_scatter | solution.py:256
  1101.0 67.2 %reduce-scatter.16.cloned.1.call-done = bf16[4,128,768]{2,1,0:T(8,128)(2,1)} async-done(((bf16[4,1024,768]{2,1,0:T(8,128)(2,1)}), bf16[4,128,768]{2,1,0:T(8,128)(2,1)}) %reduce-scatter.16.cloned.1.call-update) | async-done | bytes 786448 | tf_op jit(solution)/shard_map/reduce_scatter | solution.py:259
  1171.4 10.1 convolution_convert_fusion.2
  1181.5 23.9 %copy.141 = bf16[2,768,3072]{1,0,2:T(2,128)(2,1)} copy(bf16[2,768,3072]{2,1,0:T(8,128)(2,1)} %convolution_convert_fusion.2) | data formatting | bytes 18874368
  1205.4 9.0 copy.160
  1214.5 10.6 convolution_convert_fusion.1
  1235.5 31.2 %reduce-scatter.18.cloned.1.call-done = bf16[96,768]{1,0:T(8,128)(2,1)} async-done(((bf16[768,768]{1,0:T(8,128)(2,1)}), bf16[96,768]{1,0:T(8,128)(2,1)}) %reduce-scatter.18.cloned.1.call-update) | async-done | bytes 147472 | tf_op jit(solution)/shard_map/reduce_scatter | solution.py:296
  1272.1 26.2 %all-reduce.4 = (bf16[768]{0:T(1024)(128)(2,1)}, bf16[32,12]{1,0:T(8,128)(2,1)}, bf16[768]{0:T(1024)(128)(2,1)}) all-reduce(bf16[768]{0:T(1024)(128)(2,1)} %get-tuple-element.260, bf16[32,12]{1,0:T(8,128)(2,1)S(1)} %copy.134, bf16[768]{0:T(1024)(128)(2,1)} %get-tuple-element.258), channel_id=4, replica_groups=mesh['seq'=8,'wide'=4] {'seq'}, use_global_device_ids=true, to_apply=%region_21.22.clone | all-reduce | flops 1920 | bytes 7680
  1303.9 30.3 %reduce-scatter.22.cloned.1.call-done = bf16[96,768]{1,0:T(8,128)(2,1)} async-done(((bf16[768,768]{1,0:T(8,128)(2,1)}), bf16[96,768]{1,0:T(8,128)(2,1)}) %reduce-scatter.22.cloned.1.call-update) | async-done | bytes 147472 | tf_op jit(solution)/shard_map/reduce_scatter | solution.py:302
  1334.3 45.0 %all-reduce.6 = (f32[96]{0:T(128)}, f32[96,768]{1,0:T(8,128)}, f32[96,768]{1,0:T(8,128)}, f32[96,768]{1,0:T(8,128)}, f32[96,768]{1,0:T(8,128)}, /*index=5*/f32[4,12]{1,0:T(4,128)}, f32[96]{0:T(128)}, f32[96,8]{0,1:T(8,128)}) all-reduce(f32[96]{0:T(128)} %get-tuple-element.334, ...), channel_id=1, replica_groups=mesh['seq'=8,'wide'=4] {'wide'}, use_global_device_ids=true, to_apply=%region_22.23 | all-reduce | flops 295920 | bytes 1776000 | tf_op jit(solution)/shard_map/psum | solution.py:330
  1379.2 55.1 %reduce-scatter.30.cloned.1.call-done = bf16[384,1536]{1,0:T(8,128)(2,1)} async-done(((bf16[3072,1536]{1,0:T(8,128)(2,1)}), bf16[384,1536]{1,0:T(8,128)(2,1)}) %reduce-scatter.30.cloned.1.call-update) | async-done | bytes 1179664
  1440.8 93.9 %reduce-scatter.26.cloned.1.call-done = bf16[2,384,768]{2,1,0:T(8,128)(2,1)} async-done(((bf16[2,3072,768]{2,1,0:T(8,128)(2,1)}), bf16[2,384,768]{2,1,0:T(8,128)(2,1)}) %reduce-scatter.26.cloned.1.call-update) | async-done | bytes 1179664 | tf_op jit(solution)/shard_map/reduce_scatter | solution.py:172
  (396 shorter events, 265.1 us)
Async XLA Ops:
  7.2 6.3 copy-start
  7.2 751.4 %all-gather.5.cloned.1.call-start = ((), (), s32[]{:S(2)}) async-start(), calls=%async_computation.14 | async-start | bytes 7077888 | tf_op jit(solution)/shard_map/all_gather | solution.py:69
  13.5 745.1 %all-gather.3.cloned.1.call-start = ((), (), s32[]{:S(2)}) async-start(), calls=%async_computation.13 | async-start | bytes 7077888 | tf_op jit(solution)/shard_map/all_gather | solution.py:70
  18.5 725.0 %copy-start.25 = (bf16[512,768]{1,0:T(8,128)(2,1)S(1)}, bf16[512,768]{1,0:T(8,128)(2,1)}, u32[]{:S(2)}) copy-start(bf16[512,768]{1,0:T(8,128)(2,1)} %copy-done.24) | copy-start | bytes 2359300
  751.5 6.3 copy-start.27
  751.6 7.0 copy-start.22
  751.6 46.6 %copy-start.10 = (bf16[4,128,768]{2,1,0:T(8,128)(2,1)S(1)}, bf16[4,128,768]{2,1,0:T(8,128)(2,1)}, u32[]{:S(2)}) copy-start(bf16[4,128,768]{2,1,0:T(8,128)(2,1)} %param.18) | copy-start | bytes 2359300
  801.4 8.0 copy-start.13
  804.3 18.7 %all-to-all-start.2 = ((bf16[8,80,768]{2,1,0:T(8,128)(2,1)}), bf16[8,80,768]{2,1,0:T(8,128)(2,1)}, u32[]{:S(2)}, u32[]{:S(2)}) async-start(bf16[8,80,768]{2,1,0:T(8,128)(2,1)} %bitcast.242), calls=%async_computation.2 | async-start | bytes 1966080 | tf_op jit(solution)/shard_map/all_to_all | solution.py:152
  823.0 17.0 %all-to-all-start = ((bf16[8,80,768]{2,1,0:T(8,128)(2,1)}), bf16[8,80,768]{2,1,0:T(8,128)(2,1)}, u32[]{:S(2)}, u32[]{:S(2)}) async-start(bf16[8,80,768]{2,1,0:T(8,128)(2,1)} %bitcast.241), calls=%async_computation | async-start | bytes 1966080 | tf_op jit(solution)/shard_map/all_to_all | solution.py:132
  847.4 10.3 copy-start.7
  859.7 26.0 %all-to-all-start.1 = ((bf16[2,320,768]{2,0,1:T(2,128)(2,1)}), bf16[2,320,768]{2,0,1:T(2,128)(2,1)}, u32[]{:S(2)}, u32[]{:S(2)}) async-start(bf16[2,320,768]{2,0,1:T(2,128)(2,1)} %copy.117), calls=%async_computation.1 | async-start | bytes 1966080 | tf_op jit(solution)/shard_map/all_to_all | solution.py:138
  875.0 8.7 copy-start.68
  885.7 16.7 %all-to-all-start.3 = ((bf16[2,320,768]{2,0,1:T(2,128)(2,1)}), bf16[2,320,768]{2,0,1:T(2,128)(2,1)}, u32[]{:S(2)}, u32[]{:S(2)}) async-start(bf16[2,320,768]{2,0,1:T(2,128)(2,1)} %copy.121), calls=%async_computation.3 | async-start | bytes 1966080 | tf_op jit(solution)/shard_map/all_to_all | solution.py:161
  889.9 208.0 %reduce-scatter.14.cloned.1.call-start = ((), (), s32[]{:S(2)}) async-start(), calls=%async_computation.15 | async-start | bytes 7077888 | tf_op jit(solution)/shard_map/reduce_scatter | solution.py:256
  1028.2 140.0 %reduce-scatter.16.cloned.1.call-start = ((), (), s32[]{:S(2)}) async-start(), calls=%async_computation.16 | async-start | bytes 7077888 | tf_op jit(solution)/shard_map/reduce_scatter | solution.py:259
  1028.8 205.4 %reduce-scatter.28.cloned.1.call-start = ((), (), s32[]{:S(2)}) async-start(), calls=%async_computation.22 | async-start | bytes 221184
  1032.4 203.1 %reduce-scatter.24.cloned.1.call-start = ((), (), s32[]{:S(2)}) async-start(), calls=%async_computation.20 | async-start | bytes 1327104 | tf_op jit(solution)/shard_map/reduce_scatter | solution.py:305
  1035.5 231.2 %reduce-scatter.18.cloned.1.call-start = ((), (), s32[]{:S(2)}) async-start(), calls=%async_computation.17 | async-start | bytes 1327104 | tf_op jit(solution)/shard_map/reduce_scatter | solution.py:296
  1038.8 265.2 %reduce-scatter.20.cloned.1.call-start = ((), (), s32[]{:S(2)}) async-start(), calls=%async_computation.18 | async-start | bytes 1327104 | tf_op jit(solution)/shard_map/reduce_scatter | solution.py:299
  1101.0 233.3 %reduce-scatter.22.cloned.1.call-start = ((), (), s32[]{:S(2)}) async-start(), calls=%async_computation.19 | async-start | bytes 1327104 | tf_op jit(solution)/shard_map/reduce_scatter | solution.py:302
  1171.3 263.0 %reduce-scatter.30.cloned.1.call-start = ((), (), s32[]{:S(2)}) async-start(), calls=%async_computation.23 | async-start | bytes 10616832
  1214.4 320.2 %reduce-scatter.26.cloned.1.call-start = ((), (), s32[]{:S(2)}) async-start(), calls=%async_computation.21 | async-start | bytes 10616832 | tf_op jit(solution)/shard_map/reduce_scatter | solution.py:172
  1301.0 33.3 %copy-start.56 = (bf16[96,8]{0,1:T(8,128)(2,1)S(1)}, bf16[96,8]{0,1:T(8,128)(2,1)}, u32[]{:S(2)}) copy-start(bf16[96,8]{0,1:T(8,128)(2,1)} %copy.140) | copy-start | bytes 4612
  (84 other events, 205.6 us)
Sparse Core Ops, SparseCore 0:
  13.6 67.8 all-gather.4
  83.7 63.3 all-gather.2
  1027.7 70.0 reduce-scatter.13
  1100.1 68.1 reduce-scatter.15
  1170.9 28.6 reduce-scatter.27
  1201.9 30.9 reduce-scatter.23
  1235.9 30.7 reduce-scatter.17
  1269.7 31.3 reduce-scatter.19
  1303.4 30.7 reduce-scatter.21
  1336.5 97.7 reduce-scatter.29
  1436.7 97.8 reduce-scatter.25
where the time goes:
time: 1560 us; the launch traced here: 1540 us
  local copies, waits for them, and re-layouts  879 us (56%)
  waiting for transfers between devices  366 us (23%)
  matrix products  162 us (10%)
  blocking collectives  71.2 us (5%)
  other arithmetic  30.4 us (2%)
  starting transfers between devices  18.7 us (1%)
  between operations  16.4 us (1%)
    gather x2, local copies, waits for them, and re-layouts, per_device(): bucket_map = jnp.take(bucket_ids, offsets)  725 us
    reduce_scatter x1, waiting for transfers between devices, per_device(): lax.psum_scatter(part_out.astype(jnp.bfloat16), 'seq', scatter_dimension=...  93.9 us
    reduce_scatter x1, waiting for transfers between devices, per_device(): lax.psum_scatter(grad_values_all.astype(jnp.bfloat16), 'seq', scatter_dim...  67.2 us
    reduce_scatter x1, waiting for transfers between devices, per_device(): lax.psum_scatter(grad_keys_all.astype(jnp.bfloat16), 'seq', scatter_dimen...  59.1 us
    unnamed x13, waiting for transfers between devices  55.8 us
    unnamed x136, local copies, waits for them, and re-layouts  46.1 us
    psum x1, blocking collectives, per_device(): lax.psum((shard_query, shard_key, shard_value, shard_output, shard_gain_o...  45 us
    dynamic_slice x28, local copies, waits for them, and re-layouts, per_device(): lax.map(attend, (projected_query_rows, all_keys, all_values))  34.4 us
  transfers between devices with their start and end apart: 15, of which 9 were waited for; matrix products, arithmetic and copies ran while one was open for 56% of the time, Pallas kernels for 0%

commit v1 on v0

v1 whole, which is shorter than its diff:
```python
import functools

import jax
import jax.numpy as jnp
from jax import lax
from jax.experimental import pallas as pl
from jax.experimental.pallas import tpu as pltpu
from jax.sharding import PartitionSpec as P

EPSILON = 1e-06
F32 = jnp.float32
BF16 = jnp.bfloat16
LANES = 128


def contract(a, b, da, db):
    return lax.dot_general(a, b, (((da,), (db,)), ((), ())), preferred_element_type=F32)


def inverse_rms(source):
    return lax.rsqrt(jnp.mean(source * source, axis=-1, keepdims=True) + EPSILON)


def norm_backward(source, inv_rms, gain_vec, upstream):
    scaled = upstream * gain_vec
    gain_grad = jnp.sum(upstream * source * inv_rms, axis=0)
    mean_inner = jnp.mean(source * scaled, axis=-1, keepdims=True)
    return (inv_rms * scaled - source * (inv_rms * inv_rms * inv_rms) * mean_inner, gain_grad)


def smooth_act(values):
    return jax.nn.gelu(values, approximate=True)


def attend_kernel(length, width, q_ref, k_ref, v_ref, bias_ref, out_ref, exp_ref, inv_ref, strip, keys, scores):
    block = pl.program_id(1)
    rows = 2 * length - LANES

    @pl.when(block == 0)
    def _():
        keys[...] = k_ref[...].T
        for b in range(rows // LANES):
            start = 2 * length - 2 * LANES - LANES * b
            base = jnp.broadcast_to(bias_ref[0, :, start : start + 2 * LANES], (LANES, 2 * LANES))
            rolled = pltpu.roll(base, 0, 1, stride=1, stride_axis=0)
            strip[LANES * b : LANES * (b + 1), :] = rolled[:, LANES:]

    chunk = 256
    subs = width // LANES
    tops = [jnp.full((1, LANES), -jnp.inf, F32)] * subs
    for c in range(length // chunk):
        part = contract(keys[c * chunk : (c + 1) * chunk, :], q_ref[...], 1, 0)
        for s in range(subs):
            row = pl.multiple_of(length - LANES - (block * width + s * LANES) + c * chunk, LANES)
            piece = part[:, s * LANES : (s + 1) * LANES] + strip[pl.ds(row, chunk), :]
            scores[c * chunk : (c + 1) * chunk, s * LANES : (s + 1) * LANES] = piece
            tops[s] = jnp.maximum(tops[s], jnp.max(piece, axis=0, keepdims=True))
    sums = [jnp.zeros((1, LANES), F32)] * subs
    for c in range(length // chunk):
        for s in range(subs):
            piece = scores[c * chunk : (c + 1) * chunk, s * LANES : (s + 1) * LANES]
            grown = jnp.exp(piece - tops[s])
            sums[s] = sums[s] + jnp.sum(grown, axis=0, keepdims=True)
            exp_ref[0, c * chunk : (c + 1) * chunk, s * LANES : (s + 1) * LANES] = grown.astype(BF16)
    mixed = contract(v_ref[...], exp_ref[0], 1, 0)
    for s in range(subs):
        inverse = 1.0 / sums[s]
        inv_ref[0, :, s * LANES : (s + 1) * LANES] = inverse
        out_ref[s] = (mixed[:, s * LANES : (s + 1) * LANES] * inverse).astype(BF16)


def attend_back_kernel(
    length, width, exp_ref, inv_ref, grad_ref, out_ref, q_ref, k_ref, v_ref, dq_ref, dk_ref, dv_ref, diag_ref, strip, values, dk_sum, dv_sum, scores
):
    block = pl.program_id(1)
    rows = 2 * length - LANES
    subs = width // LANES

    @pl.when(block == 0)
    def _():
        values[...] = v_ref[...].T
        strip[...] = jnp.zeros_like(strip)
        dk_sum[...] = jnp.zeros_like(dk_sum)
        dv_sum[...] = jnp.zeros_like(dv_sum)

    grads, inner = [], []
    for s in range(subs):
        inverse = inv_ref[0, :, s * LANES : (s + 1) * LANES]
        scaled = grad_ref[s].astype(F32) * inverse
        inner.append(jnp.sum(scaled * out_ref[s].astype(F32), axis=0, keepdims=True))
        grads.append(scaled.astype(BF16))
    grad = jnp.concatenate(grads, axis=1) if subs > 1 else grads[0]
    chunk = 256
    for c in range(length // chunk):
        part = contract(values[c * chunk : (c + 1) * chunk, :], grad, 1, 0)
        for s in range(subs):
            grown = exp_ref[0, c * chunk : (c + 1) * chunk, s * LANES : (s + 1) * LANES].astype(F32)
            slope = grown * (part[:, s * LANES : (s + 1) * LANES] - inner[s])
            row = pl.multiple_of(length - LANES - (block * width + s * LANES) + c * chunk, LANES)
            strip[pl.ds(row, chunk), :] += slope
            scores[c * chunk : (c + 1) * chunk, s * LANES : (s + 1) * LANES] = slope.astype(BF16)
    dq_ref[...] = contract(k_ref[...], scores[...], 1, 0).astype(BF16)
    dk_sum[...] += contract(scores[...], q_ref[...].T, 1, 0)
    dv_sum[...] += contract(exp_ref[0], grad.T, 1, 0)

    @pl.when(block == pl.num_programs(1) - 1)
    def _():
        dk_ref[...] = dk_sum[...].T.astype(BF16)
        dv_ref[...] = dv_sum[...].T.astype(BF16)
        diag_ref[...] = jnp.zeros_like(diag_ref)
        down = lax.broadcasted_iota(jnp.int32, (LANES, LANES), 0)
        over = lax.broadcasted_iota(jnp.int32, (LANES, LANES), 1)
        mirror = (down + over == LANES - 1).astype(F32)
        for b in range(rows // LANES):
            held = lax.dot_general(
                strip[LANES * b : LANES * (b + 1), :],
                mirror,
                (((1,), (0,)), ((), ())),
                precision=lax.Precision.HIGHEST,
                preferred_element_type=F32,
            )
            spread = jnp.concatenate([held, jnp.zeros_like(held)], axis=1)
            rolled = pltpu.roll(spread, 0, 1, stride=1, stride_axis=0)
            diag_ref[0, :, LANES * b : LANES * (b + 2)] += jnp.sum(rolled, axis=0, keepdims=True)


def attention_specs(heads, size, length, width):
    subs = width // LANES
    return dict(
        query=pl.BlockSpec((size, width), lambda h, b: (h, b)),
        key=pl.BlockSpec((size, length), lambda h, b: (heads + h, 0)),
        value=pl.BlockSpec((size, length), lambda h, b: (2 * heads + h, 0)),
        whole=pl.BlockSpec((size, length), lambda h, b: (h, 0)),
        line=pl.BlockSpec((1, 1, 2 * length), lambda h, b: (h, 0, 0)),
        exps=pl.BlockSpec((1, length, width), lambda h, b: (h, 0, b)),
        inv=pl.BlockSpec((1, 1, width), lambda h, b: (h, 0, b)),
        tokens=pl.BlockSpec((subs, size, LANES), lambda h, b: (b, h, 0)),
    )


def attend(qkv, bias_line, heads, size, length, width):
    spec = attention_specs(heads, size, length, width)
    return pl.pallas_call(
        functools.partial(attend_kernel, length, width),
        grid=(heads, length // width),
        in_specs=[spec["query"], spec["key"], spec["value"], spec["line"]],
        out_specs=[spec["tokens"], spec["exps"], spec["inv"]],
        out_shape=[
            jax.ShapeDtypeStruct((length // LANES, heads * size, LANES), BF16),
            jax.ShapeDtypeStruct((heads, length, length), BF16),
            jax.ShapeDtypeStruct((heads, 1, length), F32),
        ],
        scratch_shapes=[
            pltpu.VMEM((2 * length - LANES, LANES), F32),
            pltpu.VMEM((length, size), BF16),
            pltpu.VMEM((length, width), F32),
        ],
        compiler_params=pltpu.CompilerParams(vmem_limit_bytes=40 << 20),
        cost_estimate=pl.CostEstimate(
            flops=4 * heads * length * length * size, bytes_accessed=2 * heads * length * length, transcendentals=heads * length * length
        ),
        name="attend",
    )(qkv, qkv, qkv, bias_line)


def attend_back(exps, inverse, grads, outs, qkv, heads, size, length, width):
    spec = attention_specs(heads, size, length, width)
    return pl.pallas_call(
        functools.partial(attend_back_kernel, length, width),
        grid=(heads, length // width),
        in_specs=[spec["exps"], spec["inv"], spec["tokens"], spec["tokens"], spec["query"], spec["key"], spec["value"]],
        out_specs=[spec["query"], spec["whole"], spec["whole"], spec["line"]],
        out_shape=[
            jax.ShapeDtypeStruct((heads * size, length), BF16),
            jax.ShapeDtypeStruct((heads * size, length), BF16),
            jax.ShapeDtypeStruct((heads * size, length), BF16),
            jax.ShapeDtypeStruct((heads, 1, 2 * length), F32),
        ],
        scratch_shapes=[
            pltpu.VMEM((2 * length - LANES, LANES), F32),
            pltpu.VMEM((length, size), BF16),
            pltpu.VMEM((length, size), F32),
            pltpu.VMEM((length, size), F32),
            pltpu.VMEM((length, width), BF16),
        ],
        compiler_params=pltpu.CompilerParams(vmem_limit_bytes=40 << 20),
        cost_estimate=pl.CostEstimate(
            flops=8 * heads * length * length * size, bytes_accessed=2 * heads * length * length, transcendentals=0
        ),
        name="attend_back",
    )(exps, inverse, grads, outs, qkv, qkv, qkv)


def ring_pairs(total, parts, shift):
    return [(i, i - i % parts + (i % parts + shift) % parts) for i in range(total)]


def pick(pieces, index):
    out = pieces[0]
    for k in range(1, len(pieces)):
        out = jnp.where(index == k, pieces[k], out)
    return out


def gather_parts(block, part, parts, total):
    near = [block] + [lax.ppermute(block, "seq", ring_pairs(total, parts, k)) for k in range(1, parts)]
    return [pick(near, (part - j) % parts) for j in range(parts)]


def swap_parts(pieces, part, parts, total):
    near = [pick(pieces, part)]
    for k in range(1, parts):
        near.append(lax.ppermute(pick(pieces, (part + k) % parts), "seq", ring_pairs(total, parts, k)))
    return [pick(near, (part - j) % parts) for j in range(parts)]


def sum_replicated(own, seqs):
    total, parts = lax.axis_size("seq"), lax.axis_size("seq") // seqs
    across = lax.axis_size("wide")
    _, rows, columns = own.shape
    split = own.reshape(seqs, across, rows // across, columns).transpose(1, 0, 2, 3)
    got = lax.all_to_all(split, "wide", 0, 0, tiled=True)
    mine = jnp.sum(got.astype(F32), axis=0).astype(BF16)
    groups = [[s * parts + p for s in range(seqs)] for p in range(parts)]
    got = lax.all_to_all(mine, "seq", 0, 0, tiled=True, axis_index_groups=groups)
    mine = jnp.sum(got.astype(F32), axis=0)
    return lax.all_gather(mine.astype(BF16), "wide", axis=0, tiled=True).astype(F32)


def per_device(
    inputs,
    routes,
    bucket_ids,
    gain_attn,
    w_query,
    w_key,
    w_value,
    w_output,
    rel_table,
    gain_ffn,
    w_router,
    w_in,
    w_out,
    cotangent,
):
    seqs, local_len, width = inputs.shape
    buckets, head_count = rel_table.shape
    size = width // head_count
    total = lax.axis_size("seq")
    across = lax.axis_size("wide")
    length = local_len * total
    parts = total // seqs
    heads = head_count // parts
    cols = heads * size
    me = lax.axis_index("seq")
    part = me % parts
    experts = w_router.shape[1]
    own_experts = w_in.shape[0]
    tokens = seqs * local_len
    capacity = (5 * tokens + 4 * experts - 1) // (4 * experts)
    slots = experts * capacity
    gain_one = gain_attn.astype(F32)
    gain_two = gain_ffn.astype(F32)

    got = lax.all_to_all(inputs.reshape(total, local_len // parts, width), "seq", 0, 0, tiled=True)
    seq_in = jnp.stack(gather_parts(got, part, parts, total), axis=1).reshape(length, width).astype(F32)
    inv_one = inverse_rms(seq_in)
    normed_one = (seq_in * inv_one * gain_one).astype(BF16)
    own_weights = jnp.concatenate(
        [lax.dynamic_slice(w, (0, part * cols), (width, cols)) for w in (w_query, w_key, w_value)], axis=1
    )
    qkv = contract(own_weights, normed_one, 0, 1).astype(BF16)
    own_table = lax.dynamic_slice(rel_table, (0, part * heads), (buckets, heads))
    ids = jnp.concatenate([bucket_ids, jnp.full((1,), buckets, jnp.int32)])
    bucket_hot = (ids[None, :] == jnp.arange(buckets, dtype=jnp.int32)[:, None]).astype(BF16)
    reverse_hot = (ids[::-1][None, :] == jnp.arange(buckets, dtype=jnp.int32)[:, None]).astype(BF16)
    bias_line = contract(own_table, reverse_hot, 0, 0).reshape(heads, 1, 2 * length)
    block = 256
    outs, exps, inverse = attend(qkv, bias_line, heads, size, length, block)

    attended = lax.all_to_all(outs, "seq", 0, 0, tiled=True).reshape(seqs, width, local_len)
    flat_in = inputs.reshape(tokens, width).astype(F32)
    middle = flat_in + jnp.einsum("sft,fe->ste", attended, w_output, preferred_element_type=F32).reshape(tokens, width)
    inv_two = inverse_rms(middle)
    normed_two = (middle * inv_two * gain_two).astype(BF16)
    router_probs = jax.nn.softmax(jnp.dot(normed_two, w_router, preferred_element_type=F32), axis=-1)
    chosen = routes.reshape(tokens)
    picked = chosen[:, None] == jnp.arange(experts, dtype=jnp.int32)[None, :]
    order = jnp.arange(tokens, dtype=jnp.int32)
    before = (order[None, :] < order[:, None]).astype(BF16)
    earlier = jnp.dot(before, picked.astype(BF16), preferred_element_type=F32)
    picked = picked.astype(F32)
    rank_in = jnp.sum(earlier * picked, axis=1).astype(jnp.int32)
    place = (chosen % own_experts) * (across * capacity) + (chosen // own_experts) * capacity + rank_in
    slot_of = jnp.where(rank_in < capacity, place, slots)
    slot_hot = (slot_of[:, None] == jnp.arange(slots, dtype=jnp.int32)[None, :]).astype(BF16)
    gate_prob = jnp.sum(router_probs * picked, axis=1)
    upstream = cotangent.reshape(tokens, width).astype(F32)
    weighted = (gate_prob[:, None] * upstream).astype(BF16)
    both = jnp.concatenate([normed_two, weighted], axis=1)
    packed = contract(slot_hot, both, 0, 0).astype(BF16).reshape(own_experts, across, capacity, 2 * width)
    returned, gathered = [], []
    for e in range(own_experts):
        received = lax.all_to_all(packed[e], "wide", 0, 0, tiled=True).reshape(across * capacity, 2 * width)
        gathered.append(lax.all_gather(received, "seq", axis=0, tiled=True))
        rows_in, rows_grad = received[:, :width], received[:, width:]
        pre_act = jnp.dot(rows_in, w_in[e], preferred_element_type=F32)
        act, pullback = jax.vjp(smooth_act, pre_act)
        expert_out = jnp.dot(act.astype(BF16), w_out[e], preferred_element_type=F32).astype(BF16)
        grad_hidden = contract(rows_grad, w_out[e], 1, 1).astype(BF16)
        grad_pre = pullback(grad_hidden.astype(F32))[0].astype(BF16)
        grad_rows = contract(grad_pre, w_in[e], 1, 1).astype(BF16)
        pair = jnp.concatenate([expert_out, grad_rows], axis=1).reshape(across, capacity, 2 * width)
        returned.append(lax.all_to_all(pair, "wide", 0, 0, tiled=True).reshape(across * capacity, 2 * width))
    token_rows = jnp.dot(slot_hot, jnp.concatenate(returned, axis=0), preferred_element_type=F32)
    selected, grad_token = token_rows[:, :width], token_rows[:, width:]
    output = (middle + gate_prob[:, None] * selected).astype(BF16).reshape(inputs.shape)
    grad_gate = jnp.sum(upstream * selected, axis=1)
    grad_logits = (grad_gate[:, None] * router_probs * (picked - gate_prob[:, None])).astype(BF16)
    grad_router = contract(normed_two, grad_logits, 0, 0)
    grad_normed_two = grad_token + contract(grad_logits, w_router, 1, 1)
    grad_mid_norm, grad_gain_two = norm_backward(middle, inv_two, gain_two, grad_normed_two)
    grad_middle = upstream + grad_mid_norm
    grad_branch = grad_middle.astype(BF16)
    grad_att = jnp.einsum(
        "ste,fe->sft", grad_branch.reshape(seqs, local_len, width), w_output, preferred_element_type=F32
    ).astype(BF16)
    grad_outs = lax.all_to_all(grad_att.reshape(total, cols, local_len), "seq", 0, 0, tiled=True)
    grad_w_output = jnp.einsum(
        "sft,ste->fe", attended, grad_branch.reshape(seqs, local_len, width), preferred_element_type=F32
    )

    dq, dk, dv, diagonal = attend_back(exps, inverse, grad_outs, outs, qkv, heads, size, length, block)
    grads = jnp.concatenate([dq, dk, dv], axis=0)
    grad_table = jnp.einsum(
        "bo,ho->bh", bucket_hot.astype(F32), diagonal[:, 0, :], precision=lax.Precision.HIGHEST
    )
    grad_normed_one = contract(grads, own_weights, 0, 1)
    grad_in_norm, grad_gain_one = norm_backward(seq_in, inv_one, gain_one, grad_normed_one)
    pieces = grad_in_norm.astype(BF16).reshape(total, parts, local_len // parts, width)
    swapped = swap_parts([pieces[:, p] for p in range(parts)], part, parts, total)
    home = sum(p.astype(F32) for p in swapped).astype(BF16)
    home = lax.all_to_all(home, "seq", 0, 0, tiled=True).reshape(tokens, width).astype(F32)
    grad_inputs = (grad_middle + home).reshape(inputs.shape)
    grad_w_qkv = contract(normed_one, grads, 0, 1).astype(BF16)

    share = width // total
    small = jnp.zeros((width, LANES), F32)
    table_full = lax.dynamic_update_slice(jnp.zeros((buckets, head_count), F32), grad_table, (0, part * heads))
    table_rows = jnp.pad(table_full.reshape(total, -1), ((0, 0), (0, share - buckets * head_count // total)))
    small = jnp.concatenate(
        [
            grad_gain_one[:, None],
            table_rows.reshape(width, 1),
            grad_gain_two[:, None],
            grad_router,
            jnp.zeros((width, LANES - 3 - experts), F32),
        ],
        axis=1,
    )
    summed = jnp.concatenate([grad_w_output, small], axis=1).astype(BF16)
    summed = summed.reshape(seqs, parts, share, width + LANES)
    summed = swap_parts([summed[:, p] for p in range(parts)], part, parts, total)
    summed = sum(p.astype(F32) for p in summed).astype(BF16)
    joined = grad_w_qkv.reshape(seqs, parts, share, 3, cols)
    joined = swap_parts([joined[:, p] for p in range(parts)], part, parts, total)
    joined = jnp.stack(joined, axis=3).reshape(seqs, share, 3 * width)
    result = sum_replicated(jnp.concatenate([joined, summed], axis=2), seqs)
    total_query, total_key, total_value, total_output, rest = jnp.split(
        result, [width, 2 * width, 3 * width, 4 * width], axis=1
    )
    total_table = rest[: buckets * head_count // total, 1].reshape(buckets // total, head_count)

    hidden_share = w_in.shape[2] // total
    part_in, part_out = [], []
    for e in range(own_experts):
        rows_in, rows_grad = gathered[e][:, :width], gathered[e][:, width:]
        in_share = lax.dynamic_slice(w_in[e], (0, me * hidden_share), (width, hidden_share))
        out_share = lax.dynamic_slice(w_out[e], (me * hidden_share, 0), (hidden_share, width))
        act, pullback = jax.vjp(smooth_act, jnp.dot(rows_in, in_share, preferred_element_type=F32))
        grad_hidden = contract(rows_grad, out_share, 1, 1).astype(BF16)
        grad_pre = pullback(grad_hidden.astype(F32))[0].astype(BF16)
        part_in.append(contract(rows_in, grad_pre, 0, 0))
        part_out.append(contract(act.astype(BF16), rows_grad, 0, 0))
    return (
        output,
        grad_inputs,
        rest[:, 0],
        total_query,
        total_key,
        total_value,
        total_output,
        total_table,
        rest[:, 2],
        rest[:, 3 : 3 + experts],
        jnp.stack(part_in),
        jnp.stack(part_out),
    )


def solution(mesh):
    in_specs = (
        P("wide", "seq", None),
        P("wide", "seq", None),
        P(),
        P(),
        P(),
        P(),
        P(),
        P(),
        P(),
        P(),
        P(),
        P("wide", None, None),
        P("wide", None, None),
        P("wide", "seq", None),
    )
    out_specs = (
        P("wide", "seq", None),
        P("wide", "seq", None),
        P("seq"),
        P("seq", None),
        P("seq", None),
        P("seq", None),
        P("seq", None),
        P("seq", None),
        P("seq"),
        P("seq", None),
        P("wide", None, "seq"),
        P("wide", "seq", None),
    )
    return jax.shard_map(
        per_device, mesh=mesh, in_specs=in_specs, out_specs=out_specs, check_vma=False
    )
```

time: 1560 us -> 487 us (0.31)
  local copies, waits for them, and re-layouts: 879 us -> 61.6 us
  waiting for transfers between devices: 366 us -> 109 us
  Pallas kernels: 0 us -> 56.1 us
  matrix products: 162 us -> 114 us
    gather x2 -> x0, local copies, waits for them, and re-layouts: 725 us -> none  [per_device(): bucket_map = jnp.take(bucket_ids, offsets)]
    reduce_scatter x7 -> x0, waiting for transfers between devices: 282 us -> none  [the longest x1 93.9 us: per_device(): lax.psum_scatter(part_out.astype(jnp.bfloat16), 'seq', scatter_dimension=...]
    all_to_all x4 -> x8, waiting for transfers between devices: 28.3 us -> 106 us  [the longest x1 37.1 us: per_device(): lax.all_to_all(grad_att.reshape(total, cols, local_len), 'seq', 0, 0, til...]
    pallas_call x0 -> x2, Pallas kernels: none -> 56.1 us  [the longest x1 31 us: attend_back(): pl.pallas_call(functools.partial(attend_back_kernel, length, width), grid...]
    unnamed x13 -> x2, waiting for transfers between devices: 55.8 us -> 0.71 us
    dot_general x58 -> x26, matrix products: 162 us -> 114 us  [the longest x13 66.3 us: contract(): lax.dot_general(a, b, (((da,), (db,)), ((), ())), preferred_element_type=...]
    psum x1 -> x0, blocking collectives: 45 us -> none  [per_device(): lax.psum((shard_query, shard_key, shard_value, shard_output, shard_gain_o...]
    all_to_all x0 -> x2, blocking collectives: none -> 44.5 us  [the longest x1 27.4 us: per_device(): lax.all_to_all(inputs.reshape(total, local_len // parts, width), 'seq', 0...]
  transfers between devices with their start and end apart: 15 -> 14, of which waited for: 9 -> 7; matrix products, arithmetic and copies ran while one was open for 56% -> 32% of each run, Pallas kernels for 0% -> 6%
where the time goes in v1:
time: 487 us; the launch traced here: 478 us
  matrix products  114 us (23%)
  waiting for transfers between devices  109 us (22%)
  local copies, waits for them, and re-layouts  61.6 us (13%)
  Pallas kernels  56.1 us (12%)
  blocking collectives  55.9 us (11%)
  starting transfers between devices  34 us (7%)
  other arithmetic  32.2 us (7%)
  between operations  15.1 us (3%)
    dot_general x13, matrix products, contract(): lax.dot_general(a, b, (((da,), (db,)), ((), ())), preferred_element_type=...  66.3 us
    all_to_all x1, waiting for transfers between devices, per_device(): lax.all_to_all(grad_att.reshape(total, cols, local_len), 'seq', 0, 0, til...  37.1 us
    pallas_call x1, Pallas kernels, attend_back(): pl.pallas_call(functools.partial(attend_back_kernel, length, width), grid...  31 us
    all_to_all x1, blocking collectives, per_device(): lax.all_to_all(inputs.reshape(total, local_len // parts, width), 'seq', 0...  27.4 us
    pallas_call x1, Pallas kernels, attend(): pl.pallas_call(functools.partial(attend_kernel, length, width), grid=(hea...  25.1 us
    all_to_all x1, waiting for transfers between devices, sum_replicated(): got = lax.all_to_all(split, 'wide', 0, 0, tiled=True)  22.5 us
    all_to_all x1, waiting for transfers between devices, per_device(): lax.all_to_all(outs, 'seq', 0, 0, tiled=True)  20 us
    all_to_all x1, blocking collectives, per_device(): lax.all_to_all(packed[e], 'wide', 0, 0, tiled=True)  17 us
  transfers between devices with their start and end apart: 14, of which 7 were waited for; matrix products, arithmetic and copies ran while one was open for 32% of the time, Pallas kernels for 6%

profile of v1, /device:TPU:0, one launch (start us, length us, event | category | flops | bytes accessed | tf_op | source)
XLA Modules:
  0.0 478.2 jit_solution(14042943197847154929)
XLA Ops:
  7.2 27.4 %all_to_all.50 = bf16[8,64,768]{2,1,0:T(8,128)(2,1)S(1)} all-to-all(bf16[8,64,768]{2,1,0:T(8,128)(2,1)} %bitcast.215), channel_id=1, replica_groups=mesh['seq'=8,'wide'=4] {'seq'}, dimensions={0} | all-to-all | bytes 1572864 | tf_op jit(solution)/shard_map/all_to_all | solution.py:265
  51.7 25.1 %attend.1 = (bf16[8,384,128]{2,1,0:T(8,128)(2,1)S(1)}, bf16[6,1024,1024]{2,1,0:T(8,128)(2,1)}, f32[6,1,1024]{2,1,0:T(1,128)S(1)}) custom-call(bf16[1152,1024]{1,0:T(8,128)(2,1)S(1)} %convolution_convert_fusion.2.q_ref.k_ref.v_ref, bf16[1152,1024]{1,0:T(8,128)(2,1)S(1)} %convolution_convert_fusion.2.q_ref.k_ref.v_ref, ...), custom_call_target="tpu_custom_call" | custom-call | flops 1610612736 | bytes 12582912 | tf_op jit(solution)/shard_map/attend/pallas_call | solution.py:143
  83.5 20.0 %all-to-all-done.1 = bf16[8,384,128]{2,1,0:T(8,128)(2,1)} async-done(((bf16[8,384,128]{2,1,0:T(8,128)(2,1)}), bf16[8,384,128]{2,1,0:T(8,128)(2,1)}, u32[]{:S(2)}, u32[]{:S(2)}) %all-to-all-start.1) | async-done | bytes 786464 | tf_op jit(solution)/shard_map/all_to_all | solution.py:281
  113.8 17.0 %all_to_all.51 = bf16[4,80,1536]{2,1,0:T(8,128)(2,1)} all-to-all(bf16[4,80,1536]{2,1,0:T(8,128)(2,1)S(1)} %bitcast.211), channel_id=1, replica_groups=mesh['seq'=8,'wide'=4] {'wide'}, dimensions={0} | all-to-all | bytes 1966080 | tf_op jit(solution)/shard_map/all_to_all | solution.py:304
  135.4 6.6 %fusion.6 = f32[320,3072]{1,0:T(8,128)} fusion(bf16[320,1536]{1,0:T(8,128)(2,1)} %bitcast.206, bf16[2,768,3072]{2,1,0:T(8,128)(2,1)} %param.25), kind=kOutput, calls=%fused_computation.22 | convolution fusion | flops 1509949440 | bytes 9142272 | tf_op jit(solution)/shard_map/dot_general | solution.py:307
  142.0 10.4 %fusion.141 = bf16[320,768]{1,0:T(8,128)(2,1)} fusion(f32[320,3072]{1,0:T(8,128)} %fusion.6, bf16[320,1536]{1,0:T(8,128)(2,1)} %bitcast.207, bf16[2,3072,768]{2,1,0:T(8,128)(2,1)} %param.26, bf16[2,768,3072]{2,1,0:T(8,128)(2,1)} %param.25), kind=kOutput, calls=%fused_computation.165 | convolution fusion | flops 3041771520 | bytes 14352384 | tf_op jit(solution)/shard_map/dot_general | solution.py:17
  152.4 6.1 %fusion.133 = bf16[320,768]{1,0:T(8,128)(2,1)S(1)} fusion(f32[320,3072]{1,0:T(8,128)} %fusion.6, bf16[2,3072,768]{2,1,0:T(8,128)(2,1)} %param.26), kind=kOutput, calls=%fused_computation.163 | convolution fusion | flops 1519042560 | bytes 9142272 | tf_op jit(solution)/shard_map/dot_general | solution.py:309
  164.3 6.2 %fusion.14 = f32[320,3072]{1,0:T(8,128)} fusion(bf16[320,1536]{1,0:T(8,128)(2,1)} %bitcast.11, bf16[2,768,3072]{2,1,0:T(8,128)(2,1)} %param.25), kind=kOutput, calls=%fused_computation.30 | convolution fusion | flops 1509949440 | bytes 9142272 | tf_op jit(solution)/shard_map/dot_general | solution.py:307
  170.5 10.4 %fusion.136 = bf16[320,768]{1,0:T(8,128)(2,1)} fusion(f32[320,3072]{1,0:T(8,128)} %fusion.14, bf16[320,1536]{1,0:T(8,128)(2,1)} %bitcast.11, bf16[2,3072,768]{2,1,0:T(8,128)(2,1)} %param.26, bf16[2,768,3072]{2,1,0:T(8,128)(2,1)} %param.25), kind=kOutput, calls=%fused_computation.164 | convolution fusion | flops 3041771520 | bytes 14352384 | tf_op jit(solution)/shard_map/dot_general | solution.py:17
  180.9 6.0 %fusion.130 = bf16[320,768]{1,0:T(8,128)(2,1)S(1)} fusion(f32[320,3072]{1,0:T(8,128)} %fusion.14, bf16[2,3072,768]{2,1,0:T(8,128)(2,1)} %param.26), kind=kOutput, calls=%fused_computation.162 | convolution fusion | flops 1519042560 | bytes 9142272 | tf_op jit(solution)/shard_map/dot_general | solution.py:309
  192.9 10.4 %all-to-all-done.3 = bf16[4,80,1536]{2,1,0:T(8,128)(2,1)} async-done(((bf16[4,80,1536]{2,1,0:T(8,128)(2,1)}), bf16[4,80,1536]{2,1,0:T(8,128)(2,1)}, u32[]{:S(2)}, u32[]{:S(2)}) %all-to-all-start.3) | async-done | bytes 983072 | tf_op jit(solution)/shard_map/all_to_all | solution.py:314
  225.5 37.1 %all-to-all-done.6.grad_ref = bf16[8,384,128]{2,1,0:T(8,128)(2,1)S(1)} async-done(((bf16[8,384,128]{2,1,0:T(8,128)(2,1)}), bf16[8,384,128]{2,1,0:T(8,128)(2,1)S(1)}, u32[]{:S(2)}, u32[]{:S(2)}) %all-to-all-start.6) | async-done | bytes 786464 | tf_op jit(solution)/shard_map/all_to_all | solution.py:328
  263.8 31.0 %attend_back.1 = (bf16[384,1024]{1,0:T(8,128)(2,1)S(1)}, bf16[384,1024]{1,0:T(8,128)(2,1)S(1)}, bf16[384,1024]{1,0:T(8,128)(2,1)S(1)}, f32[6,1,2048]{2,1,0:T(1,128)S(1)}) custom-call(bf16[6,1024,1024]{2,1,0:T(8,128)(2,1)} %get-tuple-element.20.exp_ref, f32[6,1,1024]{2,1,0:T(1,128)S(1)} %copy-done.6, bf16[8,384,128]{2,1,0:T(8,128)(2,1)S(1)} %all-to-all-done.6.grad_ref, ...), custom_call_target="tpu_custom_call" | custom-call | flops 3221225472 | bytes 12582912 | tf_op jit(solution)/shard_map/attend_back/pallas_call | solution.py:168
  345.5 22.5 %all-to-all-done.8 = bf16[4,4,24,3200]{3,2,1,0:T(8,128)(2,1)} async-done(((bf16[4,4,24,3200]{3,2,1,0:T(8,128)(2,1)}), bf16[4,4,24,3200]{3,2,1,0:T(8,128)(2,1)}, u32[]{:S(2)}, u32[]{:S(2)}) %all-to-all-start.8) | async-done | bytes 2457632 | tf_op jit(solution)/shard_map/all_to_all | solution.py:222
  371.5 8.2 %fusion.255 = (bf16[1,768,3072]{2,1,0:T(8,128)(2,1)}, bf16[1,768,3072]{2,1,0:T(8,128)(2,1)}) fusion(bf16[2,768,3072]{2,1,0:T(8,128)(2,1)} %param.25), kind=kLoop, calls=%fused_computation.309 | loop fusion | bytes 18874368 | tf_op jit(solution)/shard_map/slice | solution.py:307
  382.7 9.7 %all-to-all-done.7 = bf16[8,64,768]{2,1,0:T(8,128)(2,1)S(1)} async-done(((bf16[8,64,768]{2,1,0:T(8,128)(2,1)}), bf16[8,64,768]{2,1,0:T(8,128)(2,1)S(1)}, u32[]{:S(2)}, u32[]{:S(2)}) %all-to-all-start.7) | async-done | bytes 786464 | tf_op jit(solution)/shard_map/all_to_all | solution.py:343
  395.9 8.3 %fusion.254 = (bf16[1,3072,768]{2,1,0:T(8,128)(2,1)}, bf16[1,3072,768]{2,1,0:T(8,128)(2,1)}) fusion(bf16[2,3072,768]{2,1,0:T(8,128)(2,1)} %param.26), kind=kLoop, calls=%fused_computation.308 | loop fusion | bytes 18874368 | tf_op jit(solution)/shard_map/slice | solution.py:309
  405.5 6.8 %all-to-all-done.9 = bf16[4,24,3200]{2,1,0:T(8,128)(2,1)S(1)} async-done(((bf16[4,24,3200]{2,1,0:T(8,128)(2,1)}), bf16[4,24,3200]{2,1,0:T(8,128)(2,1)S(1)}, u32[]{:S(2)}, u32[]{:S(2)}) %all-to-all-start.9) | async-done | bytes 614432 | tf_op jit(solution)/shard_map/all_to_all | solution.py:225
  412.4 11.5 %all_gather.9 = bf16[96,3200]{1,0:T(8,128)(2,1)S(1)} all-gather(bf16[24,3200]{1,0:T(8,128)(2,1)S(1)} %reduce_sum.125), channel_id=1, replica_groups=mesh['seq'=8,'wide'=4] {'wide'}, dimensions={0}, use_global_device_ids=true | all-gather | bytes 768000 | tf_op jit(solution)/shard_map/all_gather | solution.py:227
  427.3 6.4 %fusion.67 = f32[2560,384]{1,0:T(8,128)} fusion(bf16[2560,1536]{1,0:T(8,128)(2,1)} %all-gather.5.cloned.1.call-done, bf16[1,768,3072]{2,1,0:T(8,128)(2,1)} %get-tuple-element.97, s32[]{:T(128)S(6)} %select_n.222), kind=kOutput, calls=%fused_computation.86 | convolution fusion | flops 1509949440 | bytes 8454148 | tf_op jit(solution)/shard_map/dot_general | solution.py:380
  433.7 9.8 %fusion.119 = f32[1,768,384]{2,1,0:T(8,128)S(1)} fusion(bf16[2560,1536]{1,0:T(8,128)(2,1)} %all-gather.5.cloned.1.call-done, f32[2560,384]{1,0:T(8,128)} %fusion.67, bf16[1,3072,768]{2,1,0:T(8,128)(2,1)} %get-tuple-element.95, s32[]{:T(128)S(6)} %select_n.222), kind=kOutput, calls=%fused_computation.157 | convolution fusion | flops 3041525760 | bytes 13565956 | tf_op jit(solution)/shard_map/dot_general | solution.py:17
  443.5 6.3 %fusion.74 = f32[2560,384]{1,0:T(8,128)} fusion(bf16[2560,1536]{1,0:T(8,128)(2,1)} %all-gather.3.cloned.1.call-done, bf16[1,768,3072]{2,1,0:T(8,128)(2,1)} %get-tuple-element.96, s32[]{:T(128)S(6)} %select_n.222), kind=kOutput, calls=%fused_computation.93 | convolution fusion | flops 1509949440 | bytes 8454148 | tf_op jit(solution)/shard_map/dot_general | solution.py:380
  449.8 10.0 %fusion.113 = f32[1,768,384]{2,1,0:T(8,128)S(1)} fusion(bf16[2560,1536]{1,0:T(8,128)(2,1)} %all-gather.3.cloned.1.call-done, f32[2560,384]{1,0:T(8,128)} %fusion.74, bf16[1,3072,768]{2,1,0:T(8,128)(2,1)} %get-tuple-element.94, s32[]{:T(128)S(6)} %select_n.222), kind=kOutput, calls=%fused_computation.155 | convolution fusion | flops 3041525760 | bytes 13565956 | tf_op jit(solution)/shard_map/dot_general | solution.py:17
  461.4 5.8 %fusion.122 = f32[1,384,768]{2,1,0:T(8,128)S(1)} fusion(bf16[2560,1536]{1,0:T(8,128)(2,1)} %all-gather.5.cloned.1.call-done, f32[2560,384]{1,0:T(8,128)} %fusion.67), kind=kOutput, calls=%fused_computation.158 | convolution fusion | flops 1518796800 | bytes 9043968 | tf_op jit(solution)/shard_map/dot_general | solution.py:17
  (232 shorter events, 144.2 us)
Async XLA Ops:
  7.2 98.7 %copy-start = (bf16[768,768]{1,0:T(8,128)(2,1)S(1)}, bf16[768,768]{1,0:T(8,128)(2,1)}, u32[]{:S(2)}) copy-start(bf16[768,768]{1,0:T(8,128)(2,1)} %param.21) | copy-start | bytes 3538948
  34.6 7.4 %collective-permute-start = (bf16[8,64,768]{2,1,0:T(8,128)(2,1)S(1)}, bf16[8,64,768]{2,1,0:T(8,128)(2,1)S(1)}, u32[]{:S(2)}, u32[]{:S(2)}) collective-permute-start(bf16[8,64,768]{2,1,0:T(8,128)(2,1)S(1)} %all_to_all.50), channel_id=1, source_target_pairs={{0,4},{4,0},{8,12},{12,8},{16,20},{20,16},{24,28},{28,24},{1,5},{5... | collective-permute-start | bytes 2359304 | tf_op jit(solution)/shard_map/ppermute | solution.py:206
  35.3 9.5 %copy-start.37 = (f32[768]{0:T(1024)}, f32[768]{0:T(1024)S(1)}, u32[]{:S(2)}) copy-start(f32[768]{0:T(1024)S(1)} %convert_element_type.179) | copy-start | bytes 9220
  51.7 30.9 %copy-start.54 = (bf16[768]{0:T(1024)(128)(2,1)S(1)}, bf16[768]{0:T(1024)(128)(2,1)}, u32[]{:S(2)}) copy-start(bf16[768]{0:T(1024)(128)(2,1)} %param.23) | copy-start | bytes 4612
  51.7 30.9 %copy-start.39 = (s32[4,128,1]{1,2,0:T(1,128)S(1)}, s32[4,128,1]{1,2,0:T(1,128)}, u32[]{:S(2)}) copy-start(s32[4,128,1]{1,2,0:T(1,128)} %param.15) | copy-start | bytes 6148
  78.3 25.2 %all-to-all-start.1 = ((bf16[8,384,128]{2,1,0:T(8,128)(2,1)}), bf16[8,384,128]{2,1,0:T(8,128)(2,1)}, u32[]{:S(2)}, u32[]{:S(2)}) async-start(bf16[8,384,128]{2,1,0:T(8,128)(2,1)} %copy-done.2), calls=%async_computation.1 | async-start | bytes 1572864 | tf_op jit(solution)/shard_map/all_to_all | solution.py:281
  82.6 344.8 %all-gather.5.cloned.1.call-start = ((), (), s32[]{:S(2)}) async-start(), calls=%async_computation.11 | async-start | bytes 8847360 | tf_op jit(solution)/shard_map/all_gather | solution.py:305
  82.6 26.2 %copy-start.27 = (f32[768]{0:T(1024)}, f32[768]{0:T(1024)S(1)}, u32[]{:S(2)}) copy-start(f32[768]{0:T(1024)S(1)} %convert_element_type.182) | copy-start | bytes 9220
  130.9 28.7 %all-to-all-start.2 = ((bf16[4,80,1536]{2,1,0:T(8,128)(2,1)}), bf16[4,80,1536]{2,1,0:T(8,128)(2,1)}, u32[]{:S(2)}, u32[]{:S(2)}) async-start(bf16[4,80,1536]{2,1,0:T(8,128)(2,1)} %bitcast.210), calls=%async_computation.2 | async-start | bytes 1966080 | tf_op jit(solution)/shard_map/all_to_all | solution.py:304
  159.6 28.3 %all-to-all-start.5 = ((bf16[4,80,1536]{2,1,0:T(8,128)(2,1)}), bf16[4,80,1536]{2,1,0:T(8,128)(2,1)}, u32[]{:S(2)}, u32[]{:S(2)}) async-start(bf16[4,80,1536]{2,1,0:T(8,128)(2,1)} %bitcast.208), calls=%async_computation.5 | async-start | bytes 1966080 | tf_op jit(solution)/shard_map/all_to_all | solution.py:314
  187.9 15.4 %all-to-all-start.3 = ((bf16[4,80,1536]{2,1,0:T(8,128)(2,1)}), bf16[4,80,1536]{2,1,0:T(8,128)(2,1)}, u32[]{:S(2)}, u32[]{:S(2)}) async-start(bf16[4,80,1536]{2,1,0:T(8,128)(2,1)} %bitcast.209), calls=%async_computation.3 | async-start | bytes 1966080 | tf_op jit(solution)/shard_map/all_to_all | solution.py:314
  192.1 251.4 %all-gather.3.cloned.1.call-start = ((), (), s32[]{:S(2)}) async-start(), calls=%async_computation.10 | async-start | bytes 8847360 | tf_op jit(solution)/shard_map/all_gather | solution.py:305
  215.6 7.6 %copy-start.45 = (f32[512]{0:T(512)S(1)}, f32[512]{0:T(512)}, u32[]{:S(2)}) copy-start(f32[512]{0:T(512)} %copy-done.43) | copy-start | bytes 6148
  215.7 47.0 %copy-start.6 = (f32[6,1,1024]{2,1,0:T(1,128)S(1)}, f32[6,1,1024]{2,1,0:T(1,128)}, u32[]{:S(2)}) copy-start(f32[6,1,1024]{2,1,0:T(1,128)} %copy-done.5) | copy-start | bytes 73732
  215.7 47.0 %all-to-all-start.6 = ((bf16[8,384,128]{2,1,0:T(8,128)(2,1)}), bf16[8,384,128]{2,1,0:T(8,128)(2,1)S(1)}, u32[]{:S(2)}, u32[]{:S(2)}) async-start(bf16[8,384,128]{2,1,0:T(8,128)(2,1)} %bitcast.212), calls=%async_computation.6 | async-start | bytes 1572864 | tf_op jit(solution)/shard_map/all_to_all | solution.py:328
  263.8 31.3 %copy-start.21 = (bf16[768,384]{1,0:T(8,128)(2,1)S(1)}, bf16[768,384]{1,0:T(8,128)(2,1)}, u32[]{:S(2)}) copy-start(bf16[768,384]{1,0:T(8,128)(2,1)} %constant_dynamic-slice_fusion.2) | copy-start | bytes 1769476
  305.8 11.1 %collective-permute-start.3 = (bf16[4,96,896]{2,1,0:T(8,128)(2,1)}, bf16[4,96,896]{2,1,0:T(8,128)(2,1)}, u32[]{:S(2)}, u32[]{:S(2)}) collective-permute-start(bf16[4,96,896]{2,1,0:T(8,128)(2,1)} %select_bitcast_fusion.4), channel_id=1, source_target_pairs={{0,4},{4,0},{8,12},{12,8},{16,20},{20,16},{24,28},{28,24},{1,5},{5... | collective-permute-start | bytes 2064392 | tf_op jit(solution)/shard_map/ppermute | solution.py:213
  316.6 3.0 collective-permute-start.2
  323.9 8.2 %copy-start.15 = (bf16[4,96,896]{2,1,0:T(8,128)(2,1)S(1)}, bf16[4,96,896]{2,1,0:T(8,128)(2,1)}, u32[]{:S(2)}) copy-start(bf16[4,96,896]{2,1,0:T(8,128)(2,1)} %add_convert_fusion.2) | copy-start | bytes 2064388
  333.9 34.0 %all-to-all-start.8 = ((bf16[4,4,24,3200]{3,2,1,0:T(8,128)(2,1)}), bf16[4,4,24,3200]{3,2,1,0:T(8,128)(2,1)}, u32[]{:S(2)}, u32[]{:S(2)}) async-start(bf16[4,4,24,3200]{3,2,1,0:T(8,128)(2,1)} %copy.116), calls=%async_computation.8 | async-start | bytes 4915200 | tf_op jit(solution)/shard_map/all_to_all | solution.py:222
  341.8 2.4 collective-permute-start.1
  367.9 24.5 %all-to-all-start.7 = ((bf16[8,64,768]{2,1,0:T(8,128)(2,1)}), bf16[8,64,768]{2,1,0:T(8,128)(2,1)S(1)}, u32[]{:S(2)}, u32[]{:S(2)}) async-start(bf16[8,64,768]{2,1,0:T(8,128)(2,1)} %add_convert_fusion), calls=%async_computation.7 | async-start | bytes 1572864 | tf_op jit(solution)/shard_map/all_to_all | solution.py:343
  392.4 20.0 %all-to-all-start.9 = ((bf16[4,24,3200]{2,1,0:T(8,128)(2,1)}), bf16[4,24,3200]{2,1,0:T(8,128)(2,1)S(1)}, u32[]{:S(2)}, u32[]{:S(2)}) async-start(bf16[4,24,3200]{2,1,0:T(8,128)(2,1)} %reduce_sum.124), calls=%async_computation.9 | async-start | bytes 1228800 | tf_op jit(solution)/shard_map/all_to_all | solution.py:225
  395.9 8.3 %copy-start.14 = (f32[512,768]{1,0:T(8,128)S(1)}, f32[512,768]{1,0:T(8,128)}, u32[]{:S(2)}) copy-start(f32[512,768]{1,0:T(8,128)} %get-tuple-element.93) | copy-start | bytes 4718596
  (49 other events, 180.8 us)
Sparse Core Ops, SparseCore 0:
  131.0 75.3 all-gather.4
  208.0 92.9 all-gather.2

commit v2 on v1

--- a/solution.py
+++ b/solution.py
@@ -70,7 +70,7 @@
 
 
 def attend_back_kernel(
-    length, width, exp_ref, inv_ref, grad_ref, out_ref, q_ref, k_ref, v_ref, dq_ref, dk_ref, dv_ref, diag_ref, strip, values, dk_sum, dv_sum, scores
+    length, width, exp_ref, inv_ref, grad_ref, out_ref, q_ref, k_ref, v_ref, three_ref, diag_ref, strip, values, dk_sum, dv_sum, scores
 ):
     block = pl.program_id(1)
     rows = 2 * length - LANES
@@ -99,14 +99,15 @@
             row = pl.multiple_of(length - LANES - (block * width + s * LANES) + c * chunk, LANES)
             strip[pl.ds(row, chunk), :] += slope
             scores[c * chunk : (c + 1) * chunk, s * LANES : (s + 1) * LANES] = slope.astype(BF16)
-    dq_ref[...] = contract(k_ref[...], scores[...], 1, 0).astype(BF16)
+    here = pl.ds(pl.multiple_of(block * width, LANES), width)
+    three_ref[0, :, here] = contract(k_ref[...], scores[...], 1, 0).astype(BF16)
     dk_sum[...] += contract(scores[...], q_ref[...].T, 1, 0)
     dv_sum[...] += contract(exp_ref[0], grad.T, 1, 0)
 
     @pl.when(block == pl.num_programs(1) - 1)
     def _():
-        dk_ref[...] = dk_sum[...].T.astype(BF16)
-        dv_ref[...] = dv_sum[...].T.astype(BF16)
+        three_ref[1] = dk_sum[...].T.astype(BF16)
+        three_ref[2] = dv_sum[...].T.astype(BF16)
         diag_ref[...] = jnp.zeros_like(diag_ref)
         down = lax.broadcasted_iota(jnp.int32, (LANES, LANES), 0)
         over = lax.broadcasted_iota(jnp.int32, (LANES, LANES), 1)
@@ -124,13 +125,14 @@
             diag_ref[0, :, LANES * b : LANES * (b + 2)] += jnp.sum(rolled, axis=0, keepdims=True)
 
 
-def attention_specs(heads, size, length, width):
+def attention_specs(heads, first, size, length, width):
     subs = width // LANES
     return dict(
-        query=pl.BlockSpec((size, width), lambda h, b: (h, b)),
-        key=pl.BlockSpec((size, length), lambda h, b: (heads + h, 0)),
-        value=pl.BlockSpec((size, length), lambda h, b: (2 * heads + h, 0)),
-        whole=pl.BlockSpec((size, length), lambda h, b: (h, 0)),
+        query=pl.BlockSpec((size, width), lambda h, b: (first + h, b)),
+        key=pl.BlockSpec((size, length), lambda h, b: (heads + first + h, 0)),
+        value=pl.BlockSpec((size, length), lambda h, b: (2 * heads + first + h, 0)),
+        three=pl.BlockSpec((3, size, length), lambda h, b: (0, h, 0)),
+        bias=pl.BlockSpec((1, 1, 2 * length), lambda h, b: (first + h, 0, 0)),
         line=pl.BlockSpec((1, 1, 2 * length), lambda h, b: (h, 0, 0)),
         exps=pl.BlockSpec((1, length, width), lambda h, b: (h, 0, b)),
         inv=pl.BlockSpec((1, 1, width), lambda h, b: (h, 0, b)),
@@ -138,43 +140,41 @@
     )
 
 
-def attend(qkv, bias_line, heads, size, length, width):
-    spec = attention_specs(heads, size, length, width)
+def attend(qkv, bias_line, heads, first, count, size, length, width):
+    spec = attention_specs(heads, first, size, length, width)
     return pl.pallas_call(
         functools.partial(attend_kernel, length, width),
-        grid=(heads, length // width),
-        in_specs=[spec["query"], spec["key"], spec["value"], spec["line"]],
+        grid=(count, length // width),
+        in_specs=[spec["query"], spec["key"], spec["value"], spec["bias"]],
         out_specs=[spec["tokens"], spec["exps"], spec["inv"]],
         out_shape=[
-            jax.ShapeDtypeStruct((length // LANES, heads * size, LANES), BF16),
-            jax.ShapeDtypeStruct((heads, length, length), BF16),
-            jax.ShapeDtypeStruct((heads, 1, length), F32),
+            jax.ShapeDtypeStruct((length // LANES, count * size, LANES), BF16),
+            jax.ShapeDtypeStruct((count, length, length), BF16),
+            jax.ShapeDtypeStruct((count, 1, length), F32),
         ],
         scratch_shapes=[
             pltpu.VMEM((2 * length - LANES, LANES), F32),
             pltpu.VMEM((length, size), BF16),
             pltpu.VMEM((length, width), F32),
         ],
-        compiler_params=pltpu.CompilerParams(vmem_limit_bytes=40 << 20),
+        compiler_params=pltpu.CompilerParams(vmem_limit_bytes=62 << 20),
         cost_estimate=pl.CostEstimate(
-            flops=4 * heads * length * length * size, bytes_accessed=2 * heads * length * length, transcendentals=heads * length * length
+            flops=4 * count * length * length * size, bytes_accessed=2 * count * length * length, transcendentals=count * length * length
         ),
         name="attend",
     )(qkv, qkv, qkv, bias_line)
 
 
-def attend_back(exps, inverse, grads, outs, qkv, heads, size, length, width):
-    spec = attention_specs(heads, size, length, width)
+def attend_back(exps, inverse, grads, outs, qkv, heads, first, count, size, length, width):
+    spec = attention_specs(heads, first, size, length, width)
     return pl.pallas_call(
         functools.partial(attend_back_kernel, length, width),
-        grid=(heads, length // width),
+        grid=(count, length // width),
         in_specs=[spec["exps"], spec["inv"], spec["tokens"], spec["tokens"], spec["query"], spec["key"], spec["value"]],
-        out_specs=[spec["query"], spec["whole"], spec["whole"], spec["line"]],
+        out_specs=[spec["three"], spec["line"]],
         out_shape=[
-            jax.ShapeDtypeStruct((heads * size, length), BF16),
-            jax.ShapeDtypeStruct((heads * size, length), BF16),
-            jax.ShapeDtypeStruct((heads * size, length), BF16),
-            jax.ShapeDtypeStruct((heads, 1, 2 * length), F32),
+            jax.ShapeDtypeStruct((3, count * size, length), BF16),
+            jax.ShapeDtypeStruct((count, 1, 2 * length), F32),
         ],
         scratch_shapes=[
             pltpu.VMEM((2 * length - LANES, LANES), F32),
@@ -183,12 +183,373 @@
             pltpu.VMEM((length, size), F32),
             pltpu.VMEM((length, width), BF16),
         ],
-        compiler_params=pltpu.CompilerParams(vmem_limit_bytes=40 << 20),
+        compiler_params=pltpu.CompilerParams(vmem_limit_bytes=62 << 20),
         cost_estimate=pl.CostEstimate(
-            flops=8 * heads * length * length * size, bytes_accessed=2 * heads * length * length, transcendentals=0
+            flops=8 * count * length * length * size, bytes_accessed=2 * count * length * length, transcendentals=0
         ),
         name="attend_back",
     )(exps, inverse, grads, outs, qkv, qkv, qkv)
+
+
+def activation(v):
+    square = v * v
+    bent = jnp.tanh(0.7978845608 * v * (1.0 + 0.044715 * square))
+    half = 0.5 * (1.0 + bent)
+    slope = half + 0.5 * v * (1.0 - bent * bent) * (0.7978845608 * (1.0 + 3.0 * 0.044715 * square))
+    return v * half, slope
+
+
+def expert_kernel(rows_ref, in_ref, out_ref, both_ref, forward, backward):
+    step = pl.program_id(0)
+    width = rows_ref.shape[1] // 2
+
+    @pl.when(step == 0)
+    def _():
+        forward[...] = jnp.zeros_like(forward)
+        backward[...] = jnp.zeros_like(backward)
+
+    hidden, slope = activation(contract(rows_ref[:, :width], in_ref[0], 1, 0))
+    grad_hidden = contract(rows_ref[:, width:], out_ref[0], 1, 1).astype(BF16).astype(F32)
+    forward[...] += contract(hidden.astype(BF16), out_ref[0], 1, 0)
+    backward[...] += contract((grad_hidden * slope).astype(BF16), in_ref[0], 1, 1)
+
+    @pl.when(step == pl.num_programs(0) - 1)
+    def _():
+        both_ref[:, :width] = forward[...].astype(BF16)
+        both_ref[:, width:] = backward[...].astype(BF16)
+
+
+def run_expert(rows, w_in, w_out, expert, block):
+    count, double = rows.shape
+    width = double // 2
+    units = w_in.shape[2]
+    return pl.pallas_call(
+        expert_kernel,
+        grid=(units // block,),
+        in_specs=[
+            pl.BlockSpec((count, double), lambda f: (0, 0)),
+            pl.BlockSpec((1, width, block), lambda f: (expert, 0, f)),
+            pl.BlockSpec((1, block, width), lambda f: (expert, f, 0)),
+        ],
+        out_specs=pl.BlockSpec((count, double), lambda f: (0, 0)),
+        out_shape=jax.ShapeDtypeStruct((count, double), BF16),
+        scratch_shapes=[pltpu.VMEM((count, width), F32), pltpu.VMEM((count, width), F32)],
+        compiler_params=pltpu.CompilerParams(vmem_limit_bytes=62 << 20),
+        cost_estimate=pl.CostEstimate(
+            flops=8 * count * width * units, bytes_accessed=4 * width * units, transcendentals=count * units
+        ),
+        name="expert",
+    )(rows, w_in, w_out)
+
+
+def share_kernel(share_ref, rows_ref, in_ref, out_ref, *refs):
+    grad_in_ref, grad_out_ref, flipped, total_in = refs[-4:]
+    step = pl.program_id(0)
+    width = rows_ref.shape[1] // 2
+
+    @pl.when(step == 0)
+    def _():
+        flipped[...] = in_ref[0].T
+        total_in[...] = jnp.zeros_like(total_in)
+        grad_out_ref[...] = jnp.zeros_like(grad_out_ref)
+
+    rows, grads = rows_ref[:, :width], rows_ref[:, width:]
+    hidden, slope = activation(contract(flipped[...], rows, 1, 1))
+    grad_hidden = contract(out_ref[0], grads, 1, 1).astype(BF16).astype(F32)
+    grad_out_ref[0] += contract(hidden.astype(BF16), grads, 1, 0)
+    total_in[...] += contract((grad_hidden * slope).astype(BF16), rows, 1, 0)
+
+    @pl.when(step == pl.num_programs(0) - 1)
+    def _():
+        grad_in_ref[0] = total_in[...].T
+
+
+def run_share(me, rows, w_in, w_out, expert, total, held, block):
+    count, double = rows.shape
+    width = double // 2
+    own = w_in.shape[0]
+    share = w_in.shape[2] // total
+    if share % LANES == 0:
+        where = jnp.full((1,), me, jnp.int32)
+        in_spec = pl.BlockSpec((1, width, share), lambda r, at: (expert, 0, at[0]))
+        out_spec = pl.BlockSpec((1, share, width), lambda r, at: (expert, at[0], 0))
+    else:
+        where = jnp.zeros((1,), jnp.int32)
+        w_in = lax.dynamic_slice(w_in, (0, 0, me * share), (own, width, share))
+        w_out = lax.dynamic_slice(w_out, (0, me * share, 0), (own, share, width))
+        in_spec = pl.BlockSpec((1, width, share), lambda r, at: (expert, 0, 0))
+        out_spec = pl.BlockSpec((1, share, width), lambda r, at: (expert, 0, 0))
+    held_specs = [pl.BlockSpec(memory_space=pl.ANY)] * len(held)
+    return pl.pallas_call(
+        share_kernel,
+        grid_spec=pltpu.PrefetchScalarGridSpec(
+            num_scalar_prefetch=1,
+            grid=(count // block,),
+            in_specs=[pl.BlockSpec((block, double), lambda r, at: (r, 0)), in_spec, out_spec, *held_specs],
+            out_specs=[
+                pl.BlockSpec((1, width, share), lambda r, at: (expert, 0, 0)),
+                pl.BlockSpec((1, share, width), lambda r, at: (expert, 0, 0)),
+            ],
+            scratch_shapes=[pltpu.VMEM((share, width), BF16), pltpu.VMEM((share, width), F32)],
+        ),
+        out_shape=[
+            jax.ShapeDtypeStruct((own, width, share), F32),
+            jax.ShapeDtypeStruct((own, share, width), F32),
+        ],
+        input_output_aliases={4 + i: i for i in range(len(held))},
+        compiler_params=pltpu.CompilerParams(vmem_limit_bytes=62 << 20),
+        cost_estimate=pl.CostEstimate(
+            flops=8 * count * width * share, bytes_accessed=2 * count * double, transcendentals=count * share
+        ),
+        name="share",
+    )(where, rows, w_in, w_out, *held)
+
+
+MESH = pl.DeviceIdType.MESH
+
+
+def remote(src, dst, send, recv, where):
+    copy = pltpu.make_async_remote_copy(src, dst, send, recv, device_id=where, device_id_type=MESH)
+    copy.start()
+    return copy
+
+
+def meet(peers):
+    barrier = pltpu.get_barrier_semaphore()
+    for where in peers:
+        pl.semaphore_signal(barrier, inc=1, device_id=where, device_id_type=MESH)
+    pl.semaphore_wait(barrier, len(peers))
+
+
+def far_first(total):
+    return sorted(range(1, total), key=lambda k: -min(k, total - k))
+
+
+def spread_kernel(parts, in_ref, out_ref, send, recv, pass_send, pass_recv, local):
+    total = lax.axis_size("seq")
+    me = lax.axis_index("seq")
+    part = lax.rem(me, parts)
+    meet([{"seq": lax.rem(me + k, total)} for k in range(1, total)])
+    copies = []
+    for k in far_first(total):
+        to = lax.rem(me + k, total)
+        copies.append(remote(in_ref.at[to], out_ref.at[me, lax.rem(to, parts)], send.at[k - 1], recv.at[k - 1], {"seq": to}))
+    own = pltpu.make_async_copy(in_ref.at[me], out_ref.at[me, part], local)
+    own.start()
+    own.wait()
+    passed = []
+
+    def forward(source, k):
+        for j in range(1, parts):
+            to = me - part + lax.rem(part + j, parts)
+            at = (j - 1) * total + k
+            block = out_ref.at[source, part]
+            passed.append(remote(block, block, pass_send.at[at], pass_recv.at[at], {"seq": to}))
+
+    forward(me, 0)
+    for k in far_first(total)[::-1]:
+        source = lax.rem(me - k + total, total)
+        block = out_ref.at[source, part]
+        pltpu.make_async_remote_copy(
+            block, block, send.at[k - 1], recv.at[k - 1], device_id={"seq": source}, device_id_type=MESH
+        ).wait_recv()
+        forward(source, k)
+    for copy in copies:
+        copy.wait_send()
+    for copy in passed:
+        copy.wait()
+
+
+def spread(blocks, parts):
+    total, rows, width = blocks.shape
+    passes = (parts - 1) * total
+    return pl.pallas_call(
+        functools.partial(spread_kernel, parts),
+        in_specs=[pl.BlockSpec(memory_space=pl.ANY)],
+        out_specs=pl.BlockSpec(memory_space=pl.ANY),
+        out_shape=jax.ShapeDtypeStruct((total, parts, rows, width), blocks.dtype),
+        scratch_shapes=[
+            pltpu.SemaphoreType.DMA((total - 1,)),
+            pltpu.SemaphoreType.DMA((total - 1,)),
+            pltpu.SemaphoreType.DMA((passes,)),
+            pltpu.SemaphoreType.DMA((passes,)),
+            pltpu.SemaphoreType.DMA,
+        ],
+        compiler_params=pltpu.CompilerParams(collective_id=0, has_side_effects=True),
+        name="spread",
+    )(blocks)
+
+
+def finish_kernel(
+    seqs,
+    grad_ref,
+    late_ref,
+    early_ref,
+    home_ref,
+    late_out,
+    early_out,
+    near,
+    summed,
+    wide_got,
+    wide_sum,
+    far_got,
+    early_got,
+    mine,
+    early_mine,
+    near_sems,
+    home_sems,
+    wide_sems,
+    far_sems,
+    early_sems,
+    last_sems,
+    last_early_sems,
+    local,
+):
+    total, across = lax.axis_size("seq"), lax.axis_size("wide")
+    parts = total // seqs
+    me, row = lax.axis_index("seq"), lax.axis_index("wide")
+    part, seq = lax.rem(me, parts), me // parts
+    base = me - part
+
+    def part_at(k):
+        return base + lax.rem(part + k, parts)
+
+    def seq_at(k):
+        return lax.rem(seq + k, seqs) * parts + part
+
+    def row_at(k):
+        return lax.rem(row + k, across)
+
+    peers = [{"seq": lax.rem(me + k, total)} for k in range(1, total)]
+    peers += [{"wide": row_at(k)} for k in range(1, across)]
+    pairs = [(a, b) for a in range(across) for b in range(parts) if a or b]
+    peers += [{"wide": row_at(a), "seq": part_at(b)} for a, b in pairs if a and b]
+    meet(peers)
+
+    near_copies = [
+        remote(
+            grad_ref.at[lax.rem(part + k, parts)],
+            near.at[k - 1],
+            near_sems.at[0, k - 1],
+            near_sems.at[1, k - 1],
+            {"seq": part_at(k)},
+        )
+        for k in range(1, parts)
+    ]
+    wide_copies = [
+        remote(late_ref.at[row_at(k)], wide_got.at[k - 1], wide_sems.at[0, k - 1], wide_sems.at[1, k - 1], {"wide": row_at(k)})
+        for k in range(1, across)
+    ]
+    for copy in near_copies:
+        copy.wait_recv()
+    home_copies = []
+    for k in far_first(total) + [0]:
+        to = lax.rem(me + k, total)
+        value = grad_ref[part, to].astype(F32)
+        for j in range(parts - 1):
+            value = value + near[j, to].astype(F32)
+        summed[to] = value.astype(BF16)
+        if k:
+            home_copies.append(
+                remote(summed.at[to], home_ref.at[me], home_sems.at[0, k - 1], home_sems.at[1, k - 1], {"seq": to})
+            )
+    own = pltpu.make_async_copy(summed.at[me], home_ref.at[me], local.at[0])
+    own.start()
+    for copy in wide_copies:
+        copy.wait_recv()
+    far_copies = []
+    for k in list(range(1, seqs)) + [0]:
+        at = lax.rem(seq + k, seqs)
+        for p in range(parts):
+            value = late_ref[row, at, p].astype(F32)
+            for j in range(across - 1):
+                value = value + wide_got[j, at, p].astype(F32)
+            wide_sum[at, p] = value.astype(BF16)
+        if k:
+            where = {"seq": seq_at(k)}
+            far_copies.append(
+                remote(wide_sum.at[at], far_got.at[k - 1], far_sems.at[0, k - 1], far_sems.at[1, k - 1], where)
+            )
+            far_copies.append(
+                remote(early_ref.at[at], early_got.at[k - 1], early_sems.at[0, k - 1], early_sems.at[1, k - 1], where)
+            )
+    for copy in far_copies:
+        copy.wait_recv()
+    for p in range(parts):
+        value = wide_sum[seq, p].astype(F32)
+        for j in range(seqs - 1):
+            value = value + far_got[j, p].astype(F32)
+        mine[p] = value.astype(BF16)
+    value = early_ref[seq].astype(F32)
+    for j in range(seqs - 1):
+        value = value + early_got[j].astype(F32)
+    early_mine[...] = value.astype(BF16)
+    last = []
+    for a, b in pairs:
+        at = a * parts + b - 1
+        last.append(
+            remote(
+                mine.at[lax.rem(part + b, parts)],
+                late_out.at[row, part],
+                last_sems.at[0, at],
+                last_sems.at[1, at],
+                {"wide": row_at(a), "seq": part_at(b)},
+            )
+        )
+    for k in range(1, across):
+        last.append(
+            remote(early_mine, early_out.at[row], last_early_sems.at[0, k - 1], last_early_sems.at[1, k - 1], {"wide": row_at(k)})
+        )
+    own_late = pltpu.make_async_copy(mine.at[part], late_out.at[row, part], local.at[1])
+    own_late.start()
+    own_early = pltpu.make_async_copy(early_mine, early_out.at[row], local.at[2])
+    own_early.start()
+    for copy in near_copies + wide_copies + far_copies:
+        copy.wait_send()
+    for copy in home_copies + last:
+        copy.wait()
+    own.wait()
+    own_late.wait()
+    own_early.wait()
+
+
+def finish(grads, late, early):
+    parts, total, rows, width = grads.shape
+    across, seqs, _, slim, columns = late.shape
+    early_columns = early.shape[2]
+    pair = pltpu.SemaphoreType.DMA
+    vmem = pl.BlockSpec(memory_space=pltpu.VMEM)
+    return pl.pallas_call(
+        functools.partial(finish_kernel, seqs),
+        in_specs=[vmem, vmem, vmem],
+        out_specs=[vmem, vmem, vmem],
+        out_shape=[
+            jax.ShapeDtypeStruct((total, rows, width), BF16),
+            jax.ShapeDtypeStruct((across, parts, slim, columns), BF16),
+            jax.ShapeDtypeStruct((across, slim, early_columns), BF16),
+        ],
+        scratch_shapes=[
+            pltpu.VMEM((parts - 1, total, rows, width), BF16),
+            pltpu.VMEM((total, rows, width), BF16),
+            pltpu.VMEM((across - 1, seqs, parts, slim, columns), BF16),
+            pltpu.VMEM((seqs, parts, slim, columns), BF16),
+            pltpu.VMEM((seqs - 1, parts, slim, columns), BF16),
+            pltpu.VMEM((seqs - 1, slim, early_columns), BF16),
+            pltpu.VMEM((parts, slim, columns), BF16),
+            pltpu.VMEM((slim, early_columns), BF16),
+            pair((2, parts - 1)),
+            pair((2, total - 1)),
+            pair((2, across - 1)),
+            pair((2, seqs - 1)),
+            pair((2, seqs - 1)),
+            pair((2, across * parts - 1)),
+            pair((2, across - 1)),
+            pair((3,)),
+        ],
+        compiler_params=pltpu.CompilerParams(collective_id=1, has_side_effects=True, vmem_limit_bytes=40 << 20),
+        cost_estimate=pl.CostEstimate(flops=0, bytes_accessed=100 << 20, transcendentals=0),
+        name="finish",
+    )(grads, late, early)
 
 
 def ring_pairs(total, parts, shift):
@@ -202,11 +563,6 @@
     return out
 
 
-def gather_parts(block, part, parts, total):
-    near = [block] + [lax.ppermute(block, "seq", ring_pairs(total, parts, k)) for k in range(1, parts)]
-    return [pick(near, (part - j) % parts) for j in range(parts)]
-
-
 def swap_parts(pieces, part, parts, total):
     near = [pick(pieces, part)]
     for k in range(1, parts):
@@ -214,17 +570,8 @@
     return [pick(near, (part - j) % parts) for j in range(parts)]
 
 
-def sum_replicated(own, seqs):
-    total, parts = lax.axis_size("seq"), lax.axis_size("seq") // seqs
-    across = lax.axis_size("wide")
-    _, rows, columns = own.shape
-    split = own.reshape(seqs, across, rows // across, columns).transpose(1, 0, 2, 3)
-    got = lax.all_to_all(split, "wide", 0, 0, tiled=True)
-    mine = jnp.sum(got.astype(F32), axis=0).astype(BF16)
-    groups = [[s * parts + p for s in range(seqs)] for p in range(parts)]
-    got = lax.all_to_all(mine, "seq", 0, 0, tiled=True, axis_index_groups=groups)
-    mine = jnp.sum(got.astype(F32), axis=0)
-    return lax.all_gather(mine.astype(BF16), "wide", axis=0, tiled=True).astype(F32)
+def head_groups(heads):
+    return [(0, heads - 2), (heads - 2, 2)] if heads % 2 == 0 and heads > 2 else [(0, heads)]
 
 
 def per_device(
@@ -262,8 +609,7 @@
     gain_one = gain_attn.astype(F32)
     gain_two = gain_ffn.astype(F32)
 
-    got = lax.all_to_all(inputs.reshape(total, local_len // parts, width), "seq", 0, 0, tiled=True)
-    seq_in = jnp.stack(gather_parts(got, part, parts, total), axis=1).reshape(length, width).astype(F32)
+    seq_in = spread(inputs.reshape(total, local_len // parts, width), parts).reshape(length, width).astype(F32)
     inv_one = inverse_rms(seq_in)
     normed_one = (seq_in * inv_one * gain_one).astype(BF16)
     own_weights = jnp.concatenate(
@@ -276,9 +622,14 @@
     reverse_hot = (ids[::-1][None, :] == jnp.arange(buckets, dtype=jnp.int32)[:, None]).astype(BF16)
     bias_line = contract(own_table, reverse_hot, 0, 0).reshape(heads, 1, 2 * length)
     block = 256
-    outs, exps, inverse = attend(qkv, bias_line, heads, size, length, block)
-
-    attended = lax.all_to_all(outs, "seq", 0, 0, tiled=True).reshape(seqs, width, local_len)
+    groups = head_groups(heads)
+    kept, attended = {}, {}
+    for first, count in groups[::-1]:
+        kept[first] = attend(qkv, bias_line, heads, first, count, size, length, block)
+        back = lax.all_to_all(kept[first][0], "seq", 0, 0, tiled=True)
+        attended[first] = back.reshape(seqs, parts, count * size, local_len)
+    attended = jnp.concatenate([attended[first] for first, _ in groups], axis=2).reshape(seqs, width, local_len)
+
     flat_in = inputs.reshape(tokens, width).astype(F32)
     middle = flat_in + jnp.einsum("sft,fe->ste", attended, w_output, preferred_element_type=F32).reshape(tokens, width)
     inv_two = inverse_rms(middle)
@@ -303,14 +654,7 @@
     for e in range(own_experts):
         received = lax.all_to_all(packed[e], "wide", 0, 0, tiled=True).reshape(across * capacity, 2 * width)
         gathered.append(lax.all_gather(received, "seq", axis=0, tiled=True))
-        rows_in, rows_grad = received[:, :width], received[:, width:]
-        pre_act = jnp.dot(rows_in, w_in[e], preferred_element_type=F32)
-        act, pullback = jax.vjp(smooth_act, pre_act)
-        expert_out = jnp.dot(act.astype(BF16), w_out[e], preferred_element_type=F32).astype(BF16)
-        grad_hidden = contract(rows_grad, w_out[e], 1, 1).astype(BF16)
-        grad_pre = pullback(grad_hidden.astype(F32))[0].astype(BF16)
-        grad_rows = contract(grad_pre, w_in[e], 1, 1).astype(BF16)
-        pair = jnp.concatenate([expert_out, grad_rows], axis=1).reshape(across, capacity, 2 * width)
+        pair = run_expert(received, w_in, w_out, e, 512).reshape(across, capacity, 2 * width)
         returned.append(lax.all_to_all(pair, "wide", 0, 0, tiled=True).reshape(across * capacity, 2 * width))
     token_rows = jnp.dot(slot_hot, jnp.concatenate(returned, axis=0), preferred_element_type=F32)
     selected, grad_token = token_rows[:, :width], token_rows[:, width:]
@@ -321,80 +665,81 @@
     grad_normed_two = grad_token + contract(grad_logits, w_router, 1, 1)
     grad_mid_norm, grad_gain_two = norm_backward(middle, inv_two, gain_two, grad_normed_two)
     grad_middle = upstream + grad_mid_norm
-    grad_branch = grad_middle.astype(BF16)
-    grad_att = jnp.einsum(
-        "ste,fe->sft", grad_branch.reshape(seqs, local_len, width), w_output, preferred_element_type=F32
-    ).astype(BF16)
-    grad_outs = lax.all_to_all(grad_att.reshape(total, cols, local_len), "seq", 0, 0, tiled=True)
-    grad_w_output = jnp.einsum(
-        "sft,ste->fe", attended, grad_branch.reshape(seqs, local_len, width), preferred_element_type=F32
-    )
-
-    dq, dk, dv, diagonal = attend_back(exps, inverse, grad_outs, outs, qkv, heads, size, length, block)
-    grads = jnp.concatenate([dq, dk, dv], axis=0)
-    grad_table = jnp.einsum(
-        "bo,ho->bh", bucket_hot.astype(F32), diagonal[:, 0, :], precision=lax.Precision.HIGHEST
-    )
-    grad_normed_one = contract(grads, own_weights, 0, 1)
+    grad_branch = grad_middle.astype(BF16).reshape(seqs, local_len, width)
+    split_output = w_output.reshape(parts, cols, width)
+    grad_outs = {}
+    for first, count in groups:
+        own = split_output[:, first * size : (first + count) * size]
+        grad_att = jnp.einsum("ste,pfe->spft", grad_branch, own, preferred_element_type=F32).astype(BF16)
+        grad_outs[first] = lax.all_to_all(grad_att.reshape(total, count * size, local_len), "seq", 0, 0, tiled=True)
+
+    share = width // total
+    slim = share // across
+    grad_w_output = jnp.einsum("sft,ste->fe", attended, grad_branch, preferred_element_type=F32)
+    early = jnp.concatenate(
+        [grad_w_output, grad_gain_two[:, None], grad_router, jnp.zeros((width, LANES - 1 - experts), F32)], axis=1
+    )
+    early = early.astype(BF16).reshape(seqs, parts, share, width + LANES)
+    early = swap_parts([early[:, p] for p in range(parts)], part, parts, total)
+    early = sum(p.astype(F32) for p in early).astype(BF16)
+    early = jnp.swapaxes(early.reshape(seqs, across, slim, width + LANES), 0, 1)
+    early = lax.all_to_all(early, "wide", 0, 0, tiled=True)
+    early = jnp.sum(early.astype(F32), axis=0).astype(BF16)
+
+    grad_normed_one = 0.0
+    own_weights = own_weights.reshape(width, 3, cols)
+    late, diagonals = [], []
+    for first, count in groups:
+        outs, exps, inverse = kept[first]
+        three, diagonal = attend_back(
+            exps, inverse, grad_outs[first], outs, qkv, heads, first, count, size, length, block
+        )
+        three = three.reshape(3 * count * size, length)
+        diagonals.append(diagonal[:, 0, :])
+        own = own_weights[:, :, first * size : (first + count) * size].reshape(width, 3 * count * size)
+        grad_normed_one = grad_normed_one + contract(three, own, 0, 1)
+        late.append(contract(normed_one, three, 0, 1))
     grad_in_norm, grad_gain_one = norm_backward(seq_in, inv_one, gain_one, grad_normed_one)
     pieces = grad_in_norm.astype(BF16).reshape(total, parts, local_len // parts, width)
-    swapped = swap_parts([pieces[:, p] for p in range(parts)], part, parts, total)
-    home = sum(p.astype(F32) for p in swapped).astype(BF16)
-    home = lax.all_to_all(home, "seq", 0, 0, tiled=True).reshape(tokens, width).astype(F32)
-    grad_inputs = (grad_middle + home).reshape(inputs.shape)
-    grad_w_qkv = contract(normed_one, grads, 0, 1).astype(BF16)
-
-    share = width // total
-    small = jnp.zeros((width, LANES), F32)
+    grad_table = jnp.einsum(
+        "bo,ho->bh", bucket_hot.astype(F32), jnp.concatenate(diagonals, axis=0), precision=lax.Precision.HIGHEST
+    )
     table_full = lax.dynamic_update_slice(jnp.zeros((buckets, head_count), F32), grad_table, (0, part * heads))
     table_rows = jnp.pad(table_full.reshape(total, -1), ((0, 0), (0, share - buckets * head_count // total)))
-    small = jnp.concatenate(
-        [
-            grad_gain_one[:, None],
-            table_rows.reshape(width, 1),
-            grad_gain_two[:, None],
-            grad_router,
-            jnp.zeros((width, LANES - 3 - experts), F32),
-        ],
-        axis=1,
-    )
-    summed = jnp.concatenate([grad_w_output, small], axis=1).astype(BF16)
-    summed = summed.reshape(seqs, parts, share, width + LANES)
-    summed = swap_parts([summed[:, p] for p in range(parts)], part, parts, total)
-    summed = sum(p.astype(F32) for p in summed).astype(BF16)
-    joined = grad_w_qkv.reshape(seqs, parts, share, 3, cols)
-    joined = swap_parts([joined[:, p] for p in range(parts)], part, parts, total)
-    joined = jnp.stack(joined, axis=3).reshape(seqs, share, 3 * width)
-    result = sum_replicated(jnp.concatenate([joined, summed], axis=2), seqs)
-    total_query, total_key, total_value, total_output, rest = jnp.split(
-        result, [width, 2 * width, 3 * width, 4 * width], axis=1
-    )
-    total_table = rest[: buckets * head_count // total, 1].reshape(buckets // total, head_count)
-
-    hidden_share = w_in.shape[2] // total
-    part_in, part_out = [], []
+    small = [grad_gain_one[:, None], table_rows.reshape(width, 1), jnp.zeros((width, LANES - 2), F32)]
+    late = jnp.concatenate([*late, *small], axis=1).astype(BF16)
+    late = late.reshape(seqs, parts, across, slim, late.shape[1]).transpose(2, 0, 1, 3, 4)
+    home, rows, early = finish(jnp.swapaxes(pieces, 0, 1), late, early)
+    grad_inputs = (grad_middle + home.reshape(tokens, width).astype(F32)).reshape(inputs.shape)
+    rows = [rows[:, p].reshape(share, rows.shape[3]) for p in range(parts)]
+    early = early.reshape(share, width + LANES).astype(F32)
+    tables, at = [[], [], []], 0
+    for _, count in groups:
+        for k in range(3):
+            tables[k].append((at, at + count * size))
+            at += count * size
+    total_query, total_key, total_value = (
+        jnp.concatenate([r[:, a:b] for r in rows for a, b in tables[k]], axis=1).astype(F32) for k in range(3)
+    )
+    small = sum(r[:, at : at + LANES].astype(F32) for r in rows)
+    total_table = small[: buckets * head_count // total, 1].reshape(buckets // total, head_count)
+    total_output, early = early[:, :width], early[:, width:]
+
+    held = []
     for e in range(own_experts):
-        rows_in, rows_grad = gathered[e][:, :width], gathered[e][:, width:]
-        in_share = lax.dynamic_slice(w_in[e], (0, me * hidden_share), (width, hidden_share))
-        out_share = lax.dynamic_slice(w_out[e], (me * hidden_share, 0), (hidden_share, width))
-        act, pullback = jax.vjp(smooth_act, jnp.dot(rows_in, in_share, preferred_element_type=F32))
-        grad_hidden = contract(rows_grad, out_share, 1, 1).astype(BF16)
-        grad_pre = pullback(grad_hidden.astype(F32))[0].astype(BF16)
-        part_in.append(contract(rows_in, grad_pre, 0, 0))
-        part_out.append(contract(act.astype(BF16), rows_grad, 0, 0))
+        held = run_share(me, gathered[e], w_in, w_out, e, total, held, 512)
     return (
         output,
         grad_inputs,
-        rest[:, 0],
+        small[:, 0],
         total_query,
         total_key,
         total_value,
         total_output,
         total_table,
-        rest[:, 2],
-        rest[:, 3 : 3 + experts],
-        jnp.stack(part_in),
-        jnp.stack(part_out),
+        early[:, 0],
+        early[:, 1 : 1 + experts],
+        *held,
     )
 
 

time: 487 us -> 385 us (0.79)
  Pallas kernels: 56.1 us -> 178 us
  waiting for transfers between devices: 109 us -> 27.5 us
  matrix products: 114 us -> 33.7 us
  local copies, waits for them, and re-layouts: 61.6 us -> 27.5 us
  blocking collectives: 55.9 us -> 32.2 us
  other arithmetic: 32.2 us -> 20.3 us
  starting transfers between devices: 34 us -> 43.5 us
    pallas_call x1 -> x8, Pallas kernels: 25.1 us -> 143 us  [the longest x1 47.4 us: finish(): pl.pallas_call(functools.partial(finish_kernel, seqs), in_specs=[vmem, vm...]
    all_to_all x6 -> x5, waiting for transfers between devices: 96.1 us -> 22.9 us  [the longest x2 15 us: per_device(): back = lax.all_to_all(kept[first][0], 'seq', 0, 0, tiled=True)]
    dot_general x13 -> x9, matrix products: 66.3 us -> 22 us  [contract(): lax.dot_general(a, b, (((da,), (db,)), ((), ())), preferred_element_type=...]
    dot_general x9 -> x4, matrix products: 41.6 us -> 5.84 us  [the longest x2 3.44 us: per_device(): jnp.einsum('ste,pfe->spft', grad_branch, own, preferred_element_type=F32)]
    all_to_all x1 -> x0, blocking collectives: 27.4 us -> none  [per_device(): lax.all_to_all(inputs.reshape(total, local_len // parts, width), 'seq', 0...]
    all_to_all x1 -> x2, blocking collectives: 17 us -> 32.2 us  [per_device(): lax.all_to_all(packed[e], 'wide', 0, 0, tiled=True)]
    slice x5 -> x10, local copies, waits for them, and re-layouts: 17.4 us -> 2.32 us  [the longest x1 0.73 us: per_device(): total_output, early = (early[:, :width], early[:, width:])]
    all_gather x1 -> x0, blocking collectives: 11.5 us -> none  [sum_replicated(): lax.all_gather(mine.astype(BF16), 'wide', axis=0, tiled=True).astype(F32)]
  transfers between devices with their start and end apart: 14 -> 10, of which waited for: 7 -> 4; matrix products, arithmetic and copies ran while one was open for 32% -> 16% of each run, Pallas kernels for 6% -> 36%
where the time goes in v2:
time: 385 us; the launch traced here: 377 us
  Pallas kernels  178 us (46%)
  starting transfers between devices  43.5 us (11%)
  matrix products  33.7 us (9%)
  blocking collectives  32.2 us (8%)
  local copies, waits for them, and re-layouts  27.5 us (7%)
  waiting for transfers between devices  27.5 us (7%)
  other arithmetic  20.3 us (5%)
  between operations  14.9 us (4%)
    pallas_call x1, Pallas kernels, finish(): pl.pallas_call(functools.partial(finish_kernel, seqs), in_specs=[vmem, vm...  47.4 us
    pallas_call x2, Pallas kernels, attend_back(): pl.pallas_call(functools.partial(attend_back_kernel, length, width), grid...  34.6 us
    all_to_all x2, blocking collectives, per_device(): lax.all_to_all(packed[e], 'wide', 0, 0, tiled=True)  32.2 us
    pallas_call x2, Pallas kernels, attend(): pl.pallas_call(functools.partial(attend_kernel, length, width), grid=(cou...  29.6 us
    pallas_call x2, Pallas kernels, run_share(): pl.pallas_call(share_kernel, grid_spec=pltpu.PrefetchScalarGridSpec(num_s...  22.8 us
    dot_general x9, matrix products, contract(): lax.dot_general(a, b, (((da,), (db,)), ((), ())), preferred_element_type=...  22 us
    pallas_call x1, Pallas kernels, spread(): pl.pallas_call(functools.partial(spread_kernel, parts), in_specs=[pl.Bloc...  21.8 us
    pallas_call x2, Pallas kernels, run_expert(): pl.pallas_call(expert_kernel, grid=(units // block,), in_specs=[pl.BlockS...  21.4 us
  transfers between devices with their start and end apart: 10, of which 4 were waited for; matrix products, arithmetic and copies ran while one was open for 16% of the time, Pallas kernels for 36%

profile of v2, /device:TPU:0, one launch (start us, length us, event | category | flops | bytes accessed | tf_op | source)
XLA Modules:
  0.0 377.4 jit_solution(4490060833075616984)
XLA Ops:
  7.2 21.8 %spread.1 = bf16[8,2,64,768]{3,2,1,0:T(8,128)(2,1)} custom-call(bf16[8,64,768]{2,1,0:T(8,128)(2,1)} %bitcast.183), custom_call_target="tpu_custom_call" | custom-call | tf_op jit(solution)/shard_map/spread/pallas_call | solution.py:366
  39.6 10.4 %attend.3 = (bf16[8,128,128]{2,1,0:T(8,128)(2,1)}, bf16[2,1024,1024]{2,1,0:T(8,128)(2,1)}, f32[2,1,1024]{2,1,0:T(1,128)}) custom-call(bf16[1152,1024]{1,0:T(8,128)(2,1)} %convolution_convert_fusion.q_ref.k_ref.v_ref, bf16[1152,1024]{1,0:T(8,128)(2,1)} %convolution_convert_fusion.q_ref.k_ref.v_ref, ...), custom_call_target="tpu_custom_call" | custom-call | flops 536870912 | bytes 4194304 | tf_op jit(solution)/shard_map/attend/pallas_call | solution.py:145
  50.0 6.8 %all-to-all-start.1 = ((bf16[8,128,128]{2,1,0:T(8,128)(2,1)}), bf16[8,128,128]{2,1,0:T(8,128)(2,1)S(1)}, u32[]{:S(2)}, u32[]{:S(2)}) async-start(bf16[8,128,128]{2,1,0:T(8,128)(2,1)} %get-tuple-element.30.out_ref), calls=%async_computation.1 | async-start | bytes 524288 | tf_op jit(solution)/shard_map/all_to_all | solution.py:629
  56.8 19.2 %attend.2 = (bf16[8,256,128]{2,1,0:T(8,128)(2,1)}, bf16[4,1024,1024]{2,1,0:T(8,128)(2,1)}, f32[4,1,1024]{2,1,0:T(1,128)}) custom-call(bf16[1152,1024]{1,0:T(8,128)(2,1)} %convolution_convert_fusion.q_ref.k_ref.v_ref, bf16[1152,1024]{1,0:T(8,128)(2,1)} %convolution_convert_fusion.q_ref.k_ref.v_ref, ...), custom_call_target="tpu_custom_call" | custom-call | flops 1073741824 | bytes 8388608 | tf_op jit(solution)/shard_map/attend/pallas_call | solution.py:145
  76.0 5.1 %all-to-all-start = ((bf16[8,256,128]{2,1,0:T(8,128)(2,1)}), bf16[8,256,128]{2,1,0:T(8,128)(2,1)S(1)}, u32[]{:S(2)}, u32[]{:S(2)}) async-start(bf16[8,256,128]{2,1,0:T(8,128)(2,1)} %get-tuple-element.29.out_ref), calls=%async_computation | async-start | bytes 1048576 | tf_op jit(solution)/shard_map/all_to_all | solution.py:629
  81.5 15.0 %all-to-all-done = bf16[8,256,128]{2,1,0:T(8,128)(2,1)S(1)} async-done(((bf16[8,256,128]{2,1,0:T(8,128)(2,1)}), bf16[8,256,128]{2,1,0:T(8,128)(2,1)S(1)}, u32[]{:S(2)}, u32[]{:S(2)}) %all-to-all-start) | async-done | bytes 524320 | tf_op jit(solution)/shard_map/all_to_all | solution.py:629
  103.5 17.0 %all_to_all.45 = bf16[4,80,1536]{2,1,0:T(8,128)(2,1)} all-to-all(bf16[4,80,1536]{2,1,0:T(8,128)(2,1)S(1)} %bitcast.162), channel_id=1, replica_groups=mesh['seq'=8,'wide'=4] {'wide'}, dimensions={0} | all-to-all | bytes 1966080 | tf_op jit(solution)/shard_map/all_to_all | solution.py:655
  120.6 15.2 %all_to_all.46 = bf16[4,80,1536]{2,1,0:T(8,128)(2,1)} all-to-all(bf16[4,80,1536]{2,1,0:T(8,128)(2,1)S(1)} %bitcast.161), channel_id=1, replica_groups=mesh['seq'=8,'wide'=4] {'wide'}, dimensions={0} | all-to-all | bytes 1966080 | tf_op jit(solution)/shard_map/all_to_all | solution.py:655
  135.8 10.7 %expert.3 = bf16[320,1536]{1,0:T(8,128)(2,1)} custom-call(bf16[320,1536]{1,0:T(8,128)(2,1)} %bitcast.160, bf16[2,768,3072]{2,1,0:T(8,128)(2,1)} %in_ref.7, bf16[2,3072,768]{2,1,0:T(8,128)(2,1)} %out_ref.7), custom_call_target="tpu_custom_call" | custom-call | flops 6039797760 | bytes 9437184 | tf_op jit(solution)/shard_map/expert/pallas_call | solution.py:226
  146.5 4.5 %all-to-all-start.5 = ((bf16[4,80,1536]{2,1,0:T(8,128)(2,1)}), bf16[4,80,1536]{2,1,0:T(8,128)(2,1)}, u32[]{:S(2)}, u32[]{:S(2)}) async-start(bf16[4,80,1536]{2,1,0:T(8,128)(2,1)} %bitcast.173), calls=%async_computation.5 | async-start | bytes 1966080 | tf_op jit(solution)/shard_map/all_to_all | solution.py:658
  151.1 10.7 %expert.2 = bf16[320,1536]{1,0:T(8,128)(2,1)} custom-call(bf16[320,1536]{1,0:T(8,128)(2,1)} %bitcast.158, bf16[2,768,3072]{2,1,0:T(8,128)(2,1)} %in_ref.7, bf16[2,3072,768]{2,1,0:T(8,128)(2,1)} %out_ref.7), custom_call_target="tpu_custom_call" | custom-call | flops 6039797760 | bytes 9437184 | tf_op jit(solution)/shard_map/expert/pallas_call | solution.py:226
  161.8 4.4 %all-to-all-start.3 = ((bf16[4,80,1536]{2,1,0:T(8,128)(2,1)}), bf16[4,80,1536]{2,1,0:T(8,128)(2,1)}, u32[]{:S(2)}, u32[]{:S(2)}) async-start(bf16[4,80,1536]{2,1,0:T(8,128)(2,1)} %bitcast.174), calls=%async_computation.3 | async-start | bytes 1966080 | tf_op jit(solution)/shard_map/all_to_all | solution.py:658
  173.0 4.6 %all-to-all-done.3 = bf16[4,80,1536]{2,1,0:T(8,128)(2,1)} async-done(((bf16[4,80,1536]{2,1,0:T(8,128)(2,1)}), bf16[4,80,1536]{2,1,0:T(8,128)(2,1)}, u32[]{:S(2)}, u32[]{:S(2)}) %all-to-all-start.3) | async-done | bytes 983072 | tf_op jit(solution)/shard_map/all_to_all | solution.py:658
  187.5 4.8 %all-to-all-start.7 = ((bf16[8,128,128]{2,1,0:T(8,128)(2,1)}), bf16[8,128,128]{2,1,0:T(8,128)(2,1)S(1)}, u32[]{:S(2)}, u32[]{:S(2)}) async-start(bf16[8,128,128]{2,1,0:T(8,128)(2,1)} %bitcast.33), calls=%async_computation.7 | async-start | bytes 524288 | tf_op jit(solution)/shard_map/all_to_all | solution.py:674
  202.1 4.2 %all-to-all-start.6 = ((bf16[8,256,128]{2,1,0:T(8,128)(2,1)}), bf16[8,256,128]{2,1,0:T(8,128)(2,1)}, u32[]{:S(2)}, u32[]{:S(2)}) async-start(bf16[8,256,128]{2,1,0:T(8,128)(2,1)} %bitcast.26), calls=%async_computation.6 | async-start | bytes 1048576 | tf_op jit(solution)/shard_map/all_to_all | solution.py:674
  206.3 12.1 %attend_back.3 = (bf16[3,128,1024]{2,1,0:T(8,128)(2,1)}, f32[2,1,2048]{2,1,0:T(1,128)}) custom-call(bf16[2,1024,1024]{2,1,0:T(8,128)(2,1)} %get-tuple-element.34.exp_ref, f32[2,1,1024]{2,1,0:T(1,128)} %get-tuple-element.35.inv_ref, bf16[8,128,128]{2,1,0:T(8,128)(2,1)} %copy-done.22, bf16[8,128,128]{2,1,0:T(8,128)(2,1)} %get-tuple-element.30.out_ref, ...), custom_call_target="tpu_custom_call" | custom-call | flops 1073741824 | bytes 4194304 | tf_op jit(solution)/shard_map/attend_back/pallas_call | solution.py:170
  223.3 3.9 %fusion.35 = f32[1024,768,1]{1,0,2:T(8,128)} fusion(bf16[3,128,1024]{2,1,0:T(8,128)(2,1)S(1)} %copy-done.25, bf16[768,3,384]{0,2,1:T(8,128)(2,1)} %bitcast.163), kind=kOutput, calls=%fused_computation.71 | convolution fusion | flops 603979776 | bytes 4521984 | tf_op jit(solution)/shard_map/dot_general | solution.py:17
  229.6 7.0 %all-to-all-done.6.grad_ref = bf16[8,256,128]{2,1,0:T(8,128)(2,1)} async-done(((bf16[8,256,128]{2,1,0:T(8,128)(2,1)}), bf16[8,256,128]{2,1,0:T(8,128)(2,1)}, u32[]{:S(2)}, u32[]{:S(2)}) %all-to-all-start.6) | async-done | bytes 524320 | tf_op jit(solution)/shard_map/all_to_all | solution.py:674
  236.6 13.2 %all-to-all-start.8 = ((bf16[4,4,24,896]{3,2,1,0:T(8,128)(2,1)}), bf16[4,4,24,896]{3,2,1,0:T(8,128)(2,1)}, u32[]{:S(2)}, u32[]{:S(2)}) async-start(bf16[4,4,24,896]{3,2,1,0:T(8,128)(2,1)} %bitcast.149), calls=%async_computation.8 | async-start | bytes 1376256 | tf_op jit(solution)/shard_map/all_to_all | solution.py:686
  249.8 22.5 %attend_back.2 = (bf16[3,256,1024]{2,1,0:T(8,128)(2,1)}, f32[4,1,2048]{2,1,0:T(1,128)}) custom-call(bf16[4,1024,1024]{2,1,0:T(8,128)(2,1)} %get-tuple-element.31.exp_ref, f32[4,1,1024]{2,1,0:T(1,128)} %get-tuple-element.32.inv_ref, bf16[8,256,128]{2,1,0:T(8,128)(2,1)} %all-to-all-done.6.grad_ref, bf16[8,256,128]{2,1,0:T(8,128)(2,1)} %get-tuple-element.29.out_ref, ...), custom_call_target="tpu_custom_call" | custom-call | flops 2147483648 | bytes 8388608 | tf_op jit(solution)/shard_map/attend_back/pallas_call | solution.py:170
  272.2 4.9 %fusion.10 = (bf16[768]{0:T(1024)(128)(2,1)S(1)}, f32[1024]{0:T(1024)S(1)}, f32[1024,768]{1,0:T(8,128)S(1)}) fusion(bf16[8,2,64,768]{3,2,1,0:T(8,128)(2,1)S(1)} %copy-done.5, f32[1024]{0:T(1024)S(1)} %rsqrt.27, f32[768]{0:T(1024)S(1)} %convert_element_type.139, f32[1024,768,1]{1,0,2:T(8,128)} %fusion.35, bf16[3,256,1024]{2,1,0:T(8,128)(2,1)} %get-tuple-element.33, ...), kind=kOutput, calls=%fused_computation.19 | convolution fusion | flops 1214249216 | bytes 10629632 | tf_op jit(solution)/shard_map/dot_general | solution.py:17
  291.9 47.4 %finish.1 = (bf16[8,64,768]{2,1,0:T(8,128)(2,1)S(1)}, bf16[4,2,24,1280]{3,2,1,0:T(8,128)(2,1)S(1)}, bf16[4,24,896]{2,1,0:T(8,128)(2,1)S(1)}) custom-call(bf16[2,8,64,768]{3,2,1,0:T(8,128)(2,1)S(1)} %bitcast.153, bf16[4,4,2,24,1280]{4,3,2,1,0:T(8,128)(2,1)S(1)} %bitcast.152, bf16[4,24,896]{2,1,0:T(8,128)(2,1)S(1)} %copy-done.4), custom_call_target="tpu_custom_call" | custom-call | bytes 104857600 | tf_op jit(solution)/shard_map/finish/pallas_call | solution.py:522
  347.5 11.4 %share.2 = (f32[2,768,384]{2,1,0:T(8,128)}, f32[2,384,768]{2,1,0:T(8,128)}) custom-call(s32[1]{0:T(128)} %bitcast.66.share_ref, bf16[2560,1536]{1,0:T(8,128)(2,1)} %all-gather.5.cloned.1.call-done.rows_ref, bf16[2,768,3072]{2,1,0:T(8,128)(2,1)} %in_ref.7, bf16[2,3072,768]{2,1,0:T(8,128)(2,1)} %out_ref.7), custom_call_target="tpu_custom_call" | custom-call | flops 6039797760 | bytes 7864320 | tf_op jit(solution)/shard_map/share/pallas_call | solution.py:283
  358.9 11.5 %share.3 = (f32[2,768,384]{2,1,0:T(8,128)}, f32[2,384,768]{2,1,0:T(8,128)}) custom-call(s32[1]{0:T(128)} %bitcast.66.share_ref, bf16[2560,1536]{1,0:T(8,128)(2,1)} %all-gather.3.cloned.1.call-done.rows_ref, bf16[2,768,3072]{2,1,0:T(8,128)(2,1)} %in_ref.7, bf16[2,3072,768]{2,1,0:T(8,128)(2,1)} %out_ref.7, ...), custom_call_target="tpu_custom_call", output_to_operand_aliasing={{0}: (4, {}), {1}: (5, {})} | custom-call | flops 6039797760 | bytes 7864320 | tf_op jit(solution)/shard_map/share/pallas_call | solution.py:283
  (170 shorter events, 74.2 us)
Async XLA Ops:
  7.2 25.7 %copy-start = (bf16[768,768]{1,0:T(8,128)(2,1)S(1)}, bf16[768,768]{1,0:T(8,128)(2,1)}, u32[]{:S(2)}) copy-start(bf16[768,768]{1,0:T(8,128)(2,1)} %param.18) | copy-start | bytes 3538948
  7.2 21.9 %copy-start.31 = (bf16[768]{0:T(1024)(128)(2,1)S(1)}, bf16[768]{0:T(1024)(128)(2,1)}, u32[]{:S(2)}) copy-start(bf16[768]{0:T(1024)(128)(2,1)} %param.17) | copy-start | bytes 4612
  32.6 3.5 copy-start.16
  32.9 3.3 copy-start.18
  50.0 26.0 %all-to-all-start.1 = ((bf16[8,128,128]{2,1,0:T(8,128)(2,1)}), bf16[8,128,128]{2,1,0:T(8,128)(2,1)S(1)}, u32[]{:S(2)}, u32[]{:S(2)}) async-start(bf16[8,128,128]{2,1,0:T(8,128)(2,1)} %get-tuple-element.30.out_ref), calls=%async_computation.1 | async-start | bytes 524288 | tf_op jit(solution)/shard_map/all_to_all | solution.py:629
  56.8 24.4 %copy-start.32 = (bf16[768]{0:T(1024)(128)(2,1)S(1)}, bf16[768]{0:T(1024)(128)(2,1)}, u32[]{:S(2)}) copy-start(bf16[768]{0:T(1024)(128)(2,1)} %param.23) | copy-start | bytes 4612
  56.8 24.4 %copy-start.27 = (s32[4,128,1]{1,2,0:T(1,128)S(1)}, s32[4,128,1]{1,2,0:T(1,128)}, u32[]{:S(2)}) copy-start(s32[4,128,1]{1,2,0:T(1,128)} %param.15) | copy-start | bytes 6148
  76.0 20.5 %all-to-all-start = ((bf16[8,256,128]{2,1,0:T(8,128)(2,1)}), bf16[8,256,128]{2,1,0:T(8,128)(2,1)S(1)}, u32[]{:S(2)}, u32[]{:S(2)}) async-start(bf16[8,256,128]{2,1,0:T(8,128)(2,1)} %get-tuple-element.29.out_ref), calls=%async_computation | async-start | bytes 1048576 | tf_op jit(solution)/shard_map/all_to_all | solution.py:629
  81.1 266.4 %all-gather.5.cloned.1.call-start = ((), (), s32[]{:S(2)}) async-start(), calls=%async_computation.10 | async-start | bytes 8847360 | tf_op jit(solution)/shard_map/all_gather | solution.py:656
  96.5 3.5 copy-start.15
  120.6 238.3 %all-gather.3.cloned.1.call-start = ((), (), s32[]{:S(2)}) async-start(), calls=%async_computation.9 | async-start | bytes 8847360 | tf_op jit(solution)/shard_map/all_gather | solution.py:656
  146.5 15.3 %all-to-all-start.5 = ((bf16[4,80,1536]{2,1,0:T(8,128)(2,1)}), bf16[4,80,1536]{2,1,0:T(8,128)(2,1)}, u32[]{:S(2)}, u32[]{:S(2)}) async-start(bf16[4,80,1536]{2,1,0:T(8,128)(2,1)} %bitcast.173), calls=%async_computation.5 | async-start | bytes 1966080 | tf_op jit(solution)/shard_map/all_to_all | solution.py:658
  161.8 4.4 %copy-start.5 = (bf16[8,2,64,768]{3,2,1,0:T(8,128)(2,1)S(1)}, bf16[8,2,64,768]{3,2,1,0:T(8,128)(2,1)}, u32[]{:S(2)}) copy-start(bf16[8,2,64,768]{3,2,1,0:T(8,128)(2,1)} %spread.1) | copy-start | bytes 4718596
  161.8 15.8 %all-to-all-start.3 = ((bf16[4,80,1536]{2,1,0:T(8,128)(2,1)}), bf16[4,80,1536]{2,1,0:T(8,128)(2,1)}, u32[]{:S(2)}, u32[]{:S(2)}) async-start(bf16[4,80,1536]{2,1,0:T(8,128)(2,1)} %bitcast.174), calls=%async_computation.3 | async-start | bytes 1966080 | tf_op jit(solution)/shard_map/all_to_all | solution.py:658
  187.5 14.6 %all-to-all-start.7 = ((bf16[8,128,128]{2,1,0:T(8,128)(2,1)}), bf16[8,128,128]{2,1,0:T(8,128)(2,1)S(1)}, u32[]{:S(2)}, u32[]{:S(2)}) async-start(bf16[8,128,128]{2,1,0:T(8,128)(2,1)} %bitcast.33), calls=%async_computation.7 | async-start | bytes 524288 | tf_op jit(solution)/shard_map/all_to_all | solution.py:674
  200.8 26.4 %collective-permute-start = (bf16[4,96,896]{2,1,0:T(8,128)(2,1)}, bf16[4,96,896]{2,1,0:T(8,128)(2,1)}, u32[]{:S(2)}, u32[]{:S(2)}) collective-permute-start(bf16[4,96,896]{2,1,0:T(8,128)(2,1)} %fusion.32), channel_id=1, source_target_pairs={{0,4},{4,0},{8,12},{12,8},{16,20},{20,16},{24,28},{28,24},{1,5},{5... | collective-permute-start | bytes 2064392 | tf_op jit(solution)/shard_map/ppermute | solution.py:569
  202.1 4.2 %copy-start.22 = (bf16[8,128,128]{2,1,0:T(8,128)(2,1)}, bf16[8,128,128]{2,1,0:T(8,128)(2,1)S(1)}, u32[]{:S(2)}) copy-start(bf16[8,128,128]{2,1,0:T(8,128)(2,1)S(1)} %all-to-all-done.7.grad_ref) | copy-start | bytes 786436
  202.1 34.5 %all-to-all-start.6 = ((bf16[8,256,128]{2,1,0:T(8,128)(2,1)}), bf16[8,256,128]{2,1,0:T(8,128)(2,1)}, u32[]{:S(2)}, u32[]{:S(2)}) async-start(bf16[8,256,128]{2,1,0:T(8,128)(2,1)} %bitcast.26), calls=%async_computation.6 | async-start | bytes 1048576 | tf_op jit(solution)/shard_map/all_to_all | solution.py:674
  219.8 3.5 copy-start.25
  223.3 4.0 %copy-start.9 = (bf16[4,2,96,896]{3,2,1,0:T(8,128)(2,1)S(1)}, bf16[4,2,96,896]{3,2,1,0:T(8,128)(2,1)}, u32[]{:S(2)}) copy-start(bf16[4,2,96,896]{3,2,1,0:T(8,128)(2,1)} %copy-done.8) | copy-start | bytes 4128772
  236.6 52.5 %all-to-all-start.8 = ((bf16[4,4,24,896]{3,2,1,0:T(8,128)(2,1)}), bf16[4,4,24,896]{3,2,1,0:T(8,128)(2,1)}, u32[]{:S(2)}, u32[]{:S(2)}) async-start(bf16[4,4,24,896]{3,2,1,0:T(8,128)(2,1)} %bitcast.149), calls=%async_computation.8 | async-start | bytes 1376256 | tf_op jit(solution)/shard_map/all_to_all | solution.py:686
  341.0 5.1 %copy-start.3 = (bf16[8,64,768]{2,1,0:T(8,128)(2,1)S(1)}, bf16[8,64,768]{2,1,0:T(8,128)(2,1)}, u32[]{:S(2)}) copy-start(bf16[8,64,768]{2,1,0:T(8,128)(2,1)} %copy-done.2) | copy-start | bytes 2359300
  341.1 5.1 %copy-start.14 = (f32[512,768]{1,0:T(8,128)S(1)}, f32[512,768]{1,0:T(8,128)}, u32[]{:S(2)}) copy-start(f32[512,768]{1,0:T(8,128)} %get-tuple-element.51) | copy-start | bytes 4718596
  358.9 11.5 %copy-start.1 = (bf16[768,768]{1,0:T(8,128)(2,1)S(1)}, bf16[768,768]{1,0:T(8,128)(2,1)}, u32[]{:S(2)}) copy-start(bf16[768,768]{1,0:T(8,128)(2,1)} %param.18) | copy-start | bytes 3538948
  (20 other events, 35.9 us)
Sparse Core Ops, SparseCore 0:
  120.7 75.3 all-gather.4
  197.7 87.3 all-gather.2

commit v3 on v1

v3 whole, which is shorter than its diff:
```python
import functools

import jax
import jax.numpy as jnp
from jax import lax
from jax.experimental import pallas as pl
from jax.experimental.pallas import tpu as pltpu
from jax.sharding import PartitionSpec as P

EPSILON = 1e-06
F32 = jnp.float32
BF16 = jnp.bfloat16
LANES = 128


def contract(a, b, da, db):
    return lax.dot_general(a, b, (((da,), (db,)), ((), ())), preferred_element_type=F32)


def inverse_rms(source):
    return lax.rsqrt(jnp.mean(source * source, axis=-1, keepdims=True) + EPSILON)


def norm_backward(source, inv_rms, gain_vec, upstream):
    scaled = upstream * gain_vec
    gain_grad = jnp.sum(upstream * source * inv_rms, axis=0)
    mean_inner = jnp.mean(source * scaled, axis=-1, keepdims=True)
    return (inv_rms * scaled - source * (inv_rms * inv_rms * inv_rms) * mean_inner, gain_grad)


def smooth_act(values):
    return jax.nn.gelu(values, approximate=True)


MESH = pl.DeviceIdType.MESH


def remote(src, dst, send, recv, where):
    copy = pltpu.make_async_remote_copy(src, dst, send, recv, device_id=where, device_id_type=MESH)
    copy.start()
    return copy


def meet(peers):
    barrier = pltpu.get_barrier_semaphore()
    for where in peers:
        pl.semaphore_signal(barrier, inc=1, device_id=where, device_id_type=MESH)
    pl.semaphore_wait(barrier, len(peers))


def far_first(total):
    return sorted(range(1, total), key=lambda k: -min(k, total - k))


def twist(a, b, total):
    out, bit = 0, 1
    while bit < total:
        out = out + lax.rem(lax.div(a, bit) + lax.div(b, bit), 2) * bit
        bit *= 2
    return out


def attend_kernel(
    qkv_ref, bias_ref, out_ref, home_ref, exp_ref, inv_ref, strip, keys, scores, held, send, recv, local, exp_sems
):
    _, heads, size, length = qkv_ref.shape
    total = lax.axis_size("seq")
    me = lax.axis_index("seq")
    tokens = out_ref.shape[3]
    width = 2 * tokens
    pairs = total // 2
    rows = 2 * length - tokens
    chunk = 256
    meet([{"seq": lax.rem(me + k, total)} for k in range(1, total)])

    def prepare(h, carry):
        keys[h] = qkv_ref[1, h].T
        for b in range(rows // tokens):
            start = 2 * length - 2 * tokens - tokens * b
            base = jnp.broadcast_to(bias_ref[h, :, start : start + 2 * tokens], (tokens, 2 * tokens))
            rolled = pltpu.roll(base, 0, 1, stride=1, stride_axis=0)
            strip[h, tokens * b : tokens * (b + 1), :] = rolled[:, tokens:]
        return carry

    lax.fori_loop(0, heads, prepare, 0)

    def store(slot, pair, h):
        return pltpu.make_async_copy(held.at[slot], exp_ref.at[pair, h], exp_sems.at[slot])

    def step(t, carry):
        pair = twist(lax.div(me, 2), pairs - 1 - t, pairs)
        at = pl.ds(pl.multiple_of(pair * width, tokens), width)

        def head(h, carry):
            count = t * heads + h
            slot = lax.rem(count, 2)

            @pl.when(count >= 2)
            def _():
                store(slot, pair, h).wait()

            query = qkv_ref[0, h, :, at]
            tops = [jnp.full((1, tokens), -jnp.inf, F32)] * 2
            for c in range(length // chunk):
                part = contract(keys[h, c * chunk : (c + 1) * chunk, :], query, 1, 0)
                for s in range(2):
                    row = pl.multiple_of(length - tokens - (pair * width + s * tokens) + c * chunk, tokens)
                    piece = part[:, s * tokens : (s + 1) * tokens] + strip[h, pl.ds(row, chunk), :]
                    scores[c * chunk : (c + 1) * chunk, s * tokens : (s + 1) * tokens] = piece
                    tops[s] = jnp.maximum(tops[s], jnp.max(piece, axis=0, keepdims=True))
            sums = [jnp.zeros((1, tokens), F32)] * 2
            for c in range(length // chunk):
                for s in range(2):
                    piece = scores[c * chunk : (c + 1) * chunk, s * tokens : (s + 1) * tokens]
                    grown = jnp.exp(piece - tops[s])
                    sums[s] = sums[s] + jnp.sum(grown, axis=0, keepdims=True)
                    held[slot, c * chunk : (c + 1) * chunk, s * tokens : (s + 1) * tokens] = grown.astype(BF16)
            store(slot, pair, h).start()
            mixed = contract(qkv_ref[2, h], held[slot], 1, 0)
            for s in range(2):
                inverse = 1.0 / sums[s]
                inv_ref[pair, h, :, s * tokens : (s + 1) * tokens] = inverse
                out_ref[2 * pair + s, h] = (mixed[:, s * tokens : (s + 1) * tokens] * inverse).astype(BF16)
            return carry

        lax.fori_loop(0, heads, head, 0)
        for s in range(2):
            to = 2 * pair + s
            k = twist(me, to, total)

            @pl.when(to != me)
            def _():
                pltpu.make_async_remote_copy(
                    out_ref.at[to], home_ref.at[me], send.at[k], recv.at[k], device_id={"seq": to}, device_id_type=MESH
                ).start()

        return carry

    lax.fori_loop(0, pairs, step, 0)
    own = pltpu.make_async_copy(out_ref.at[me], home_ref.at[me], local)
    own.start()
    for slot in range(2):
        store(slot, 0, 0).wait()

    def settle(k, carry):
        source = twist(me, k, total)
        pltpu.make_async_remote_copy(
            out_ref.at[source], home_ref.at[source], send.at[k], recv.at[k], device_id={"seq": source}, device_id_type=MESH
        ).wait()
        return carry

    lax.fori_loop(1, total, settle, 0)
    own.wait()


def attend(qkv, bias_line, total):
    _, heads, size, length = qkv.shape
    tokens = length // total
    vmem = pl.BlockSpec(memory_space=pltpu.VMEM)
    return pl.pallas_call(
        attend_kernel,
        in_specs=[vmem, vmem],
        out_specs=[vmem, vmem, pl.BlockSpec(memory_space=pl.ANY), vmem],
        out_shape=[
            jax.ShapeDtypeStruct((total, heads, size, tokens), BF16),
            jax.ShapeDtypeStruct((total, heads, size, tokens), BF16),
            jax.ShapeDtypeStruct((total // 2, heads, length, 2 * tokens), BF16),
            jax.ShapeDtypeStruct((total // 2, heads, 1, 2 * tokens), F32),
        ],
        scratch_shapes=[
            pltpu.VMEM((heads, 2 * length - tokens, tokens), F32),
            pltpu.VMEM((heads, length, size), BF16),
            pltpu.VMEM((length, 2 * tokens), F32),
            pltpu.VMEM((2, length, 2 * tokens), BF16),
            pltpu.SemaphoreType.DMA((total,)),
            pltpu.SemaphoreType.DMA((total,)),
            pltpu.SemaphoreType.DMA,
            pltpu.SemaphoreType.DMA((2,)),
        ],
        compiler_params=pltpu.CompilerParams(collective_id=2, has_side_effects=True, vmem_limit_bytes=62 << 20),
        cost_estimate=pl.CostEstimate(
            flops=4 * heads * length * length * size, bytes_accessed=2 * heads * length * length, transcendentals=heads * length * length
        ),
        name="attend",
    )(qkv, bias_line)


def attend_back_kernel(early, *refs):
    refs = list(refs)
    exp_ref, inv_ref, branch_ref, weight_ref, out_ref, qkv_ref, hot_ref = refs[:7]
    early_ref = refs.pop(7) if early else None
    three_ref, table_ref = refs[7:9]
    early_out = refs.pop(9) if early else None
    leaving, got, strip, values, dq_all, dk_sum, dv_sum, scores, held, diagonal, send, recv, exp_sems = refs[9:22]
    _, heads, size, length = qkv_ref.shape
    total = lax.axis_size("seq")
    me = lax.axis_index("seq")
    tokens = out_ref.shape[3]
    parts = weight_ref.shape[0]
    part = lax.rem(me, parts)
    width = 2 * tokens
    pairs = total // 2
    rows = 2 * length - tokens
    chunk = 256

    def pair_at(t):
        return twist(lax.div(me, 2), t, pairs)

    def load(count):
        slot = lax.rem(count, 2)
        at = exp_ref.at[pair_at(lax.div(count, heads)), lax.rem(count, heads)]
        return pltpu.make_async_copy(at, held.at[slot], exp_sems.at[slot])

    load(0).start()
    peers = [{"seq": lax.rem(me + k, total)} for k in range(1, total)]
    if early:
        across, row = lax.axis_size("wide"), lax.axis_index("wide")
        other = twist(me, 1, total)
        peers += [{"wide": lax.rem(row + k, across)} for k in range(1, across)]
    meet(peers)
    if early:
        near, near_sum, wide_got, near_sems, wide_sems = refs[22:]
        seqs = early_ref.shape[0]

        def near_copy():
            return pltpu.make_async_remote_copy(
                early_ref.at[:, lax.rem(part + 1, parts)],
                near,
                near_sems.at[0],
                near_sems.at[1],
                device_id={"seq": other},
                device_id_type=MESH,
            )

        def wide_copy(k):
            to = lax.rem(row + k, across)
            return pltpu.make_async_remote_copy(
                near_sum.at[to],
                wide_got.at[k - 1],
                wide_sems.at[0, k - 1],
                wide_sems.at[1, k - 1],
                device_id={"wide": to},
                device_id_type=MESH,
            )

        near_copy().start()

    def product(to):
        value = contract(weight_ref[lax.rem(to, parts)], branch_ref[lax.div(to, parts)], 1, 1)
        return value.astype(BF16).reshape(heads, size, tokens)

    def leave(k, carry):
        to = twist(me, k, total)
        leaving[to] = product(to)
        pltpu.make_async_remote_copy(
            leaving.at[to], got.at[me], send.at[k], recv.at[k], device_id={"seq": to}, device_id_type=MESH
        ).start()
        return carry

    lax.fori_loop(1, total, leave, 0)
    got[me] = product(me)

    def prepare(h, carry):
        values[h] = qkv_ref[2, h].T
        strip[h] = jnp.zeros(strip.shape[1:], F32)
        dk_sum[h] = jnp.zeros(dk_sum.shape[1:], F32)
        dv_sum[h] = jnp.zeros(dv_sum.shape[1:], F32)
        return carry

    lax.fori_loop(0, heads, prepare, 0)

    def arrive(k):
        source = twist(me, k, total)
        pltpu.make_async_remote_copy(
            leaving.at[source], got.at[source], send.at[k], recv.at[k], device_id={"seq": source}, device_id_type=MESH
        ).wait()

    def step(t, carry):
        pair = pair_at(t)
        at = pl.ds(pl.multiple_of(pair * width, tokens), width)

        @pl.when(t > 0)
        def _():
            arrive(2 * t)

        arrive(2 * t + 1)
        if early:

            @pl.when(t == 1)
            def _():
                near_copy().wait()
                for n in range(seqs):
                    for a in range(across):
                        value = early_ref[n, part, a].astype(F32) + near[n, a].astype(F32)
                        near_sum[a, n] = value.astype(BF16)
                for k in range(1, across):
                    wide_copy(k).start()

            @pl.when(t == pairs - 1)
            def _():
                for k in range(1, across):
                    wide_copy(k).wait()
                for n in range(seqs):
                    value = near_sum[row, n].astype(F32)
                    for k in range(1, across):
                        value = value + wide_got[k - 1, n].astype(F32)
                    early_out[n] = value.astype(BF16)

        def head(h, carry):
            count = t * heads + h
            slot = lax.rem(count, 2)

            @pl.when(count + 1 < pairs * heads)
            def _():
                load(count + 1).start()

            grads, inner = [], []
            for s in range(2):
                inverse = inv_ref[pair, h, :, s * tokens : (s + 1) * tokens]
                scaled = got[2 * pair + s, h].astype(F32) * inverse
                inner.append(jnp.sum(scaled * out_ref[2 * pair + s, h].astype(F32), axis=0, keepdims=True))
                grads.append(scaled.astype(BF16))
            grad = jnp.concatenate(grads, axis=1)
            load(count).wait()
            for c in range(length // chunk):
                part_grad = contract(values[h, c * chunk : (c + 1) * chunk, :], grad, 1, 0)
                for s in range(2):
                    grown = held[slot, c * chunk : (c + 1) * chunk, s * tokens : (s + 1) * tokens].astype(F32)
                    slope = grown * (part_grad[:, s * tokens : (s + 1) * tokens] - inner[s])
                    line = pl.multiple_of(length - tokens - (pair * width + s * tokens) + c * chunk, tokens)
                    strip[h, pl.ds(line, chunk), :] += slope
                    scores[c * chunk : (c + 1) * chunk, s * tokens : (s + 1) * tokens] = slope.astype(BF16)
            dq_all[h, at, :] = contract(qkv_ref[1, h], scores[...], 1, 0).T.astype(BF16)
            dk_sum[h] += contract(scores[...], qkv_ref[0, h, :, at].T, 1, 0)
            dv_sum[h] += contract(held[slot], grad.T, 1, 0)
            return carry

        lax.fori_loop(0, heads, head, 0)
        return carry

    lax.fori_loop(0, pairs, step, 0)
    down = lax.broadcasted_iota(jnp.int32, (tokens, tokens), 0)
    over = lax.broadcasted_iota(jnp.int32, (tokens, tokens), 1)
    mirror = (down + over == tokens - 1).astype(F32)
    cols = heads * size
    for c in range(length // chunk):
        here = slice(c * chunk, (c + 1) * chunk)
        for n, ref in enumerate((dq_all, dk_sum, dv_sum)):
            joined = jnp.concatenate([ref[h, here, :].astype(F32) for h in range(heads)], axis=1)
            three_ref[here, n * cols : (n + 1) * cols] = joined.astype(BF16)

    def close(h, carry):
        diagonal[h] = jnp.zeros(diagonal.shape[1:], F32)
        for b in range(rows // tokens):
            flipped = lax.dot_general(
                strip[h, tokens * b : tokens * (b + 1), :],
                mirror,
                (((1,), (0,)), ((), ())),
                precision=lax.Precision.HIGHEST,
                preferred_element_type=F32,
            )
            spread_out = jnp.concatenate([flipped, jnp.zeros_like(flipped)], axis=1)
            rolled = pltpu.roll(spread_out, 0, 1, stride=1, stride_axis=0)
            diagonal[h, :, tokens * b : tokens * (b + 2)] += jnp.sum(rolled, axis=0, keepdims=True)
        return carry

    lax.fori_loop(0, heads, close, 0)
    sums = jnp.concatenate([diagonal[h] for h in range(heads)], axis=0)
    table = lax.dot_general(
        hot_ref[...].astype(F32),
        sums,
        (((1,), (1,)), ((), ())),
        precision=lax.Precision.HIGHEST,
        preferred_element_type=F32,
    )
    column = lax.broadcasted_iota(jnp.int32, (heads, LANES), 1)
    first = lax.broadcasted_iota(jnp.int32, (heads, LANES), 0) + part * heads
    table_ref[...] = lax.dot_general(
        table,
        (column == first).astype(F32),
        (((1,), (0,)), ((), ())),
        precision=lax.Precision.HIGHEST,
        preferred_element_type=F32,
    )


def attend_back(exps, inverse, branch, weight, outs, qkv, hot, early):
    _, heads, size, length = qkv.shape
    total, tokens = outs.shape[0], outs.shape[3]
    vmem = pl.BlockSpec(memory_space=pltpu.VMEM)
    sems = pltpu.SemaphoreType.DMA
    out_shape = [
        jax.ShapeDtypeStruct((length, 3 * heads * size), BF16),
        jax.ShapeDtypeStruct((hot.shape[0], LANES), F32),
    ]
    more, given = [], []
    if early is not None:
        seqs, _, across, slim, columns = early.shape
        given = [early]
        out_shape.append(jax.ShapeDtypeStruct((seqs, slim, columns), BF16))
        more = [
            pltpu.VMEM((seqs, across, slim, columns), BF16),
            pltpu.VMEM((across, seqs, slim, columns), BF16),
            pltpu.VMEM((across - 1, seqs, slim, columns), BF16),
            sems((2,)),
            sems((2, across - 1)),
        ]
    return pl.pallas_call(
        functools.partial(attend_back_kernel, early is not None),
        in_specs=[pl.BlockSpec(memory_space=pl.ANY)] + [vmem] * (6 + len(given)),
        out_specs=[vmem] * len(out_shape),
        out_shape=out_shape,
        scratch_shapes=[
            pltpu.VMEM((total, heads, size, tokens), BF16),
            pltpu.VMEM((total, heads, size, tokens), BF16),
            pltpu.VMEM((heads, 2 * length - tokens, tokens), F32),
            pltpu.VMEM((heads, length, size), BF16),
            pltpu.VMEM((heads, length, size), BF16),
            pltpu.VMEM((heads, length, size), F32),
            pltpu.VMEM((heads, length, size), F32),
            pltpu.VMEM((length, 2 * tokens), BF16),
            pltpu.VMEM((2, length, 2 * tokens), BF16),
            pltpu.VMEM((heads, 1, 2 * length), F32),
            sems((total,)),
            sems((total,)),
            sems((2,)),
            *more,
        ],
        compiler_params=pltpu.CompilerParams(collective_id=3, has_side_effects=True, vmem_limit_bytes=62 << 20),
        cost_estimate=pl.CostEstimate(
            flops=8 * heads * length * length * size, bytes_accessed=2 * heads * length * length, transcendentals=0
        ),
        name="attend_back",
    )(exps, inverse, branch, weight, outs, qkv, hot, *given)


def activation(v):
    square = v * v
    bent = jnp.tanh(0.7978845608 * v * (1.0 + 0.044715 * square))
    half = 0.5 * (1.0 + bent)
    slope = half + 0.5 * v * (1.0 - bent * bent) * (0.7978845608 * (1.0 + 3.0 * 0.044715 * square))
    return v * half, slope


def gated(rows, cots):
    width = cots.shape[1]
    gate = rows[:, width : width + 1].astype(F32) + rows[:, width + 1 : width + 2].astype(F32)
    return rows[:, :width], (gate * cots.astype(F32)).astype(BF16)


def expert_kernel(rows_ref, cot_ref, in_ref, out_ref, both_ref, forward, backward):
    step = pl.program_id(0)
    width = cot_ref.shape[1]

    @pl.when(step == 0)
    def _():
        forward[...] = jnp.zeros_like(forward)
        backward[...] = jnp.zeros_like(backward)

    rows, grads = gated(rows_ref[...], cot_ref[...])
    hidden, slope = activation(contract(rows, in_ref[0], 1, 0))
    grad_hidden = contract(grads, out_ref[0], 1, 1).astype(BF16).astype(F32)
    forward[...] += contract(hidden.astype(BF16), out_ref[0], 1, 0)
    backward[...] += contract((grad_hidden * slope).astype(BF16), in_ref[0], 1, 1)

    @pl.when(step == pl.num_programs(0) - 1)
    def _():
        both_ref[:, :width] = forward[...].astype(BF16)
        both_ref[:, width:] = backward[...].astype(BF16)


def run_expert(rows, cots, w_in, w_out, expert, block):
    count, width = cots.shape
    units = w_in.shape[2]
    return pl.pallas_call(
        expert_kernel,
        grid=(units // block,),
        in_specs=[
            pl.BlockSpec(rows.shape, lambda f: (0, 0)),
            pl.BlockSpec(cots.shape, lambda f: (0, 0)),
            pl.BlockSpec((1, width, block), lambda f: (expert, 0, f)),
            pl.BlockSpec((1, block, width), lambda f: (expert, f, 0)),
        ],
        out_specs=pl.BlockSpec((count, 2 * width), lambda f: (0, 0)),
        out_shape=jax.ShapeDtypeStruct((count, 2 * width), BF16),
        scratch_shapes=[pltpu.VMEM((count, width), F32), pltpu.VMEM((count, width), F32)],
        compiler_params=pltpu.CompilerParams(vmem_limit_bytes=40 << 20),
        name="expert",
    )(rows, cots, w_in, w_out)


def exchange_kernel(axis, in_ref, out_ref, send, recv, local):
    total = lax.axis_size(axis)
    me = lax.axis_index(axis)
    own = in_ref.shape[0]
    count = in_ref.shape[1] // total
    meet([{axis: lax.rem(me + k, total)} for k in range(1, total)])
    copies = []
    mine = pl.ds(me * count, count)
    for n in range(own):
        for k in range(1, total):
            to = lax.rem(me + k, total)
            copies.append(
                remote(
                    in_ref.at[n, pl.ds(to * count, count)],
                    out_ref.at[n, mine],
                    send.at[n, k - 1],
                    recv.at[n, k - 1],
                    {axis: to},
                )
            )
    kept = [pltpu.make_async_copy(in_ref.at[n, mine], out_ref.at[n, mine], local.at[n]) for n in range(own)]
    for copy in kept:
        copy.start()
    for copy in kept + copies:
        copy.wait()


def exchange(rows, axis):
    total = lax.axis_size(axis)
    own = rows.shape[0]
    vmem = pl.BlockSpec(memory_space=pltpu.VMEM)
    return pl.pallas_call(
        functools.partial(exchange_kernel, axis),
        in_specs=[vmem],
        out_specs=pl.BlockSpec(memory_space=pl.ANY),
        out_shape=jax.ShapeDtypeStruct(rows.shape, rows.dtype),
        scratch_shapes=[
            pltpu.SemaphoreType.DMA((own, total - 1)),
            pltpu.SemaphoreType.DMA((own, total - 1)),
            pltpu.SemaphoreType.DMA((own,)),
        ],
        compiler_params=pltpu.CompilerParams(collective_id=4, has_side_effects=True, vmem_limit_bytes=62 << 20),
        name="exchange",
    )(rows)


def experts_kernel(
    block,
    rows_ref,
    cot_ref,
    in_ref,
    out_ref,
    back_ref,
    done,
    grads,
    forward,
    backward,
    in_held,
    out_held,
    back_send,
    back_recv,
    local,
    held_sems,
):
    own, rows, double = back_ref.shape
    width = double // 2
    across = lax.axis_size("wide")
    me = lax.axis_index("wide")
    count = rows // across
    steps = in_ref.shape[2] // block

    def load(at):
        slot = lax.rem(at, 2)
        expert, place = lax.div(at, steps), pl.multiple_of(lax.rem(at, steps) * block, block)
        return (
            pltpu.make_async_copy(in_ref.at[expert, :, pl.ds(place, block)], in_held.at[slot], held_sems.at[0, slot]),
            pltpu.make_async_copy(out_ref.at[expert, pl.ds(place, block), :], out_held.at[slot], held_sems.at[1, slot]),
        )

    for copy in load(0):
        copy.start()
    meet([{"wide": lax.rem(me + k, across)} for k in range(1, across)])
    coming = []
    mine = pl.ds(me * count, count)
    for e in range(own):
        grads[...] = gated(rows_ref[e], cot_ref[e])[1]
        forward[...] = jnp.zeros_like(forward)
        backward[...] = jnp.zeros_like(backward)

        def step(f, carry):
            at = e * steps + f
            slot = lax.rem(at, 2)

            @pl.when(at + 1 < own * steps)
            def _():
                for copy in load(at + 1):
                    copy.start()

            for copy in load(at):
                copy.wait()
            hidden, slope = activation(contract(rows_ref[e, :, :width], in_held[slot], 1, 0))
            grad_hidden = contract(grads[...], out_held[slot], 1, 1).astype(BF16).astype(F32)
            forward[...] += contract(hidden.astype(BF16), out_held[slot], 1, 0)
            backward[...] += contract((grad_hidden * slope).astype(BF16), in_held[slot], 1, 1)
            return carry

        lax.fori_loop(0, steps, step, 0)
        done[e, :, :width] = forward[...].astype(BF16)
        done[e, :, width:] = backward[...].astype(BF16)
        for k in range(1, across):
            to = lax.rem(me + k, across)
            coming.append(
                remote(
                    done.at[e, pl.ds(to * count, count)],
                    back_ref.at[e, mine],
                    back_send.at[e, k - 1],
                    back_recv.at[e, k - 1],
                    {"wide": to},
                )
            )
        kept = pltpu.make_async_copy(done.at[e, mine], back_ref.at[e, mine], local.at[e])
        kept.start()
        kept.wait()
    for copy in coming:
        copy.wait()


def run_experts(rows, cots, w_in, w_out, block):
    own, count, width = cots.shape
    units = w_in.shape[2]
    across = lax.axis_size("wide")
    vmem, hbm = pl.BlockSpec(memory_space=pltpu.VMEM), pl.BlockSpec(memory_space=pl.ANY)
    sems = pltpu.SemaphoreType.DMA
    return pl.pallas_call(
        functools.partial(experts_kernel, block),
        in_specs=[vmem, vmem, hbm, hbm],
        out_specs=vmem,
        out_shape=jax.ShapeDtypeStruct((own, count, 2 * width), BF16),
        scratch_shapes=[
            pltpu.VMEM((own, count, 2 * width), BF16),
            pltpu.VMEM((count, width), BF16),
            pltpu.VMEM((count, width), F32),
            pltpu.VMEM((count, width), F32),
            pltpu.VMEM((2, width, block), BF16),
            pltpu.VMEM((2, block, width), BF16),
            sems((own, across - 1)),
            sems((own, across - 1)),
            sems((own,)),
            sems((2, 2)),
        ],
        compiler_params=pltpu.CompilerParams(collective_id=5, has_side_effects=True, vmem_limit_bytes=62 << 20),
        cost_estimate=pl.CostEstimate(
            flops=8 * own * count * width * units, bytes_accessed=4 * own * width * units, transcendentals=own * count * units
        ),
        name="experts",
    )(rows, cots, w_in, w_out)


def share_kernel(share_ref, rows_ref, cot_ref, in_ref, out_ref, *refs):
    grad_in_ref, grad_out_ref, flipped, total_in = refs[-4:]
    step = pl.program_id(0)

    @pl.when(step == 0)
    def _():
        flipped[...] = in_ref[0].T
        total_in[...] = jnp.zeros_like(total_in)
        grad_out_ref[...] = jnp.zeros_like(grad_out_ref)

    rows, grads = gated(rows_ref[0], cot_ref[0])
    hidden, slope = activation(contract(flipped[...], rows, 1, 1))
    grad_hidden = contract(out_ref[0], grads, 1, 1).astype(BF16).astype(F32)
    grad_out_ref[0] += contract(hidden.astype(BF16), grads, 1, 0)
    total_in[...] += contract((grad_hidden * slope).astype(BF16), rows, 1, 0)

    @pl.when(step == pl.num_programs(0) - 1)
    def _():
        grad_in_ref[0] = total_in[...].T


def run_share(me, rows, cots, w_in, w_out, expert, held):
    own, width, units = w_in.shape
    sources, count = rows.shape[0] // own, rows.shape[1]
    share = units // sources
    if share % LANES == 0:
        where = jnp.full((1,), me, jnp.int32)
        in_spec = pl.BlockSpec((1, width, share), lambda r, at: (expert, 0, at[0]))
        out_spec = pl.BlockSpec((1, share, width), lambda r, at: (expert, at[0], 0))
    else:
        where = jnp.zeros((1,), jnp.int32)
        w_in = lax.dynamic_slice(w_in, (0, 0, me * share), (own, width, share))
        w_out = lax.dynamic_slice(w_out, (0, me * share, 0), (own, share, width))
        in_spec = pl.BlockSpec((1, width, share), lambda r, at: (expert, 0, 0))
        out_spec = pl.BlockSpec((1, share, width), lambda r, at: (expert, 0, 0))
    held_specs = [pl.BlockSpec(memory_space=pl.ANY)] * len(held)
    return pl.pallas_call(
        share_kernel,
        grid_spec=pltpu.PrefetchScalarGridSpec(
            num_scalar_prefetch=1,
            grid=(sources,),
            in_specs=[
                pl.BlockSpec((1, count, rows.shape[2]), lambda r, at: (own * r + expert, 0, 0)),
                pl.BlockSpec((1, count, width), lambda r, at: (own * r + expert, 0, 0)),
                in_spec,
                out_spec,
                *held_specs,
            ],
            out_specs=[
                pl.BlockSpec((1, width, share), lambda r, at: (expert, 0, 0)),
                pl.BlockSpec((1, share, width), lambda r, at: (expert, 0, 0)),
            ],
            scratch_shapes=[pltpu.VMEM((share, width), BF16), pltpu.VMEM((share, width), F32)],
        ),
        out_shape=[
            jax.ShapeDtypeStruct((own, width, share), F32),
            jax.ShapeDtypeStruct((own, share, width), F32),
        ],
        input_output_aliases={5 + i: i for i in range(len(held))},
        compiler_params=pltpu.CompilerParams(vmem_limit_bytes=62 << 20),
        cost_estimate=pl.CostEstimate(
            flops=8 * sources * count * width * share, bytes_accessed=4 * sources * count * width, transcendentals=0
        ),
        name="share",
    )(where, rows, cots, w_in, w_out, *held)


def spread_kernel(parts, in_ref, out_ref, send, recv, pass_send, pass_recv, local):
    total = lax.axis_size("seq")
    me = lax.axis_index("seq")
    part = lax.rem(me, parts)
    meet([{"seq": lax.rem(me + k, total)} for k in range(1, total)])
    copies = []
    for k in far_first(total):
        to = lax.rem(me + k, total)
        copies.append(remote(in_ref.at[to], out_ref.at[me, lax.rem(to, parts)], send.at[k - 1], recv.at[k - 1], {"seq": to}))
    own = pltpu.make_async_copy(in_ref.at[me], out_ref.at[me, part], local)
    own.start()
    own.wait()
    passed = []

    def forward(source, k):
        for j in range(1, parts):
            to = me - part + lax.rem(part + j, parts)
            at = (j - 1) * total + k
            block = out_ref.at[source, part]
            passed.append(remote(block, block, pass_send.at[at], pass_recv.at[at], {"seq": to}))

    forward(me, 0)
    for k in far_first(total)[::-1]:
        source = lax.rem(me - k + total, total)
        block = out_ref.at[source, part]
        pltpu.make_async_remote_copy(
            block, block, send.at[k - 1], recv.at[k - 1], device_id={"seq": source}, device_id_type=MESH
        ).wait_recv()
        forward(source, k)
    for copy in copies:
        copy.wait_send()
    for copy in passed:
        copy.wait()


def spread(blocks, parts):
    total, rows, width = blocks.shape
    passes = (parts - 1) * total
    return pl.pallas_call(
        functools.partial(spread_kernel, parts),
        in_specs=[pl.BlockSpec(memory_space=pl.ANY)],
        out_specs=pl.BlockSpec(memory_space=pl.ANY),
        out_shape=jax.ShapeDtypeStruct((total, parts, rows, width), blocks.dtype),
        scratch_shapes=[
            pltpu.SemaphoreType.DMA((total - 1,)),
            pltpu.SemaphoreType.DMA((total - 1,)),
            pltpu.SemaphoreType.DMA((passes,)),
            pltpu.SemaphoreType.DMA((passes,)),
            pltpu.SemaphoreType.DMA,
        ],
        compiler_params=pltpu.CompilerParams(collective_id=0, has_side_effects=True),
        name="spread",
    )(blocks)


def begin_kernel(
    capacity,
    in_ref,
    query_ref,
    key_ref,
    value_ref,
    gain_ref,
    routes_ref,
    base_ref,
    cot_ref,
    all_ref,
    qkv_ref,
    flip_ref,
    hot_ref,
    rows_ref,
    weights,
    packed,
    send,
    recv,
    pass_send,
    pass_recv,
    wide_send,
    wide_recv,
    local,
):
    total, parts, rows, width = all_ref.shape
    _, heads, size, _ = qkv_ref.shape
    own = rows_ref.shape[0]
    cols = heads * size
    across = lax.axis_size("wide")
    me, row = lax.axis_index("seq"), lax.axis_index("wide")
    part = lax.rem(me, parts)
    other = twist(me, 1, total)
    pairs = total // 2
    peers = [{"seq": lax.rem(me + k, total)} for k in range(1, total)]
    peers += [{"wide": lax.rem(row + k, across)} for k in range(1, across)]
    meet(peers)
    sent = []
    for k in range(total - 1, 0, -1):
        to = twist(me, k, total)
        sent.append(remote(in_ref.at[to], all_ref.at[me, lax.rem(to, parts)], send.at[to], recv.at[me], {"seq": to}))
    kept = pltpu.make_async_copy(in_ref.at[me], all_ref.at[me, part], local.at[0])
    kept.start()
    kept.wait()
    passed = []

    def forward(source):
        block = all_ref.at[source, part]
        passed.append(remote(block, block, pass_send.at[source], pass_recv.at[source], {"seq": other}))

    def await_recv(block, sem):
        pltpu.make_async_remote_copy(
            block, block, local.at[1], sem, device_id={"seq": other}, device_id_type=MESH
        ).wait_recv()

    forward(me)

    tokens, slots = hot_ref.shape
    picked = (routes_ref[...] == lax.broadcasted_iota(jnp.int32, (tokens, LANES), 1)).astype(F32)
    down = lax.broadcasted_iota(jnp.int32, (tokens, tokens), 0)
    over = lax.broadcasted_iota(jnp.int32, (tokens, tokens), 1)
    earlier = contract((over < down).astype(F32).astype(BF16), picked.astype(BF16), 1, 0)
    rank = jnp.sum(earlier * picked, axis=1, keepdims=True)
    place = jnp.sum(base_ref[...] * picked, axis=1, keepdims=True) + rank
    place = jnp.where(rank < capacity, place, float(slots)).astype(jnp.int32)
    hot = (place == lax.broadcasted_iota(jnp.int32, (tokens, slots), 1)).astype(F32).astype(BF16)
    hot_ref[...] = hot
    packed[...] = contract(hot, cot_ref[...], 0, 0).astype(BF16).reshape(packed.shape)
    wide = []
    mine = pl.ds(row * capacity, capacity)
    for e in range(own):
        for k in range(1, across):
            to = lax.rem(row + k, across)
            wide.append(
                remote(
                    packed.at[e, pl.ds(to * capacity, capacity)],
                    rows_ref.at[e, mine],
                    wide_send.at[e, k - 1],
                    wide_recv.at[e, k - 1],
                    {"wide": to},
                )
            )
    stay = [pltpu.make_async_copy(packed.at[e, mine], rows_ref.at[e, mine], local.at[2 + e]) for e in range(own)]
    for copy in stay:
        copy.start()
    at = pl.ds(pl.multiple_of(part * cols, LANES), cols)
    for n, ref in enumerate((query_ref, key_ref, value_ref)):
        weights[n * cols : (n + 1) * cols, :] = ref[:, at].T

    for t in range(pairs):
        pair = twist(lax.div(me, 2), t, pairs)
        for b in range(2):
            if 2 * t + b:
                source = twist(me, 2 * t + b, total)
                await_recv(all_ref.at[source, part], recv.at[source])
                forward(source)
        for b in range(2):
            source = 2 * pair + b
            await_recv(all_ref.at[source, lax.rem(part + 1, parts)], pass_recv.at[source])
        block = all_ref[pl.ds(2 * pair, 2)].reshape(2 * parts * rows, width).astype(F32)
        normed = (block * inverse_rms(block) * gain_ref[...]).astype(BF16)
        here = pl.ds(pl.multiple_of(pair * (2 * parts * rows), LANES), 2 * parts * rows)
        flip_ref[:, here] = normed.T
        projected = contract(weights[...], normed, 1, 1).astype(BF16)
        qkv_ref[:, :, :, here] = projected.reshape(3, heads, size, 2 * parts * rows)
    for copy in sent + passed:
        copy.wait_send()
    for copy in wide + stay:
        copy.wait()


def begin(blocks, w_query, w_key, w_value, gain, routes, base, cot, heads, size, own, capacity):
    total, rows, width = blocks.shape
    tokens = cot.shape[0]
    across = lax.axis_size("wide")
    slots = own * across * capacity
    length = total * 2 * rows
    vmem = pl.BlockSpec(memory_space=pltpu.VMEM)
    sems = pltpu.SemaphoreType.DMA
    return pl.pallas_call(
        functools.partial(begin_kernel, capacity),
        in_specs=[vmem] * 8,
        out_specs=[vmem] * 5,
        out_shape=[
            jax.ShapeDtypeStruct((total, 2, rows, width), BF16),
            jax.ShapeDtypeStruct((3, heads, size, length), BF16),
            jax.ShapeDtypeStruct((width, length), BF16),
            jax.ShapeDtypeStruct((tokens, slots), BF16),
            jax.ShapeDtypeStruct((own, across * capacity, width), BF16),
        ],
        scratch_shapes=[
            pltpu.VMEM((3 * heads * size, width), BF16),
            pltpu.VMEM((own, across * capacity, width), BF16),
            sems((total,)),
            sems((total,)),
            sems((total,)),
            sems((total,)),
            sems((own, across - 1)),
            sems((own, across - 1)),
            sems((2 + own,)),
        ],
        compiler_params=pltpu.CompilerParams(collective_id=6, has_side_effects=True, vmem_limit_bytes=62 << 20),
        cost_estimate=pl.CostEstimate(flops=4 << 30, bytes_accessed=80 << 20, transcendentals=0),
        name="begin",
    )(blocks, w_query, w_key, w_value, gain, routes, base, cot)


def finish_kernel(
    seqs,
    three_ref,
    flip_ref,
    weight_ref,
    x_ref,
    gain_ref,
    early_ref,
    tiny_ref,
    table_ref,
    rows_ref,
    cots_ref,
    in_ref,
    out_ref,
    home_ref,
    query_out,
    key_out,
    value_out,
    output_out,
    tiny_out,
    table_out,
    grad_in_ref,
    grad_out_ref,
    grads,
    near,
    summed,
    gw,
    wide_got,
    wide_sum,
    far_got,
    early_got,
    mine,
    early_mine,
    late_all,
    early_all,
    tiny,
    tiny_got,
    table,
    table_got,
    rows_held,
    cots_held,
    in_held,
    out_held,
    sums,
    total_in,
    leaving,
    share_got,
    share_sems,
    near_sems,
    home_sems,
    wide_sems,
    far_sems,
    early_sems,
    last_sems,
    last_early_sems,
    tiny_sems,
    table_sems,
    held_sems,
    local,
):
    total, across = lax.axis_size("seq"), lax.axis_size("wide")
    parts = total // seqs
    me, row = lax.axis_index("seq"), lax.axis_index("wide")
    part, seq = lax.rem(me, parts), lax.div(me, parts)
    other = twist(me, 1, total)
    width = gain_ref.shape[1]
    slim = gw.shape[2]
    own = in_ref.shape[0]
    share = in_ref.shape[2] // total
    cols = three_ref.shape[1] // 3
    half = three_ref.shape[0] // 2

    def seq_at(k):
        return lax.rem(seq + k, seqs) * parts + part

    def row_at(k):
        return lax.rem(row + k, across)

    def part_at(k):
        return me - part + lax.rem(part + k, parts)

    at = pl.ds(pl.multiple_of(lax.div(me, 2) * (2 * share), LANES), 2 * share)
    weights = [
        pltpu.make_async_copy(in_ref.at[:, :, at], in_held, local.at[0]),
        pltpu.make_async_copy(out_ref.at[:, at, :], out_held, local.at[1]),
    ]
    for copy in weights:
        copy.start()

    def load(e):
        return (
            pltpu.make_async_copy(rows_ref.at[:, e], rows_held.at[e], held_sems.at[0, e]),
            pltpu.make_async_copy(cots_ref.at[:, e], cots_held.at[e], held_sems.at[1, e]),
        )

    for e in range(own):
        for copy in load(e):
            copy.start()

    pairs = [(a, b) for a in range(across) for b in range(parts) if a or b]
    peers = [{"seq": lax.rem(me + k, total)} for k in range(1, total)]
    peers += [{"wide": row_at(k)} for k in range(1, across)]
    peers += [{"wide": row_at(a), "seq": part_at(b)} for a, b in pairs if a and b]
    meet(peers)

    late = contract(flip_ref[...], three_ref[...], 1, 0).astype(BF16)
    gw[...] = late.reshape(gw.shape)
    wide_copies = [
        remote(gw.at[:, row_at(k)], wide_got.at[k - 1], wide_sems.at[0, k - 1], wide_sems.at[1, k - 1], {"wide": row_at(k)})
        for k in range(1, across)
    ]

    gain = gain_ref[...]
    gain_grad = jnp.zeros((1, width), F32)
    near_copies = []
    for n in range(2):
        scaled = contract(three_ref[n * half : (n + 1) * half, :], weight_ref[...], 1, 1)
        x = x_ref[n * total // 2 : (n + 1) * total // 2].reshape(half, width).astype(F32)
        inverse = inverse_rms(x)
        gain_grad = gain_grad + jnp.sum(scaled * x * inverse, axis=0, keepdims=True)
        scaled = scaled * gain
        mean_inner = jnp.mean(x * scaled, axis=-1, keepdims=True)
        value = inverse * scaled - x * (inverse * inverse * inverse) * mean_inner
        here = pl.ds(n * total // 2, total // 2)
        grads[here] = value.astype(BF16).reshape(total // 2, *grads.shape[1:])
        near_copies.append(
            remote(
                grads.at[here, lax.rem(part + 1, parts)],
                near.at[here],
                near_sems.at[0, n],
                near_sems.at[1, n],
                {"seq": other},
            )
        )
    first = lax.broadcasted_iota(jnp.int32, tiny_ref.shape, 0) == 0
    tiny[...] = jnp.where(first, gain_grad, tiny_ref[...]).astype(BF16)
    table[...] = table_ref[...].astype(BF16)

    def pass_tiny(stage, wheres):
        copies = []
        for n, where in enumerate(wheres):
            for src, dst, sem in ((tiny, tiny_got, tiny_sems), (table, table_got, table_sems)):
                copies.append(remote(src, dst.at[stage, n], sem.at[0, stage, n], sem.at[1, stage, n], where))
        return copies

    def take_tiny(stage, copies):
        for copy in copies:
            copy.wait()
        for src, dst in ((tiny, tiny_got), (table, table_got)):
            value = src[...].astype(F32)
            for n in range(len(copies) // 2):
                value = value + dst[stage, n].astype(F32)
            src[...] = value.astype(BF16)

    tiny_copies = pass_tiny(0, [{"wide": row_at(k)} for k in range(1, across)])
    for copy in near_copies:
        copy.wait()
    home_copies = []
    for k in range(total - 1, -1, -1):
        to = twist(me, k, total)
        summed[to] = (grads[to, part].astype(F32) + near[to].astype(F32)).astype(BF16)
        if k:
            home_copies.append(
                remote(summed.at[to], home_ref.at[me], home_sems.at[0, k - 1], home_sems.at[1, k - 1], {"seq": to})
            )
    kept = pltpu.make_async_copy(summed.at[me], home_ref.at[me], local.at[2])
    kept.start()
    for copy in weights:
        copy.wait()

    mine_rows = pl.ds(pl.multiple_of(part * share, LANES), share)
    other_rows = pl.ds(pl.multiple_of((1 - part) * share, LANES), share)

    def share_turn(e, n):
        if n == 0:
            for copy in load(e):
                copy.wait()
        some = rows_held.shape[1] // 2
        count = some * rows_held.shape[2]
        here = slice(n * some, (n + 1) * some)
        rows, cots = gated(rows_held[e, here].reshape(count, -1), cots_held[e, here].reshape(count, width))
        hidden, slope = activation(contract(in_held[e].T, rows, 1, 1))
        grad_hidden = contract(out_held[e], cots, 1, 1).astype(BF16).astype(F32)
        part_out = contract(hidden.astype(BF16), cots, 1, 0)
        part_in = contract((grad_hidden * slope).astype(BF16), rows, 1, 0)
        if n == 0:
            sums[0] = part_out
            sums[1] = part_in
            return []
        sums[0] += part_out
        sums[1] += part_in
        grad_out_ref[e] = sums[0, mine_rows, :]
        total_in[e] = sums[1, mine_rows, :]
        copies = []
        for k in range(2):
            leaving[e, k] = sums[k, other_rows, :].astype(BF16)
            copies.append(
                remote(leaving.at[e, k], share_got.at[e, k], share_sems.at[0, e, k], share_sems.at[1, e, k], {"seq": other})
            )
        return copies

    def share_end(e, copies):
        for copy in copies:
            copy.wait()
        grad_out_ref[e] += share_got[e, 0].astype(F32)
        grad_in_ref[e] = (total_in[e] + share_got[e, 1].astype(F32)).T

    share_turn(0, 0)
    first_share = share_turn(0, 1)
    take_tiny(0, tiny_copies)
    for copy in wide_copies:
        copy.wait_recv()
    far_copies = []
    for k in list(range(1, seqs)) + [0]:
        place = lax.rem(seq + k, seqs)
        for p in range(parts):
            block = place * parts + p
            value = gw[block, row].astype(F32)
            for j in range(across - 1):
                value = value + wide_got[j, block].astype(F32)
            wide_sum[place, p] = value.astype(BF16)
        if k:
            where = {"seq": seq_at(k)}
            far_copies.append(
                remote(wide_sum.at[place], far_got.at[k - 1], far_sems.at[0, k - 1], far_sems.at[1, k - 1], where)
            )
            far_copies.append(
                remote(early_ref.at[place], early_got.at[k - 1], early_sems.at[0, k - 1], early_sems.at[1, k - 1], where)
            )
    tiny_copies = pass_tiny(1, [{"seq": seq_at(k)} for k in range(1, seqs)])
    share_turn(1, 0)
    share_end(0, first_share)
    take_tiny(1, tiny_copies)
    for copy in far_copies:
        copy.wait_recv()
    for p in range(parts):
        value = wide_sum[seq, p].astype(F32)
        for j in range(seqs - 1):
            value = value + far_got[j, p].astype(F32)
        mine[p] = value.astype(BF16)
    value = early_ref[seq].astype(F32)
    for j in range(seqs - 1):
        value = value + early_got[j].astype(F32)
    early_mine[...] = value.astype(BF16)
    last = pass_tiny(2, [{"seq": part_at(k)} for k in range(1, parts)])
    count = len(last)
    for a, b in pairs:
        n = a * parts + b - 1
        last.append(
            remote(
                mine.at[lax.rem(part + b, parts)],
                late_all.at[row, part],
                last_sems.at[0, n],
                last_sems.at[1, n],
                {"wide": row_at(a), "seq": part_at(b)},
            )
        )
    for k in range(1, across):
        last.append(
            remote(
                early_mine, early_all.at[row], last_early_sems.at[0, k - 1], last_early_sems.at[1, k - 1], {"wide": row_at(k)}
            )
        )
    stay = [
        pltpu.make_async_copy(mine.at[part], late_all.at[row, part], local.at[3]),
        pltpu.make_async_copy(early_mine, early_all.at[row], local.at[4]),
    ]
    for copy in stay:
        copy.start()
    second_share = share_turn(1, 1)
    take_tiny(2, last[:count])
    share_end(1, second_share)
    for copy in last[count:] + stay + home_copies + [kept]:
        copy.wait()
    for copy in wide_copies + far_copies:
        copy.wait_send()
    for a in range(across):
        here = slice(a * slim, (a + 1) * slim)
        for p in range(parts):
            for n, ref in enumerate((query_out, key_out, value_out)):
                ref[here, p * cols : (p + 1) * cols] = late_all[a, p, :, n * cols : (n + 1) * cols].astype(F32)
        output_out[here, :] = early_all[a].astype(F32)
    piece = tiny_out.shape[1]
    chosen = lax.broadcasted_iota(jnp.int32, (width, piece), 0) == (
        lax.broadcasted_iota(jnp.int32, (width, piece), 1) + me * piece
    )
    tiny_out[...] = contract(tiny[...], chosen.astype(F32).astype(BF16), 1, 0)
    lines = table_out.shape[0]
    chosen = lax.broadcasted_iota(jnp.int32, (lines, table.shape[0]), 1) == (
        lax.broadcasted_iota(jnp.int32, (lines, table.shape[0]), 0) + me * lines
    )
    table_out[...] = contract(chosen.astype(F32).astype(BF16), table[...], 1, 0)


def finish(three, flipped, weights, x, gain, early, tiny, table, rows, cots, w_in, w_out):
    length, columns = three.shape
    total, parts, piece, width = x.shape
    seqs, slim, _ = early.shape
    across = lax.axis_size("wide")
    own, _, units = w_in.shape
    share, part = units // total, width // total
    vmem, hbm = pl.BlockSpec(memory_space=pltpu.VMEM), pl.BlockSpec(memory_space=pl.ANY)
    sems = pltpu.SemaphoreType.DMA
    most = max(across, seqs, parts) - 1
    return pl.pallas_call(
        functools.partial(finish_kernel, seqs),
        in_specs=[vmem] * 8 + [hbm] * 4,
        out_specs=[vmem] * 9,
        out_shape=[
            jax.ShapeDtypeStruct((total, piece, width), BF16),
            *[jax.ShapeDtypeStruct((part, width), F32)] * 4,
            jax.ShapeDtypeStruct((tiny.shape[0], part), F32),
            jax.ShapeDtypeStruct((table.shape[0] // total, LANES), F32),
            jax.ShapeDtypeStruct((own, width, share), F32),
            jax.ShapeDtypeStruct((own, share, width), F32),
        ],
        scratch_shapes=[
            pltpu.VMEM((total, parts, piece, width), BF16),
            pltpu.VMEM((total, piece, width), BF16),
            pltpu.VMEM((total, piece, width), BF16),
            pltpu.VMEM((total, across, slim, columns), BF16),
            pltpu.VMEM((across - 1, total, slim, columns), BF16),
            pltpu.VMEM((seqs, parts, slim, columns), BF16),
            pltpu.VMEM((seqs - 1, parts, slim, columns), BF16),
            pltpu.VMEM((seqs - 1, slim, width), BF16),
            pltpu.VMEM((parts, slim, columns), BF16),
            pltpu.VMEM((slim, width), BF16),
            pltpu.VMEM((across, parts, slim, columns), BF16),
            pltpu.VMEM((across, slim, width), BF16),
            pltpu.VMEM(tiny.shape, BF16),
            pltpu.VMEM((3, most, *tiny.shape), BF16),
            pltpu.VMEM(table.shape, BF16),
            pltpu.VMEM((3, most, *table.shape), BF16),
            pltpu.VMEM((own, seqs, *rows.shape[2:]), BF16),
            pltpu.VMEM((own, seqs, *cots.shape[2:]), BF16),
            pltpu.VMEM((own, width, 2 * share), BF16),
            pltpu.VMEM((own, 2 * share, width), BF16),
            pltpu.VMEM((2, 2 * share, width), F32),
            pltpu.VMEM((own, share, width), F32),
            pltpu.VMEM((own, 2, share, width), BF16),
            pltpu.VMEM((own, 2, share, width), BF16),
            sems((2, own, 2)),
            sems((2, 2)),
            sems((2, total - 1)),
            sems((2, across - 1)),
            sems((2, seqs - 1)),
            sems((2, seqs - 1)),
            sems((2, across * parts - 1)),
            sems((2, across - 1)),
            sems((2, 3, most)),
            sems((2, 3, most)),
            sems((2, own)),
            sems((5,)),
        ],
        compiler_params=pltpu.CompilerParams(collective_id=1, has_side_effects=True, vmem_limit_bytes=62 << 20),
        cost_estimate=pl.CostEstimate(flops=16 << 30, bytes_accessed=60 << 20, transcendentals=0),
        name="finish",
    )(three, flipped, weights, x, gain, early, tiny, table, rows, cots, w_in, w_out)


def ring_pairs(total, parts, shift):
    return [(i, i - i % parts + (i % parts + shift) % parts) for i in range(total)]


def pick(pieces, index):
    out = pieces[0]
    for k in range(1, len(pieces)):
        out = jnp.where(index == k, pieces[k], out)
    return out


def swap_parts(pieces, part, parts, total):
    near = [pick(pieces, part)]
    for k in range(1, parts):
        near.append(lax.ppermute(pick(pieces, (part + k) % parts), "seq", ring_pairs(total, parts, k)))
    return [pick(near, (part - j) % parts) for j in range(parts)]


def per_device(
    inputs,
    routes,
    bucket_ids,
    gain_attn,
    w_query,
    w_key,
    w_value,
    w_output,
    rel_table,
    gain_ffn,
    w_router,
    w_in,
    w_out,
    cotangent,
):
    seqs, local_len, width = inputs.shape
    buckets, head_count = rel_table.shape
    size = width // head_count
    total = lax.axis_size("seq")
    across = lax.axis_size("wide")
    length = local_len * total
    parts = total // seqs
    heads = head_count // parts
    cols = heads * size
    me = lax.axis_index("seq")
    part = me % parts
    experts = w_router.shape[1]
    own_experts = w_in.shape[0]
    tokens = seqs * local_len
    capacity = (5 * tokens + 4 * experts - 1) // (4 * experts)
    slots = experts * capacity
    gain_one = gain_attn.astype(F32)
    gain_two = gain_ffn.astype(F32)

    fast = parts == 2 and capacity % 16 == 0 and own_experts == 2 and seqs % 2 == 0 and cols % LANES == 0 and local_len == LANES
    flat_cot = cotangent.reshape(tokens, width)
    chosen = routes.reshape(tokens)
    blocks = inputs.reshape(total, local_len // parts, width)
    own_weights = jnp.concatenate(
        [lax.dynamic_slice(w, (0, part * cols), (width, cols)) for w in (w_query, w_key, w_value)], axis=1
    )

    if fast:
        first_slot = [(e % own_experts) * (across * capacity) + (e // own_experts) * capacity for e in range(experts)]
        base = jnp.array(first_slot + [0] * (LANES - experts), F32)[None]
        seq_in, qkv, flipped, slot_hot, cot_rows = begin(
            blocks,
            w_query,
            w_key,
            w_value,
            gain_one[None],
            chosen[:, None],
            base,
            flat_cot,
            heads,
            size,
            own_experts,
            capacity,
        )
    else:
        seq_in = spread(blocks, parts).reshape(length, width).astype(F32)
        inv_one = inverse_rms(seq_in)
        normed_one = (seq_in * inv_one * gain_one).astype(BF16)
        flipped = normed_one.T
        qkv = contract(own_weights, normed_one, 0, 1).astype(BF16).reshape(3, heads, size, length)
        picked = (chosen[:, None] == jnp.arange(experts, dtype=jnp.int32)[None, :]).astype(F32)
        order = jnp.arange(tokens, dtype=jnp.int32)
        before = (order[None, :] < order[:, None]).astype(BF16)
        earlier = jnp.dot(before, picked.astype(BF16), preferred_element_type=F32)
        rank_in = jnp.sum(earlier * picked, axis=1).astype(jnp.int32)
        place = (chosen % own_experts) * (across * capacity) + (chosen // own_experts) * capacity + rank_in
        slot_of = jnp.where(rank_in < capacity, place, slots)
        slot_hot = (slot_of[:, None] == jnp.arange(slots, dtype=jnp.int32)[None, :]).astype(BF16)
        packed = contract(slot_hot, flat_cot, 0, 0).astype(BF16).reshape(own_experts, across, capacity, width)
        cot_rows = jnp.stack([lax.all_to_all(packed[e], "wide", 0, 0, tiled=True) for e in range(own_experts)])
        cot_rows = cot_rows.reshape(own_experts, across * capacity, width)
    rings = [[n * parts + p for n in range(seqs)] for p in range(parts)] if fast else None
    all_cots = lax.all_gather(cot_rows, "seq", axis=0, axis_index_groups=rings)
    own_table = lax.dynamic_slice(rel_table, (0, part * heads), (buckets, heads))
    ids = jnp.concatenate([bucket_ids, jnp.full((1,), buckets, jnp.int32)])
    bucket_hot = (ids[None, :] == jnp.arange(buckets, dtype=jnp.int32)[:, None]).astype(BF16)
    reverse_hot = (ids[::-1][None, :] == jnp.arange(buckets, dtype=jnp.int32)[:, None]).astype(BF16)
    bias_line = contract(own_table, reverse_hot, 0, 0).reshape(heads, 1, 2 * length)
    outs, attended, exps, inverse = attend(qkv, bias_line, total)
    attended = attended.reshape(seqs, width, local_len)

    flat_in = inputs.reshape(tokens, width).astype(F32)
    middle = flat_in + jnp.einsum("sft,fe->ste", attended, w_output, preferred_element_type=F32).reshape(tokens, width)
    inv_two = inverse_rms(middle)
    normed_two = (middle * inv_two * gain_two).astype(BF16)
    router_probs = jax.nn.softmax(jnp.dot(normed_two, w_router, preferred_element_type=F32), axis=-1)
    picked = (chosen[:, None] == jnp.arange(experts, dtype=jnp.int32)[None, :]).astype(F32)
    gate_prob = jnp.sum(router_probs * picked, axis=1)
    upstream = flat_cot.astype(F32)
    gate_high = gate_prob.astype(BF16)
    gate_low = (gate_prob - gate_high.astype(F32)).astype(BF16)
    pad = jnp.zeros((tokens, LANES - 2), BF16)
    both = jnp.concatenate([normed_two, gate_high[:, None], gate_low[:, None], pad], axis=1)
    packed = contract(slot_hot, both, 0, 0).astype(BF16)
    if fast:
        received = exchange(packed.reshape(own_experts, across * capacity, width + LANES), "wide")
        returned = run_experts(received, cot_rows, w_in, w_out, 512).reshape(slots, 2 * width)
    else:
        packed = packed.reshape(own_experts, across, capacity, width + LANES)
        received, returned = [], []
        for e in range(own_experts):
            got = lax.all_to_all(packed[e], "wide", 0, 0, tiled=True).reshape(across * capacity, width + LANES)
            received.append(got)
            pair = run_expert(got, cot_rows[e], w_in, w_out, e, 512).reshape(across, capacity, 2 * width)
            returned.append(lax.all_to_all(pair, "wide", 0, 0, tiled=True).reshape(across * capacity, 2 * width))
        received, returned = jnp.stack(received), jnp.concatenate(returned, axis=0)
    all_rows = lax.all_gather(received, "seq", axis=0, axis_index_groups=rings)
    token_rows = jnp.dot(slot_hot, returned, preferred_element_type=F32)
    selected, grad_token = token_rows[:, :width], token_rows[:, width:]
    output = (middle + gate_prob[:, None] * selected).astype(BF16).reshape(inputs.shape)
    grad_gate = jnp.sum(upstream * selected, axis=1)
    grad_logits = (grad_gate[:, None] * router_probs * (picked - gate_prob[:, None])).astype(BF16)
    grad_router = contract(grad_logits, normed_two, 0, 0)
    grad_normed_two = grad_token + contract(grad_logits, w_router, 1, 1)
    grad_mid_norm, grad_gain_two = norm_backward(middle, inv_two, gain_two, grad_normed_two)
    grad_middle = upstream + grad_mid_norm
    grad_branch = grad_middle.astype(BF16).reshape(seqs, local_len, width)
    grad_w_output = jnp.einsum("sft,ste->fe", attended, grad_branch, preferred_element_type=F32)
    share = width // total
    slim = share // across
    back = (exps, inverse, grad_branch, w_output.reshape(parts, cols, width), outs, qkv, bucket_hot)
    if fast:
        early = grad_w_output.astype(BF16).reshape(seqs, parts, across, slim, width)
        three, table, early = attend_back(*back, early)
        tiny = jnp.concatenate(
            [jnp.zeros((1, width), F32), grad_gain_two[None], grad_router, jnp.zeros((14 - experts, width), F32)], axis=0
        )
        home, total_query, total_key, total_value, total_output, tiny, table, grad_w_in, grad_w_out = finish(
            three,
            flipped,
            own_weights,
            seq_in,
            gain_one[None],
            early,
            tiny,
            table,
            all_rows,
            all_cots,
            w_in,
            w_out,
        )
        return (
            output,
            (grad_middle + home.reshape(tokens, width).astype(F32)).reshape(inputs.shape),
            tiny[0],
            total_query,
            total_key,
            total_value,
            total_output,
            table[:, :head_count],
            tiny[1],
            tiny[2 : 2 + experts].T,
            grad_w_in,
            grad_w_out,
        )

    three, table = attend_back(*back, None)
    grad_normed_one = contract(three, own_weights, 1, 1)
    grad_in_norm, grad_gain_one = norm_backward(seq_in, inv_one, gain_one, grad_normed_one)
    pieces = grad_in_norm.astype(BF16).reshape(total, parts, local_len // parts, width)
    swapped = swap_parts([pieces[:, p] for p in range(parts)], part, parts, total)
    home = sum(p.astype(F32) for p in swapped).astype(BF16)
    home = lax.all_to_all(home, "seq", 0, 0, tiled=True).reshape(tokens, width).astype(F32)
    grad_projections = lax.dynamic_update_slice(
        jnp.zeros((width, 3, width), F32), contract(flipped, three, 1, 0).reshape(width, 3, cols), (0, 0, part * cols)
    )
    rows = [grad_projections[:, k] for k in range(3)]
    rows += [grad_w_output, grad_gain_one[:, None], grad_gain_two[:, None], grad_router.T]
    rows, table = lax.psum((jnp.concatenate(rows, axis=1).astype(BF16), table.astype(BF16)), "wide")
    rows = lax.psum_scatter(rows, "seq", scatter_dimension=0, tiled=True).astype(F32)
    table = lax.psum_scatter(table, "seq", scatter_dimension=0, tiled=True).astype(F32)
    held = []
    for e in range(own_experts):
        held = run_share(
            me,
            all_rows.reshape(total * own_experts, *received.shape[1:]),
            all_cots.reshape(total * own_experts, *cot_rows.shape[1:]),
            w_in,
            w_out,
            e,
            held,
        )
    last = rows[:, 4 * width :]
    return (
        output,
        (grad_middle + home).reshape(inputs.shape),
        last[:, 0],
        *[rows[:, k * width : (k + 1) * width] for k in range(4)],
        table[:, :head_count],
        last[:, 1],
        last[:, 2 : 2 + experts],
        *held,
    )


def solution(mesh):
    in_specs = (
        P("wide", "seq", None),
        P("wide", "seq", None),
        P(),
        P(),
        P(),
        P(),
        P(),
        P(),
        P(),
        P(),
        P(),
        P("wide", None, None),
        P("wide", None, None),
        P("wide", "seq", None),
    )
    out_specs = (
        P("wide", "seq", None),
        P("wide", "seq", None),
        P("seq"),
        P("seq", None),
        P("seq", None),
        P("seq", None),
        P("seq", None),
        P("seq", None),
        P("seq"),
        P("seq", None),
        P("wide", None, "seq"),
        P("wide", "seq", None),
    )
    return jax.shard_map(
        per_device, mesh=mesh, in_specs=in_specs, out_specs=out_specs, check_vma=False
    )
```

time: 487 us -> 326 us (0.67)
  Pallas kernels: 56.1 us -> 247 us
  matrix products: 114 us -> 12.9 us
  waiting for transfers between devices: 109 us -> 16.5 us
  blocking collectives: 55.9 us -> 0 us
  local copies, waits for them, and re-layouts: 61.6 us -> 21.2 us
  starting transfers between devices: 34 us -> 0.25 us
  other arithmetic: 32.2 us -> 8.62 us
    pallas_call x2 -> x6, Pallas kernels: 56.1 us -> 247 us  [the longest x1 60 us: attend_back(): pl.pallas_call(functools.partial(attend_back_kernel, early is not None),...]
    all_to_all x8 -> x0, waiting for transfers between devices: 106 us -> none  [the longest x1 37.1 us: per_device(): lax.all_to_all(grad_att.reshape(total, cols, local_len), 'seq', 0, 0, til...]
    dot_general x13 -> x4, matrix products: 66.3 us -> 5.17 us  [contract(): lax.dot_general(a, b, (((da,), (db,)), ((), ())), preferred_element_type=...]
    all_to_all x2 -> x0, blocking collectives: 44.5 us -> none  [the longest x1 27.4 us: per_device(): lax.all_to_all(inputs.reshape(total, local_len // parts, width), 'seq', 0...]
    dot_general x11 -> x2, matrix products: 44.9 us -> 5.12 us  [the longest x1 3.33 us: per_device(): token_rows = jnp.dot(slot_hot, returned, preferred_element_type=F32)]
    all_to_all x8 -> x0, starting transfers between devices: 33.3 us -> none  [the longest x2 8.99 us: per_device(): lax.all_to_all(pair, 'wide', 0, 0, tiled=True)]
    slice x6 -> x0, local copies, waits for them, and re-layouts: 18.4 us -> none  [the longest x1 8.26 us: per_device(): w_out[e]]
    all_gather x2, waiting for transfers between devices: 0.02 us -> 16.5 us  [the longest x1 16.5 us: per_device(): all_rows = lax.all_gather(received, 'seq', axis=0, axis_index_groups=rings)]
  transfers between devices with their start and end apart: 14 -> 2, of which waited for: 7 -> 1; matrix products, arithmetic and copies ran while one was open for 32% -> 8% of each run, Pallas kernels for 6% -> 48%
where the time goes in v3:
time: 326 us; the launch traced here: 321 us
  Pallas kernels  247 us (76%)
  local copies, waits for them, and re-layouts  21.2 us (7%)
  waiting for transfers between devices  16.5 us (5%)
  between operations  14.5 us (4%)
  matrix products  12.9 us (4%)
  other arithmetic  8.62 us (3%)
    pallas_call x1, Pallas kernels, attend_back(): pl.pallas_call(functools.partial(attend_back_kernel, early is not None),...  60 us
    pallas_call x1, Pallas kernels, finish(): pl.pallas_call(functools.partial(finish_kernel, seqs), in_specs=[vmem] *...  59.9 us
    pallas_call x1, Pallas kernels, attend(): pl.pallas_call(attend_kernel, in_specs=[vmem, vmem], out_specs=[vmem, vme...  45.2 us
    pallas_call x1, Pallas kernels, run_experts(): pl.pallas_call(functools.partial(experts_kernel, block), in_specs=[vmem,...  35.3 us
    pallas_call x1, Pallas kernels, begin(): pl.pallas_call(functools.partial(begin_kernel, capacity), in_specs=[vmem]...  34.5 us
    all_gather x1, waiting for transfers between devices, per_device(): all_rows = lax.all_gather(received, 'seq', axis=0, axis_index_groups=rings)  16.5 us
    pallas_call x1, Pallas kernels, exchange(): pl.pallas_call(functools.partial(exchange_kernel, axis), in_specs=[vmem],...  12 us
    unnamed x55, local copies, waits for them, and re-layouts  7.55 us
  transfers between devices with their start and end apart: 2, of which 1 were waited for; matrix products, arithmetic and copies ran while one was open for 8% of the time, Pallas kernels for 48%

profile of v3, /device:TPU:0, one launch (start us, length us, event | category | flops | bytes accessed | tf_op | source)
XLA Modules:
  0.0 320.9 jit_solution(15593969948561699466)
XLA Ops:
  8.5 1.5 copy.35.routes_ref
  10.0 34.5 %begin.1 = (bf16[8,2,64,768]{3,2,1,0:T(8,128)(2,1)}, bf16[3,6,64,1024]{3,2,1,0:T(8,128)(2,1)}, bf16[768,1024]{1,0:T(8,128)(2,1)}, bf16[512,640]{1,0:T(8,128)(2,1)}, bf16[2,320,768]{2,1,0:T(8,128)(2,1)}) custom-call(bf16[8,64,768]{2,1,0:T(8,128)(2,1)} %bitcast.68, bf16[768,768]{1,0:T(8,128)(2,1)} %query_ref.1, bf16[768,768]{1,0:T(8,128)(2,1)} %key_ref.1, ...), custom_call_target="tpu_custom_call" | custom-call | flops 4294967296 | bytes 83886080 | tf_op jit(solution)/shard_map/begin/pallas_call | solution.py:891
  45.8 45.2 %attend.1 = (bf16[8,6,64,128]{3,2,1,0:T(8,128)(2,1)}, bf16[8,6,64,128]{3,2,1,0:T(8,128)(2,1)}, bf16[4,6,1024,256]{3,2,1,0:T(8,128)(2,1)}, f32[4,6,1,256]{3,2,1,0:T(1,128)}) custom-call(bf16[3,6,64,1024]{3,2,1,0:T(8,128)(2,1)} %get-tuple-element.33.qkv_ref.refs_5_, f32[6,1,2048]{2,1,0:T(1,128)} %reshape.113.bias_ref), custom_call_target="tpu_custom_call" | custom-call | flops 1610612736 | bytes 12582912 | tf_op jit(solution)/shard_map/attend/pallas_call | solution.py:160
  91.0 2.4 copy.36
  93.4 2.3 multiply_reduce_fusion.2
  97.0 3.0 convolution_convert_fusion
  100.0 12.0 %exchange.1.rows_ref = bf16[2,320,896]{2,1,0:T(8,128)(2,1)} custom-call(bf16[2,320,896]{2,1,0:T(8,128)(2,1)} %bitcast.53), custom_call_target="tpu_custom_call" | custom-call | tf_op jit(solution)/shard_map/exchange/pallas_call | solution.py:523
  112.1 35.3 %experts.1 = bf16[2,320,1536]{2,1,0:T(8,128)(2,1)} custom-call(bf16[2,320,896]{2,1,0:T(8,128)(2,1)} %exchange.1.rows_ref, bf16[2,320,768]{2,1,0:T(8,128)(2,1)} %get-tuple-element.36.cot_ref, bf16[2,768,3072]{2,1,0:T(8,128)(2,1)} %in_ref.3, bf16[2,3072,768]{2,1,0:T(8,128)(2,1)} %out_ref.3), custom_call_target="tpu_custom_call" | custom-call | flops 12079595520 | bytes 18874368 | tf_op jit(solution)/shard_map/experts/pallas_call | solution.py:625
  147.4 3.3 %fusion.19 = f32[512,1536]{1,0:T(8,128)S(1)} fusion(bf16[512,640]{1,0:T(8,128)(2,1)} %get-tuple-element.35, bf16[640,1536]{1,0:T(8,128)(2,1)} %bitcast.70), kind=kOutput, calls=%fused_computation.51 | convolution fusion | flops 1006632960 | bytes 5767168 | tf_op jit(solution)/shard_map/dot_general | solution.py:1410
  150.7 1.3 fusion
  152.0 1.8 multiply_reduce_fusion
  153.9 2.0 constant_dynamic-slice_fusion.2
  156.0 2.5 constant_dynamic-slice_fusion
  159.4 1.6 fusion.16
  161.1 1.8 bitcast_convert_fusion
  163.5 60.0 %attend_back.1 = (bf16[1024,1152]{1,0:T(8,128)(2,1)}, f32[32,128]{1,0:T(8,128)}, bf16[4,24,768]{2,1,0:T(8,128)(2,1)}) custom-call(bf16[4,6,1024,256]{3,2,1,0:T(8,128)(2,1)} %get-tuple-element.37.refs_0_, f32[4,6,1,256]{3,2,1,0:T(1,128)} %get-tuple-element.38.refs_1_, bf16[4,128,768]{2,1,0:T(8,128)(2,1)} %bitcast.48, bf16[2,384,768]{2,1,0:T(8,128)(2,1)} %bitcast.51, ...), custom_call_target="tpu_custom_call" | custom-call | flops 3221225472 | bytes 12582912 | tf_op jit(solution)/shard_map/attend_back/pallas_call | solution.py:408
  223.6 1.4 pad_maximum_fusion.weight_ref
  225.0 16.5 %all-gather.5.cloned.1.call-done = bf16[8,320,896]{2,1,0:T(8,128)(2,1)} async-done(((bf16[2,320,896]{2,1,0:T(8,128)(2,1)}), bf16[8,320,896]{2,1,0:T(8,128)(2,1)}) %all-gather.5.cloned.1.call-update) | async-done | bytes 4587536 | tf_op jit(solution)/shard_map/all_gather | solution.py:1409
  241.5 59.9 %finish.1 = (bf16[8,64,768]{2,1,0:T(8,128)(2,1)}, f32[96,768]{1,0:T(8,128)}, f32[96,768]{1,0:T(8,128)}, f32[96,768]{1,0:T(8,128)}, f32[96,768]{1,0:T(8,128)}, /*...) custom-call(bf16[1024,1152]{1,0:T(8,128)(2,1)} %get-tuple-element.40.three_ref, ...), custom_call_target="tpu_custom_call" | custom-call | flops 17179869184 | bytes 62914560 | tf_op jit(solution)/shard_map/finish/pallas_call | solution.py:1223
  301.3 1.3 slice_bitcast_fusion
  302.6 1.3 slice_bitcast_fusion.1
  303.9 2.6 convert_add_fusion.1
  310.0 1.4 copy.52
  312.5 1.4 copy.53
  (85 shorter events, 10.1 us)
Async XLA Ops:
  7.2 88.7 %copy-start = (bf16[768,8]{0,1:T(8,128)(2,1)S(1)}, bf16[768,8]{0,1:T(8,128)(2,1)}, u32[]{:S(2)}) copy-start(bf16[768,8]{0,1:T(8,128)(2,1)} %param.25) | copy-start | bytes 36868
  7.2 217.8 %all-gather.7.cloned.1.call-start = ((), (), s32[]{:S(2)}) async-start(), calls=%async_computation.1 | async-start | bytes 4915200 | tf_op jit(solution)/shard_map/all_gather | solution.py:1375
  10.0 34.7 %copy-start.20 = (s32[2047]{0:T(1024)S(1)}, s32[2047]{0:T(1024)}, u32[]{:S(2)}) copy-start(s32[2047]{0:T(1024)} %param.17) | copy-start | bytes 24568
  10.0 34.9 %copy-start.23 = (bf16[32,12]{0,1:T(8,128)(2,1)S(1)}, bf16[32,12]{0,1:T(8,128)(2,1)}, u32[]{:S(2)}) copy-start(bf16[32,12]{0,1:T(8,128)(2,1)} %param.23) | copy-start | bytes 2308
  44.5 196.9 %all-gather.5.cloned.1.call-start = ((), (), s32[]{:S(2)}) async-start(), calls=%async_computation | async-start | bytes 5734400 | tf_op jit(solution)/shard_map/all_gather | solution.py:1409
  91.0 2.4 copy-start.21
  91.0 2.4 copy-start.13
  95.9 4.1 %copy-start.2 = (bf16[512,768]{1,0:T(8,128)(2,1)}, bf16[512,768]{1,0:T(8,128)(2,1)S(1)}, u32[]{:S(2)}) copy-start(bf16[512,768]{1,0:T(8,128)(2,1)S(1)} %multiply_convert_fusion) | copy-start | bytes 2359300
  147.4 3.4 %copy-start.7 = (bf16[4,128,768]{2,1,0:T(8,128)(2,1)S(1)}, bf16[4,128,768]{2,1,0:T(8,128)(2,1)}, u32[]{:S(2)}) copy-start(bf16[4,128,768]{2,1,0:T(8,128)(2,1)} %param.28) | copy-start | bytes 2359300
  153.9 4.6 %copy-start.3 = (bf16[512,768]{1,0:T(8,128)(2,1)S(1)}, bf16[512,768]{1,0:T(8,128)(2,1)}, u32[]{:S(2)}) copy-start(bf16[512,768]{1,0:T(8,128)(2,1)} %copy-done.2) | copy-start | bytes 2359300
  156.0 3.5 %copy-start.5 = (f32[512,768]{1,0:T(8,128)S(1)}, f32[512,768]{1,0:T(8,128)}, u32[]{:S(2)}) copy-start(f32[512,768]{1,0:T(8,128)} %get-tuple-element.68) | copy-start | bytes 4718596
  161.1 1.8 copy-start.6
  163.5 60.0 %copy-start.8 = (bf16[768,384]{1,0:T(8,128)(2,1)S(1)}, bf16[768,384]{1,0:T(8,128)(2,1)}, u32[]{:S(2)}) copy-start(bf16[768,384]{1,0:T(8,128)(2,1)} %get-tuple-element.69) | copy-start | bytes 1769476
  163.5 60.0 %copy-start.9 = (bf16[768,384]{1,0:T(8,128)(2,1)S(1)}, bf16[768,384]{1,0:T(8,128)(2,1)}, u32[]{:S(2)}) copy-start(bf16[768,384]{1,0:T(8,128)(2,1)} %get-tuple-element.70) | copy-start | bytes 1769476
  163.5 60.1 %copy-start.10 = (bf16[768,384]{1,0:T(8,128)(2,1)S(1)}, bf16[768,384]{1,0:T(8,128)(2,1)}, u32[]{:S(2)}) copy-start(bf16[768,384]{1,0:T(8,128)(2,1)} %constant_dynamic-slice_fusion.2) | copy-start | bytes 1769476
  241.5 62.4 %copy-start.4 = (f32[512,768]{1,0:T(8,128)S(1)}, f32[512,768]{1,0:T(8,128)}, u32[]{:S(2)}) copy-start(f32[512,768]{1,0:T(8,128)} %get-tuple-element.57) | copy-start | bytes 4718596
  303.9 2.6 copy-start.18
  303.9 3.3 %copy-start.17 = (f32[96,768]{1,0:T(8,128)S(1)}, f32[96,768]{1,0:T(8,128)}, u32[]{:S(2)}) copy-start(f32[96,768]{1,0:T(8,128)} %get-tuple-element.87) | copy-start | bytes 884740
  303.9 4.0 %copy-start.16 = (f32[96,768]{1,0:T(8,128)S(1)}, f32[96,768]{1,0:T(8,128)}, u32[]{:S(2)}) copy-start(f32[96,768]{1,0:T(8,128)} %get-tuple-element.88) | copy-start | bytes 884740
  303.9 4.7 %copy-start.15 = (f32[96,768]{1,0:T(8,128)S(1)}, f32[96,768]{1,0:T(8,128)}, u32[]{:S(2)}) copy-start(f32[96,768]{1,0:T(8,128)} %get-tuple-element.89) | copy-start | bytes 884740
  306.5 2.9 copy-start.22
  306.5 3.5 %copy-start.12 = (f32[2,768,384]{2,1,0:T(8,128)S(1)}, f32[2,768,384]{2,1,0:T(8,128)}, u32[]{:S(2)}) copy-start(f32[2,768,384]{2,1,0:T(8,128)} %get-tuple-element.93) | copy-start | bytes 7077892
  310.0 2.5 copy-start.11
  310.0 3.9 %copy-start.1 = (bf16[768,8]{0,1:T(8,128)(2,1)S(1)}, bf16[768,8]{0,1:T(8,128)(2,1)}, u32[]{:S(2)}) copy-start(bf16[768,8]{0,1:T(8,128)(2,1)} %param.25) | copy-start | bytes 36868
  (2 other events, 2.3 us)
Sparse Core Ops, SparseCore 0:
  44.7 92.7 all-gather.6
  139.1 102.3 all-gather.4

commit v4 on v3

--- a/solution.py
+++ b/solution.py
@@ -188,9 +188,9 @@
 def attend_back_kernel(early, *refs):
     refs = list(refs)
     exp_ref, inv_ref, branch_ref, weight_ref, out_ref, qkv_ref, hot_ref = refs[:7]
-    early_ref = refs.pop(7) if early else None
+    early_ref, *line_refs = [refs.pop(7) for _ in range(3)] if early else [None]
     three_ref, table_ref = refs[7:9]
-    early_out = refs.pop(9) if early else None
+    early_out, *line_outs = [refs.pop(9) for _ in range(3)] if early else [None]
     leaving, got, strip, values, dq_all, dk_sum, dv_sum, scores, held, diagonal, send, recv, exp_sems = refs[9:22]
     _, heads, size, length = qkv_ref.shape
     total = lax.axis_size("seq")
@@ -219,7 +219,7 @@
         peers += [{"wide": lax.rem(row + k, across)} for k in range(1, across)]
     meet(peers)
     if early:
-        near, near_sum, wide_got, near_sems, wide_sems = refs[22:]
+        near, near_sum, wide_got, near_sems, wide_sems, line_sems = refs[22:]
         seqs = early_ref.shape[0]
 
         def near_copy():
@@ -258,6 +258,11 @@
         return carry
 
     lax.fori_loop(1, total, leave, 0)
+    line_ends = []
+    if early:
+        for e in range(line_refs[0].shape[0]):
+            up, down = ((1, seqs - 2, line_refs[n].at[e], line_outs[n].at[e]) for n in range(2))
+            line_ends.append(pass_on(parts, up, down, line_sems.at[e]))
     got[me] = product(me)
 
     def prepare(h, carry):
@@ -367,48 +372,53 @@
     lax.fori_loop(0, heads, close, 0)
     sums = jnp.concatenate([diagonal[h] for h in range(heads)], axis=0)
     table = lax.dot_general(
+        sums,
         hot_ref[...].astype(F32),
-        sums,
         (((1,), (1,)), ((), ())),
         precision=lax.Precision.HIGHEST,
         preferred_element_type=F32,
     )
-    column = lax.broadcasted_iota(jnp.int32, (heads, LANES), 1)
-    first = lax.broadcasted_iota(jnp.int32, (heads, LANES), 0) + part * heads
+    line = lax.broadcasted_iota(jnp.int32, (table_ref.shape[0], heads), 0)
+    head_line = lax.broadcasted_iota(jnp.int32, (table_ref.shape[0], heads), 1) + part * heads
     table_ref[...] = lax.dot_general(
+        (line == head_line).astype(F32),
         table,
-        (column == first).astype(F32),
         (((1,), (0,)), ((), ())),
         precision=lax.Precision.HIGHEST,
         preferred_element_type=F32,
     )
-
-
-def attend_back(exps, inverse, branch, weight, outs, qkv, hot, early):
+    for end in line_ends:
+        end()
+
+
+def attend_back(exps, inverse, branch, weight, outs, qkv, hot, early, line):
     _, heads, size, length = qkv.shape
     total, tokens = outs.shape[0], outs.shape[3]
     vmem = pl.BlockSpec(memory_space=pltpu.VMEM)
     sems = pltpu.SemaphoreType.DMA
     out_shape = [
         jax.ShapeDtypeStruct((length, 3 * heads * size), BF16),
-        jax.ShapeDtypeStruct((hot.shape[0], LANES), F32),
+        jax.ShapeDtypeStruct((16, hot.shape[0]), F32),
     ]
     more, given = [], []
     if early is not None:
         seqs, _, across, slim, columns = early.shape
-        given = [early]
+        given = [early, *line]
         out_shape.append(jax.ShapeDtypeStruct((seqs, slim, columns), BF16))
+        out_shape += [jax.ShapeDtypeStruct(rows.shape, BF16) for rows in line]
         more = [
             pltpu.VMEM((seqs, across, slim, columns), BF16),
             pltpu.VMEM((across, seqs, slim, columns), BF16),
             pltpu.VMEM((across - 1, seqs, slim, columns), BF16),
             sems((2,)),
             sems((2, across - 1)),
+            sems((line[0].shape[0], 2, 2)),
         ]
+    hbm = pl.BlockSpec(memory_space=pl.ANY)
     return pl.pallas_call(
         functools.partial(attend_back_kernel, early is not None),
-        in_specs=[pl.BlockSpec(memory_space=pl.ANY)] + [vmem] * (6 + len(given)),
-        out_specs=[vmem] * len(out_shape),
+        in_specs=[hbm] + [vmem] * (6 + len(given[:1])) + [hbm] * len(line),
+        out_specs=[vmem] * (len(out_shape) - len(line)) + [hbm] * len(line),
         out_shape=out_shape,
         scratch_shapes=[
             pltpu.VMEM((total, heads, size, tokens), BF16),
@@ -442,13 +452,15 @@
     return v * half, slope
 
 
-def gated(rows, cots):
-    width = cots.shape[1]
-    gate = rows[:, width : width + 1].astype(F32) + rows[:, width + 1 : width + 2].astype(F32)
-    return rows[:, :width], (gate * cots.astype(F32)).astype(BF16)
-
-
-def expert_kernel(rows_ref, cot_ref, in_ref, out_ref, both_ref, forward, backward):
+def gated(rows, cots, router, expert):
+    logits = contract(rows, router, 1, 0)
+    grown = jnp.exp(logits - jnp.max(logits, axis=1, keepdims=True))
+    named = lax.broadcasted_iota(jnp.int32, grown.shape, 1) == expert
+    gate = jnp.sum(jnp.where(named, grown, 0.0), axis=1, keepdims=True) / jnp.sum(grown, axis=1, keepdims=True)
+    return (gate * cots.astype(F32)).astype(BF16)
+
+
+def expert_kernel(expert, rows_ref, cot_ref, router_ref, in_ref, out_ref, both_ref, forward, backward):
     step = pl.program_id(0)
     width = cot_ref.shape[1]
 
@@ -457,7 +469,9 @@
         forward[...] = jnp.zeros_like(forward)
         backward[...] = jnp.zeros_like(backward)
 
-    rows, grads = gated(rows_ref[...], cot_ref[...])
+    rows = rows_ref[...]
+    own = router_ref.shape[1] // lax.axis_size("wide")
+    grads = gated(rows, cot_ref[...], router_ref[...], lax.axis_index("wide") * own + expert)
     hidden, slope = activation(contract(rows, in_ref[0], 1, 0))
     grad_hidden = contract(grads, out_ref[0], 1, 1).astype(BF16).astype(F32)
     forward[...] += contract(hidden.astype(BF16), out_ref[0], 1, 0)
@@ -469,15 +483,16 @@
         both_ref[:, width:] = backward[...].astype(BF16)
 
 
-def run_expert(rows, cots, w_in, w_out, expert, block):
+def run_expert(rows, cots, router, w_in, w_out, expert, block):
     count, width = cots.shape
     units = w_in.shape[2]
     return pl.pallas_call(
-        expert_kernel,
+        functools.partial(expert_kernel, expert),
         grid=(units // block,),
         in_specs=[
             pl.BlockSpec(rows.shape, lambda f: (0, 0)),
             pl.BlockSpec(cots.shape, lambda f: (0, 0)),
+            pl.BlockSpec(router.shape, lambda f: (0, 0)),
             pl.BlockSpec((1, width, block), lambda f: (expert, 0, f)),
             pl.BlockSpec((1, block, width), lambda f: (expert, f, 0)),
         ],
@@ -486,27 +501,69 @@
         scratch_shapes=[pltpu.VMEM((count, width), F32), pltpu.VMEM((count, width), F32)],
         compiler_params=pltpu.CompilerParams(vmem_limit_bytes=40 << 20),
         name="expert",
-    )(rows, cots, w_in, w_out)
-
-
-def exchange_kernel(axis, in_ref, out_ref, send, recv, local):
-    total = lax.axis_size(axis)
-    me = lax.axis_index(axis)
+    )(rows, cots, router, w_in, w_out)
+
+
+def line_peers(parts):
+    total, me = lax.axis_size("seq"), lax.axis_index("seq")
+    return [{"seq": lax.rem(me + parts, total)}, {"seq": lax.rem(me - parts + total, total)}]
+
+
+def pass_on(parts, up, down, sems):
+    me = lax.axis_index("seq")
+    z = lax.div(me, parts)
+
+    def copy(n, src, dst, step):
+        return pltpu.make_async_remote_copy(
+            src, dst, sems.at[0, n], sems.at[1, n], device_id={"seq": me + step}, device_id_type=MESH
+        )
+
+    legs = [(0, *up, parts), (1, *down, -parts)]
+    for n, low, high, src, dst, step in legs:
+
+        @pl.when(jnp.logical_and(z >= low, z <= high))
+        def _():
+            copy(n, src, dst, step).start()
+
+    def end():
+        for n, low, high, src, dst, step in legs:
+            move = 1 if step > 0 else -1
+
+            @pl.when(jnp.logical_and(z >= low, z <= high))
+            def _():
+                copy(n, src, dst, step).wait_send()
+
+            @pl.when(jnp.logical_and(z >= low + move, z <= high + move))
+            def _():
+                copy(n, src, dst, -step).wait_recv()
+
+    return end
+
+
+def exchange_kernel(
+    seqs, in_ref, before_ref, after_ref, out_ref, before_out, after_out, send, recv, local, line_sems
+):
+    across = lax.axis_size("wide")
+    parts = lax.axis_size("seq") // seqs
+    me = lax.axis_index("wide")
     own = in_ref.shape[0]
-    count = in_ref.shape[1] // total
-    meet([{axis: lax.rem(me + k, total)} for k in range(1, total)])
+    count = in_ref.shape[1] // across
+    meet([{"wide": lax.rem(me + k, across)} for k in range(1, across)] + line_peers(parts))
+    line_end = pass_on(
+        parts, (1, seqs - 2, before_ref.at[0], before_out), (1, seqs - 2, after_ref.at[0], after_out), line_sems
+    )
     copies = []
     mine = pl.ds(me * count, count)
     for n in range(own):
-        for k in range(1, total):
-            to = lax.rem(me + k, total)
+        for k in range(1, across):
+            to = lax.rem(me + k, across)
             copies.append(
                 remote(
                     in_ref.at[n, pl.ds(to * count, count)],
                     out_ref.at[n, mine],
                     send.at[n, k - 1],
                     recv.at[n, k - 1],
-                    {axis: to},
+                    {"wide": to},
                 )
             )
     kept = [pltpu.make_async_copy(in_ref.at[n, mine], out_ref.at[n, mine], local.at[n]) for n in range(own)]
@@ -514,34 +571,46 @@
         copy.start()
     for copy in kept + copies:
         copy.wait()
-
-
-def exchange(rows, axis):
-    total = lax.axis_size(axis)
+    line_end()
+
+
+def exchange(rows, before, after, seqs):
+    across = lax.axis_size("wide")
     own = rows.shape[0]
-    vmem = pl.BlockSpec(memory_space=pltpu.VMEM)
+    vmem, hbm = pl.BlockSpec(memory_space=pltpu.VMEM), pl.BlockSpec(memory_space=pl.ANY)
+    one = jax.ShapeDtypeStruct(before.shape[1:], before.dtype)
     return pl.pallas_call(
-        functools.partial(exchange_kernel, axis),
-        in_specs=[vmem],
-        out_specs=pl.BlockSpec(memory_space=pl.ANY),
-        out_shape=jax.ShapeDtypeStruct(rows.shape, rows.dtype),
+        functools.partial(exchange_kernel, seqs),
+        in_specs=[vmem, hbm, hbm],
+        out_specs=[hbm, hbm, hbm],
+        out_shape=[jax.ShapeDtypeStruct(rows.shape, rows.dtype), one, one],
         scratch_shapes=[
-            pltpu.SemaphoreType.DMA((own, total - 1)),
-            pltpu.SemaphoreType.DMA((own, total - 1)),
+            pltpu.SemaphoreType.DMA((own, across - 1)),
+            pltpu.SemaphoreType.DMA((own, across - 1)),
             pltpu.SemaphoreType.DMA((own,)),
+            pltpu.SemaphoreType.DMA((2, 2)),
         ],
         compiler_params=pltpu.CompilerParams(collective_id=4, has_side_effects=True, vmem_limit_bytes=62 << 20),
         name="exchange",
-    )(rows)
+    )(rows, before, after)
 
 
 def experts_kernel(
     block,
+    seqs,
     rows_ref,
     cot_ref,
+    router_ref,
     in_ref,
     out_ref,
+    line_ref,
+    before_ref,
+    after_ref,
     back_ref,
+    before_out,
+    after_out,
+    line_before,
+    line_after,
     done,
     grads,
     forward,
@@ -552,6 +621,7 @@
     back_recv,
     local,
     held_sems,
+    line_sems,
 ):
     own, rows, double = back_ref.shape
     width = double // 2
@@ -570,11 +640,21 @@
 
     for copy in load(0):
         copy.start()
-    meet([{"wide": lax.rem(me + k, across)} for k in range(1, across)])
+    parts = lax.axis_size("seq") // seqs
+    meet([{"wide": lax.rem(me + k, across)} for k in range(1, across)] + line_peers(parts))
+    line_ends = [
+        pass_on(
+            parts,
+            (1, seqs - 2, before_ref.at[1], before_out),
+            (1, seqs - 2, after_ref.at[1], after_out),
+            line_sems.at[0],
+        ),
+        pass_on(parts, (0, seqs - 2, line_ref, line_before), (1, seqs - 1, line_ref, line_after), line_sems.at[1]),
+    ]
     coming = []
     mine = pl.ds(me * count, count)
     for e in range(own):
-        grads[...] = gated(rows_ref[e], cot_ref[e])[1]
+        grads[...] = gated(rows_ref[e], cot_ref[e], router_ref[...], me * own + e)
         forward[...] = jnp.zeros_like(forward)
         backward[...] = jnp.zeros_like(backward)
 
@@ -589,7 +669,7 @@
 
             for copy in load(at):
                 copy.wait()
-            hidden, slope = activation(contract(rows_ref[e, :, :width], in_held[slot], 1, 0))
+            hidden, slope = activation(contract(rows_ref[e], in_held[slot], 1, 0))
             grad_hidden = contract(grads[...], out_held[slot], 1, 1).astype(BF16).astype(F32)
             forward[...] += contract(hidden.astype(BF16), out_held[slot], 1, 0)
             backward[...] += contract((grad_hidden * slope).astype(BF16), in_held[slot], 1, 1)
@@ -614,19 +694,25 @@
         kept.wait()
     for copy in coming:
         copy.wait()
-
-
-def run_experts(rows, cots, w_in, w_out, block):
+    for end in line_ends:
+        end()
+
+
+def run_experts(rows, cots, router, w_in, w_out, before, after, seqs, block):
     own, count, width = cots.shape
     units = w_in.shape[2]
     across = lax.axis_size("wide")
     vmem, hbm = pl.BlockSpec(memory_space=pltpu.VMEM), pl.BlockSpec(memory_space=pl.ANY)
     sems = pltpu.SemaphoreType.DMA
     return pl.pallas_call(
-        functools.partial(experts_kernel, block),
-        in_specs=[vmem, vmem, hbm, hbm],
-        out_specs=vmem,
-        out_shape=jax.ShapeDtypeStruct((own, count, 2 * width), BF16),
+        functools.partial(experts_kernel, block, seqs),
+        in_specs=[vmem, vmem, vmem, hbm, hbm, hbm, hbm, hbm],
+        out_specs=[vmem, hbm, hbm, hbm, hbm],
+        out_shape=[
+            jax.ShapeDtypeStruct((own, count, 2 * width), BF16),
+            *[jax.ShapeDtypeStruct(before.shape[1:], BF16)] * 2,
+            *[jax.ShapeDtypeStruct(rows.shape, BF16)] * 2,
+        ],
         scratch_shapes=[
             pltpu.VMEM((own, count, 2 * width), BF16),
             pltpu.VMEM((count, width), BF16),
@@ -638,16 +724,17 @@
             sems((own, across - 1)),
             sems((own,)),
             sems((2, 2)),
+            sems((2, 2, 2)),
         ],
         compiler_params=pltpu.CompilerParams(collective_id=5, has_side_effects=True, vmem_limit_bytes=62 << 20),
         cost_estimate=pl.CostEstimate(
             flops=8 * own * count * width * units, bytes_accessed=4 * own * width * units, transcendentals=own * count * units
         ),
         name="experts",
-    )(rows, cots, w_in, w_out)
-
-
-def share_kernel(share_ref, rows_ref, cot_ref, in_ref, out_ref, *refs):
+    )(rows, cots, router, w_in, w_out, rows, before, after)
+
+
+def share_kernel(expert, share_ref, rows_ref, cot_ref, router_ref, in_ref, out_ref, *refs):
     grad_in_ref, grad_out_ref, flipped, total_in = refs[-4:]
     step = pl.program_id(0)
 
@@ -657,7 +744,9 @@
         total_in[...] = jnp.zeros_like(total_in)
         grad_out_ref[...] = jnp.zeros_like(grad_out_ref)
 
-    rows, grads = gated(rows_ref[0], cot_ref[0])
+    rows = rows_ref[0]
+    own = router_ref.shape[1] // lax.axis_size("wide")
+    grads = gated(rows, cot_ref[0], router_ref[...], lax.axis_index("wide") * own + expert)
     hidden, slope = activation(contract(flipped[...], rows, 1, 1))
     grad_hidden = contract(out_ref[0], grads, 1, 1).astype(BF16).astype(F32)
     grad_out_ref[0] += contract(hidden.astype(BF16), grads, 1, 0)
@@ -668,7 +757,7 @@
         grad_in_ref[0] = total_in[...].T
 
 
-def run_share(me, rows, cots, w_in, w_out, expert, held):
+def run_share(me, rows, cots, router, w_in, w_out, expert, held):
     own, width, units = w_in.shape
     sources, count = rows.shape[0] // own, rows.shape[1]
     share = units // sources
@@ -684,13 +773,14 @@
         out_spec = pl.BlockSpec((1, share, width), lambda r, at: (expert, 0, 0))
     held_specs = [pl.BlockSpec(memory_space=pl.ANY)] * len(held)
     return pl.pallas_call(
-        share_kernel,
+        functools.partial(share_kernel, expert),
         grid_spec=pltpu.PrefetchScalarGridSpec(
             num_scalar_prefetch=1,
             grid=(sources,),
             in_specs=[
                 pl.BlockSpec((1, count, rows.shape[2]), lambda r, at: (own * r + expert, 0, 0)),
                 pl.BlockSpec((1, count, width), lambda r, at: (own * r + expert, 0, 0)),
+                pl.BlockSpec(router.shape, lambda r, at: (0, 0)),
                 in_spec,
                 out_spec,
                 *held_specs,
@@ -705,13 +795,13 @@
             jax.ShapeDtypeStruct((own, width, share), F32),
             jax.ShapeDtypeStruct((own, share, width), F32),
         ],
-        input_output_aliases={5 + i: i for i in range(len(held))},
+        input_output_aliases={6 + i: i for i in range(len(held))},
         compiler_params=pltpu.CompilerParams(vmem_limit_bytes=62 << 20),
         cost_estimate=pl.CostEstimate(
             flops=8 * sources * count * width * share, bytes_accessed=4 * sources * count * width, transcendentals=0
         ),
         name="share",
-    )(where, rows, cots, w_in, w_out, *held)
+    )(where, rows, cots, router, w_in, w_out, *held)
 
 
 def spread_kernel(parts, in_ref, out_ref, send, recv, pass_send, pass_recv, local):
@@ -807,7 +897,7 @@
     peers += [{"wide": lax.rem(row + k, across)} for k in range(1, across)]
     meet(peers)
     sent = []
-    for k in range(total - 1, 0, -1):
+    for k in range(1, total):
         to = twist(me, k, total)
         sent.append(remote(in_ref.at[to], all_ref.at[me, lax.rem(to, parts)], send.at[to], recv.at[me], {"seq": to}))
     kept = pltpu.make_async_copy(in_ref.at[me], all_ref.at[me, part], local.at[0])
@@ -891,16 +981,16 @@
     return pl.pallas_call(
         functools.partial(begin_kernel, capacity),
         in_specs=[vmem] * 8,
-        out_specs=[vmem] * 5,
+        out_specs=[vmem] * 6,
         out_shape=[
             jax.ShapeDtypeStruct((total, 2, rows, width), BF16),
             jax.ShapeDtypeStruct((3, heads, size, length), BF16),
             jax.ShapeDtypeStruct((width, length), BF16),
             jax.ShapeDtypeStruct((tokens, slots), BF16),
             jax.ShapeDtypeStruct((own, across * capacity, width), BF16),
+            jax.ShapeDtypeStruct((3 * heads * size, width), BF16),
         ],
         scratch_shapes=[
-            pltpu.VMEM((3 * heads * size, width), BF16),
             pltpu.VMEM((own, across * capacity, width), BF16),
             sems((total,)),
             sems((total,)),
@@ -926,17 +1016,48 @@
     early_ref,
     tiny_ref,
     table_ref,
-    rows_ref,
-    cots_ref,
+    router_ref,
+    *refs,
+):
+    own, steps = 2, 2 * seqs - 1
+    rows_refs = refs[: steps - 2]
+    cots_refs = refs[steps - 2 : steps - 2 + 3 + own * (steps - 3)]
+    finish_rest(
+        seqs,
+        rows_refs,
+        cots_refs,
+        three_ref,
+        flip_ref,
+        weight_ref,
+        x_ref,
+        gain_ref,
+        early_ref,
+        tiny_ref,
+        table_ref,
+        router_ref,
+        *refs[len(rows_refs) + len(cots_refs) :],
+    )
+
+
+def finish_rest(
+    seqs,
+    rows_refs,
+    cots_refs,
+    three_ref,
+    flip_ref,
+    weight_ref,
+    x_ref,
+    gain_ref,
+    early_ref,
+    tiny_ref,
+    table_ref,
+    router_ref,
     in_ref,
     out_ref,
     home_ref,
-    query_out,
-    key_out,
-    value_out,
-    output_out,
-    tiny_out,
-    table_out,
+    late_all,
+    early_all,
+    tiny,
     grad_in_ref,
     grad_out_ref,
     grads,
@@ -949,12 +1070,7 @@
     early_got,
     mine,
     early_mine,
-    late_all,
-    early_all,
-    tiny,
     tiny_got,
-    table,
-    table_got,
     rows_held,
     cots_held,
     in_held,
@@ -972,8 +1088,8 @@
     last_sems,
     last_early_sems,
     tiny_sems,
-    table_sems,
     held_sems,
+    line_sems,
     local,
 ):
     total, across = lax.axis_size("seq"), lax.axis_size("wide")
@@ -1005,21 +1121,50 @@
     for copy in weights:
         copy.start()
 
-    def load(e):
-        return (
-            pltpu.make_async_copy(rows_ref.at[:, e], rows_held.at[e], held_sems.at[0, e]),
-            pltpu.make_async_copy(cots_ref.at[:, e], cots_held.at[e], held_sems.at[1, e]),
-        )
-
+    def load_rows(e, n, k):
+        return pltpu.make_async_copy(rows_refs[k].at[e], rows_held.at[e, n], held_sems.at[0, e, n])
+
+    def load_cots(e, n, k):
+        src = cots_refs[k].at[e] if k < 3 else cots_refs[3 + own * (k - 3) + e]
+        return pltpu.make_async_copy(src, cots_held.at[e, n], held_sems.at[1, e, n])
+
+    last_place = seqs - 1
+    far_end = jnp.logical_or(seq == 0, seq == last_place)
     for e in range(own):
-        for copy in load(e):
-            copy.start()
+        load_rows(e, 0, 0).start()
+        load_cots(e, 0, 0).start()
+        for here in range(seqs):
+
+            @pl.when(seq == here)
+            def _():
+                sources = [2 * k - 1 for k in range(1, here + 1)] + [2 * k for k in range(1, seqs - here)]
+                for n, k in enumerate(sources):
+                    load_cots(e, n + 1, k).start()
+                    if k < len(rows_refs):
+                        load_rows(e, n + 1, k).start()
 
     pairs = [(a, b) for a in range(across) for b in range(parts) if a or b]
     peers = [{"seq": lax.rem(me + k, total)} for k in range(1, total)]
     peers += [{"wide": row_at(k)} for k in range(1, across)]
     peers += [{"wide": row_at(a), "seq": part_at(b)} for a, b in pairs if a and b]
     meet(peers)
+
+    def far_rows(e, up):
+        src = rows_refs[3 if up else 4].at[e]
+        to = lax.rem(me + (parts if up else total - parts), total)
+        return pltpu.make_async_remote_copy(
+            src, rows_held.at[e, last_place], line_sems.at[0, e], line_sems.at[1, e], device_id={"seq": to}, device_id_type=MESH
+        )
+
+    for e in range(own):
+
+        @pl.when(seq == last_place - 1)
+        def _():
+            far_rows(e, True).start()
+
+        @pl.when(seq == 1)
+        def _():
+            far_rows(e, False).start()
 
     late = contract(flip_ref[...], three_ref[...], 1, 0).astype(BF16)
     gw[...] = late.reshape(gw.shape)
@@ -1032,7 +1177,7 @@
     gain_grad = jnp.zeros((1, width), F32)
     near_copies = []
     for n in range(2):
-        scaled = contract(three_ref[n * half : (n + 1) * half, :], weight_ref[...], 1, 1)
+        scaled = contract(three_ref[n * half : (n + 1) * half, :], weight_ref[...], 1, 0)
         x = x_ref[n * total // 2 : (n + 1) * total // 2].reshape(half, width).astype(F32)
         inverse = inverse_rms(x)
         gain_grad = gain_grad + jnp.sum(scaled * x * inverse, axis=0, keepdims=True)
@@ -1050,25 +1195,25 @@
                 {"seq": other},
             )
         )
+    lines = tiny_ref.shape[0]
     first = lax.broadcasted_iota(jnp.int32, tiny_ref.shape, 0) == 0
-    tiny[...] = jnp.where(first, gain_grad, tiny_ref[...]).astype(BF16)
-    table[...] = table_ref[...].astype(BF16)
+    tiny[:lines, :] = jnp.where(first, gain_grad, tiny_ref[...]).astype(BF16)
+    table = table_ref[...]
+    tiny[lines:, :] = jnp.concatenate([table, jnp.zeros((table.shape[0], width - table.shape[1]), F32)], axis=1).astype(BF16)
 
     def pass_tiny(stage, wheres):
-        copies = []
-        for n, where in enumerate(wheres):
-            for src, dst, sem in ((tiny, tiny_got, tiny_sems), (table, table_got, table_sems)):
-                copies.append(remote(src, dst.at[stage, n], sem.at[0, stage, n], sem.at[1, stage, n], where))
-        return copies
+        return [
+            remote(tiny, tiny_got.at[stage, n], tiny_sems.at[0, stage, n], tiny_sems.at[1, stage, n], where)
+            for n, where in enumerate(wheres)
+        ]
 
     def take_tiny(stage, copies):
         for copy in copies:
             copy.wait()
-        for src, dst in ((tiny, tiny_got), (table, table_got)):
-            value = src[...].astype(F32)
-            for n in range(len(copies) // 2):
-                value = value + dst[stage, n].astype(F32)
-            src[...] = value.astype(BF16)
+        value = tiny[...].astype(F32)
+        for n in range(len(copies)):
+            value = value + tiny_got[stage, n].astype(F32)
+        tiny[...] = value.astype(BF16)
 
     tiny_copies = pass_tiny(0, [{"wide": row_at(k)} for k in range(1, across)])
     for copy in near_copies:
@@ -1090,28 +1235,40 @@
     other_rows = pl.ds(pl.multiple_of((1 - part) * share, LANES), share)
 
     def share_turn(e, n):
-        if n == 0:
-            for copy in load(e):
-                copy.wait()
         some = rows_held.shape[1] // 2
+        for m in range(n * some, (n + 1) * some):
+            load_cots(e, m, 0).wait()
+            if m < last_place:
+                load_rows(e, m, 0).wait()
+            else:
+
+                @pl.when(far_end)
+                def _():
+                    far_rows(e, True).wait_recv()
+
+                @pl.when(jnp.logical_not(far_end))
+                def _():
+                    load_rows(e, m, 0).wait()
+
         count = some * rows_held.shape[2]
         here = slice(n * some, (n + 1) * some)
-        rows, cots = gated(rows_held[e, here].reshape(count, -1), cots_held[e, here].reshape(count, width))
+        rows = rows_held[e, here].reshape(count, width)
+        cots = gated(rows, cots_held[e, here].reshape(count, width), router_ref[...], row * own + e)
         hidden, slope = activation(contract(in_held[e].T, rows, 1, 1))
         grad_hidden = contract(out_held[e], cots, 1, 1).astype(BF16).astype(F32)
         part_out = contract(hidden.astype(BF16), cots, 1, 0)
         part_in = contract((grad_hidden * slope).astype(BF16), rows, 1, 0)
         if n == 0:
-            sums[0] = part_out
-            sums[1] = part_in
+            sums[e, 0] = part_out
+            sums[e, 1] = part_in
             return []
-        sums[0] += part_out
-        sums[1] += part_in
-        grad_out_ref[e] = sums[0, mine_rows, :]
-        total_in[e] = sums[1, mine_rows, :]
+        sums[e, 0] += part_out
+        sums[e, 1] += part_in
+        grad_out_ref[e] = sums[e, 0, mine_rows, :]
+        total_in[e] = sums[e, 1, mine_rows, :]
         copies = []
         for k in range(2):
-            leaving[e, k] = sums[k, other_rows, :].astype(BF16)
+            leaving[e, k] = sums[e, k, other_rows, :].astype(BF16)
             copies.append(
                 remote(leaving.at[e, k], share_got.at[e, k], share_sems.at[0, e, k], share_sems.at[1, e, k], {"seq": other})
             )
@@ -1124,7 +1281,7 @@
         grad_in_ref[e] = (total_in[e] + share_got[e, 1].astype(F32)).T
 
     share_turn(0, 0)
-    first_share = share_turn(0, 1)
+    share_turn(1, 0)
     take_tiny(0, tiny_copies)
     for copy in wide_copies:
         copy.wait_recv()
@@ -1146,8 +1303,7 @@
                 remote(early_ref.at[place], early_got.at[k - 1], early_sems.at[0, k - 1], early_sems.at[1, k - 1], where)
             )
     tiny_copies = pass_tiny(1, [{"seq": seq_at(k)} for k in range(1, seqs)])
-    share_turn(1, 0)
-    share_end(0, first_share)
+    first_share = share_turn(0, 1)
     take_tiny(1, tiny_copies)
     for copy in far_copies:
         copy.wait_recv()
@@ -1186,49 +1342,41 @@
     for copy in stay:
         copy.start()
     second_share = share_turn(1, 1)
+    share_end(0, first_share)
     take_tiny(2, last[:count])
     share_end(1, second_share)
+    for e in range(own):
+
+        @pl.when(jnp.logical_or(seq == 1, seq == last_place - 1))
+        def _():
+            far_rows(e, True).wait_send()
+
     for copy in last[count:] + stay + home_copies + [kept]:
         copy.wait()
     for copy in wide_copies + far_copies:
         copy.wait_send()
-    for a in range(across):
-        here = slice(a * slim, (a + 1) * slim)
-        for p in range(parts):
-            for n, ref in enumerate((query_out, key_out, value_out)):
-                ref[here, p * cols : (p + 1) * cols] = late_all[a, p, :, n * cols : (n + 1) * cols].astype(F32)
-        output_out[here, :] = early_all[a].astype(F32)
-    piece = tiny_out.shape[1]
-    chosen = lax.broadcasted_iota(jnp.int32, (width, piece), 0) == (
-        lax.broadcasted_iota(jnp.int32, (width, piece), 1) + me * piece
-    )
-    tiny_out[...] = contract(tiny[...], chosen.astype(F32).astype(BF16), 1, 0)
-    lines = table_out.shape[0]
-    chosen = lax.broadcasted_iota(jnp.int32, (lines, table.shape[0]), 1) == (
-        lax.broadcasted_iota(jnp.int32, (lines, table.shape[0]), 0) + me * lines
-    )
-    table_out[...] = contract(chosen.astype(F32).astype(BF16), table[...], 1, 0)
-
-
-def finish(three, flipped, weights, x, gain, early, tiny, table, rows, cots, w_in, w_out):
-    length, columns = three.shape
+
+
+def finish(three, flipped, weights, x, gain, early, tiny, table, router, rows, cots, w_in, w_out):
+    columns = three.shape[1]
     total, parts, piece, width = x.shape
     seqs, slim, _ = early.shape
     across = lax.axis_size("wide")
     own, _, units = w_in.shape
-    share, part = units // total, width // total
+    share = units // total
     vmem, hbm = pl.BlockSpec(memory_space=pltpu.VMEM), pl.BlockSpec(memory_space=pl.ANY)
     sems = pltpu.SemaphoreType.DMA
     most = max(across, seqs, parts) - 1
+    lines = tiny.shape[0] + table.shape[0]
     return pl.pallas_call(
         functools.partial(finish_kernel, seqs),
-        in_specs=[vmem] * 8 + [hbm] * 4,
-        out_specs=[vmem] * 9,
+        in_specs=[vmem] * 9 + [hbm] * (len(rows) + len(cots) + 2),
+        out_specs=[vmem] * 6,
         out_shape=[
             jax.ShapeDtypeStruct((total, piece, width), BF16),
-            *[jax.ShapeDtypeStruct((part, width), F32)] * 4,
-            jax.ShapeDtypeStruct((tiny.shape[0], part), F32),
-            jax.ShapeDtypeStruct((table.shape[0] // total, LANES), F32),
+            jax.ShapeDtypeStruct((across, parts, slim, columns), BF16),
+            jax.ShapeDtypeStruct((across, slim, width), BF16),
+            jax.ShapeDtypeStruct((lines, width), BF16),
             jax.ShapeDtypeStruct((own, width, share), F32),
             jax.ShapeDtypeStruct((own, share, width), F32),
         ],
@@ -1243,17 +1391,12 @@
             pltpu.VMEM((seqs - 1, slim, width), BF16),
             pltpu.VMEM((parts, slim, columns), BF16),
             pltpu.VMEM((slim, width), BF16),
-            pltpu.VMEM((across, parts, slim, columns), BF16),
-            pltpu.VMEM((across, slim, width), BF16),
-            pltpu.VMEM(tiny.shape, BF16),
-            pltpu.VMEM((3, most, *tiny.shape), BF16),
-            pltpu.VMEM(table.shape, BF16),
-            pltpu.VMEM((3, most, *table.shape), BF16),
-            pltpu.VMEM((own, seqs, *rows.shape[2:]), BF16),
-            pltpu.VMEM((own, seqs, *cots.shape[2:]), BF16),
+            pltpu.VMEM((3, most, lines, width), BF16),
+            pltpu.VMEM((own, seqs, *rows[0].shape[1:]), BF16),
+            pltpu.VMEM((own, seqs, *cots[0].shape[1:]), BF16),
             pltpu.VMEM((own, width, 2 * share), BF16),
             pltpu.VMEM((own, 2 * share, width), BF16),
-            pltpu.VMEM((2, 2 * share, width), F32),
+            pltpu.VMEM((own, 2, 2 * share, width), F32),
             pltpu.VMEM((own, share, width), F32),
             pltpu.VMEM((own, 2, share, width), BF16),
             pltpu.VMEM((own, 2, share, width), BF16),
@@ -1266,14 +1409,96 @@
             sems((2, across * parts - 1)),
             sems((2, across - 1)),
             sems((2, 3, most)),
-            sems((2, 3, most)),
+            sems((2, own, seqs)),
             sems((2, own)),
             sems((5,)),
         ],
         compiler_params=pltpu.CompilerParams(collective_id=1, has_side_effects=True, vmem_limit_bytes=62 << 20),
         cost_estimate=pl.CostEstimate(flops=16 << 30, bytes_accessed=60 << 20, transcendentals=0),
         name="finish",
-    )(three, flipped, weights, x, gain, early, tiny, table, rows, cots, w_in, w_out)
+    )(three, flipped, weights, x, gain, early, tiny, table, router, *rows, *cots, w_in, w_out)
+
+
+def close_kernel(
+    heads,
+    home_ref,
+    middle_ref,
+    late_ref,
+    early_ref,
+    tiny_ref,
+    in_ref,
+    out_ref,
+    inputs_ref,
+    query_ref,
+    key_ref,
+    value_ref,
+    output_ref,
+    gain_one_ref,
+    gain_two_ref,
+    router_ref,
+    table_ref,
+    grad_in_ref,
+    grad_out_ref,
+    sems,
+):
+    copies = [
+        pltpu.make_async_copy(in_ref, grad_in_ref, sems.at[0]),
+        pltpu.make_async_copy(out_ref, grad_out_ref, sems.at[1]),
+    ]
+    for copy in copies:
+        copy.start()
+    me = lax.axis_index("seq")
+    across, parts, slim, columns = late_ref.shape
+    cols = columns // 3
+    inputs_ref[...] = middle_ref[...] + home_ref[...].reshape(middle_ref.shape).astype(F32)
+    for a in range(across):
+        here = slice(a * slim, (a + 1) * slim)
+        for p in range(parts):
+            for n, ref in enumerate((query_ref, key_ref, value_ref)):
+                ref[here, p * cols : (p + 1) * cols] = late_ref[a, p, :, n * cols : (n + 1) * cols].astype(F32)
+        output_ref[here, :] = early_ref[a].astype(F32)
+    width, piece = tiny_ref.shape[1], gain_one_ref.shape[1]
+    chosen = lax.broadcasted_iota(jnp.int32, (width, piece), 0) == (
+        lax.broadcasted_iota(jnp.int32, (width, piece), 1) + me * piece
+    )
+    picked = contract(tiny_ref[...], chosen.astype(F32).astype(BF16), 1, 0)
+    gain_one_ref[...] = picked[0:1]
+    gain_two_ref[...] = picked[1:2]
+    router_ref[...] = picked[2 : 2 + router_ref.shape[0]]
+    lines = table_ref.shape[0]
+    chosen = lax.broadcasted_iota(jnp.int32, (lines, LANES), 1) == (
+        lax.broadcasted_iota(jnp.int32, (lines, LANES), 0) + me * lines
+    )
+    table_ref[...] = contract(chosen.astype(F32).astype(BF16), tiny_ref[16:, :LANES], 1, 1)[:, :heads]
+    for copy in copies:
+        copy.wait()
+
+
+def close(home, middle, late, early, tiny, grad_in, grad_out, heads, buckets, experts):
+    across, parts, slim, columns = late.shape
+    width = early.shape[2]
+    total = home.shape[0]
+    rows = across * slim
+    vmem, hbm = pl.BlockSpec(memory_space=pltpu.VMEM), pl.BlockSpec(memory_space=pl.ANY)
+    shapes = [
+        middle.shape,
+        *[(rows, width)] * 4,
+        (1, width // total),
+        (1, width // total),
+        (experts, width // total),
+        (buckets // total, heads),
+        grad_in.shape,
+        grad_out.shape,
+    ]
+    return pl.pallas_call(
+        functools.partial(close_kernel, heads),
+        in_specs=[vmem] * 5 + [hbm] * 2,
+        out_specs=[vmem] * 9 + [hbm] * 2,
+        out_shape=[jax.ShapeDtypeStruct(shape, F32) for shape in shapes],
+        scratch_shapes=[pltpu.SemaphoreType.DMA((2,))],
+        compiler_params=pltpu.CompilerParams(vmem_limit_bytes=62 << 20),
+        name="close",
+    )(home, middle, late, early, tiny, grad_in, grad_out)
 
 
 def ring_pairs(total, parts, shift):
@@ -1292,6 +1517,14 @@
     for k in range(1, parts):
         near.append(lax.ppermute(pick(pieces, (part + k) % parts), "seq", ring_pairs(total, parts, k)))
     return [pick(near, (part - j) % parts) for j in range(parts)]
+
+
+def line_step(before, after, seqs, step):
+    total = lax.axis_size("seq")
+    parts = total // seqs
+    up = [(i, i + parts) for i in range(total - parts) if i // parts >= step - 1]
+    down = [(i, i - parts) for i in range(parts, total) if i // parts <= seqs - step]
+    return [lax.ppermute(before, "seq", up), lax.ppermute(after, "seq", down)]
 
 
 def per_device(
@@ -1329,18 +1562,15 @@
     gain_one = gain_attn.astype(F32)
     gain_two = gain_ffn.astype(F32)
 
-    fast = parts == 2 and capacity % 16 == 0 and own_experts == 2 and seqs % 2 == 0 and cols % LANES == 0 and local_len == LANES
+    fast = parts == 2 and capacity % 16 == 0 and own_experts == 2 and seqs == 4 and cols % LANES == 0 and local_len == LANES
     flat_cot = cotangent.reshape(tokens, width)
     chosen = routes.reshape(tokens)
     blocks = inputs.reshape(total, local_len // parts, width)
-    own_weights = jnp.concatenate(
-        [lax.dynamic_slice(w, (0, part * cols), (width, cols)) for w in (w_query, w_key, w_value)], axis=1
-    )
 
     if fast:
         first_slot = [(e % own_experts) * (across * capacity) + (e // own_experts) * capacity for e in range(experts)]
         base = jnp.array(first_slot + [0] * (LANES - experts), F32)[None]
-        seq_in, qkv, flipped, slot_hot, cot_rows = begin(
+        seq_in, qkv, flipped, slot_hot, cot_rows, own_weights = begin(
             blocks,
             w_query,
             w_key,
@@ -1355,6 +1585,9 @@
             capacity,
         )
     else:
+        own_weights = jnp.concatenate(
+            [lax.dynamic_slice(w, (0, part * cols), (width, cols)) for w in (w_query, w_key, w_value)], axis=1
+        )
         seq_in = spread(blocks, parts).reshape(length, width).astype(F32)
         inv_one = inverse_rms(seq_in)
         normed_one = (seq_in * inv_one * gain_one).astype(BF16)
@@ -1371,11 +1604,9 @@
         packed = contract(slot_hot, flat_cot, 0, 0).astype(BF16).reshape(own_experts, across, capacity, width)
         cot_rows = jnp.stack([lax.all_to_all(packed[e], "wide", 0, 0, tiled=True) for e in range(own_experts)])
         cot_rows = cot_rows.reshape(own_experts, across * capacity, width)
-    rings = [[n * parts + p for n in range(seqs)] for p in range(parts)] if fast else None
-    all_cots = lax.all_gather(cot_rows, "seq", axis=0, axis_index_groups=rings)
     own_table = lax.dynamic_slice(rel_table, (0, part * heads), (buckets, heads))
-    ids = jnp.concatenate([bucket_ids, jnp.full((1,), buckets, jnp.int32)])
-    bucket_hot = (ids[None, :] == jnp.arange(buckets, dtype=jnp.int32)[:, None]).astype(BF16)
+    ids = jnp.concatenate([bucket_ids, jnp.full((1,), LANES, jnp.int32)])
+    bucket_hot = (ids[None, :] == jnp.arange(LANES, dtype=jnp.int32)[:, None]).astype(BF16)
     reverse_hot = (ids[::-1][None, :] == jnp.arange(buckets, dtype=jnp.int32)[:, None]).astype(BF16)
     bias_line = contract(own_table, reverse_hot, 0, 0).reshape(heads, 1, 2 * length)
     outs, attended, exps, inverse = attend(qkv, bias_line, total)
@@ -1389,24 +1620,27 @@
     picked = (chosen[:, None] == jnp.arange(experts, dtype=jnp.int32)[None, :]).astype(F32)
     gate_prob = jnp.sum(router_probs * picked, axis=1)
     upstream = flat_cot.astype(F32)
-    gate_high = gate_prob.astype(BF16)
-    gate_low = (gate_prob - gate_high.astype(F32)).astype(BF16)
-    pad = jnp.zeros((tokens, LANES - 2), BF16)
-    both = jnp.concatenate([normed_two, gate_high[:, None], gate_low[:, None], pad], axis=1)
-    packed = contract(slot_hot, both, 0, 0).astype(BF16)
+    packed = contract(slot_hot, normed_two, 0, 0).astype(BF16)
     if fast:
-        received = exchange(packed.reshape(own_experts, across * capacity, width + LANES), "wide")
-        returned = run_experts(received, cot_rows, w_in, w_out, 512).reshape(slots, 2 * width)
+        near_cots = line_step(cot_rows, cot_rows, seqs, 1)
+        received, *second = exchange(
+            packed.reshape(own_experts, across * capacity, width), *near_cots, seqs
+        )
+        returned, *more = run_experts(received, cot_rows, w_router, w_in, w_out, *near_cots, seqs, 512)
+        second = [second[0], more[0], second[1], more[1]]
+        near_rows = more[2:]
+        third = [line_step(second[e], second[2 + e], seqs, 3) for e in range(own_experts)]
+        all_cots = [cot_rows, *near_cots, *second, third[0][0], third[1][0], third[0][1], third[1][1]]
+        returned = returned.reshape(slots, 2 * width)
     else:
-        packed = packed.reshape(own_experts, across, capacity, width + LANES)
+        packed = packed.reshape(own_experts, across, capacity, width)
         received, returned = [], []
         for e in range(own_experts):
-            got = lax.all_to_all(packed[e], "wide", 0, 0, tiled=True).reshape(across * capacity, width + LANES)
+            got = lax.all_to_all(packed[e], "wide", 0, 0, tiled=True).reshape(across * capacity, width)
             received.append(got)
-            pair = run_expert(got, cot_rows[e], w_in, w_out, e, 512).reshape(across, capacity, 2 * width)
+            pair = run_expert(got, cot_rows[e], w_router, w_in, w_out, e, 512).reshape(across, capacity, 2 * width)
             returned.append(lax.all_to_all(pair, "wide", 0, 0, tiled=True).reshape(across * capacity, 2 * width))
         received, returned = jnp.stack(received), jnp.concatenate(returned, axis=0)
-    all_rows = lax.all_gather(received, "seq", axis=0, axis_index_groups=rings)
     token_rows = jnp.dot(slot_hot, returned, preferred_element_type=F32)
     selected, grad_token = token_rows[:, :width], token_rows[:, width:]
     output = (middle + gate_prob[:, None] * selected).astype(BF16).reshape(inputs.shape)
@@ -1423,11 +1657,12 @@
     back = (exps, inverse, grad_branch, w_output.reshape(parts, cols, width), outs, qkv, bucket_hot)
     if fast:
         early = grad_w_output.astype(BF16).reshape(seqs, parts, across, slim, width)
-        three, table, early = attend_back(*back, early)
+        three, table, early, *far_rows = attend_back(*back, early, near_rows)
+        all_rows = [received, *near_rows, *far_rows]
         tiny = jnp.concatenate(
             [jnp.zeros((1, width), F32), grad_gain_two[None], grad_router, jnp.zeros((14 - experts, width), F32)], axis=0
         )
-        home, total_query, total_key, total_value, total_output, tiny, table, grad_w_in, grad_w_out = finish(
+        home, *found = finish(
             three,
             flipped,
             own_weights,
@@ -1436,27 +1671,30 @@
             early,
             tiny,
             table,
+            w_router,
             all_rows,
             all_cots,
             w_in,
             w_out,
         )
+        grad_inputs, *grads_qkvo, grad_gain_one, grad_gain_two, grad_router, grad_table, grad_in, grad_out = close(
+            home, grad_middle, *found, head_count, buckets, experts
+        )
         return (
             output,
-            (grad_middle + home.reshape(tokens, width).astype(F32)).reshape(inputs.shape),
-            tiny[0],
-            total_query,
-            total_key,
-            total_value,
-            total_output,
-            table[:, :head_count],
-            tiny[1],
-            tiny[2 : 2 + experts].T,
-            grad_w_in,
-            grad_w_out,
+            grad_inputs.reshape(inputs.shape),
+            grad_gain_one[0],
+            *grads_qkvo,
+            grad_table,
+            grad_gain_two[0],
+            grad_router.T,
+            grad_in,
+            grad_out,
         )
 
-    three, table = attend_back(*back, None)
+    all_cots = lax.all_gather(cot_rows, "seq", axis=0)
+    all_rows = lax.all_gather(received, "seq", axis=0)
+    three, table = attend_back(*back, None, [])
     grad_normed_one = contract(three, own_weights, 1, 1)
     grad_in_norm, grad_gain_one = norm_backward(seq_in, inv_one, gain_one, grad_normed_one)
     pieces = grad_in_norm.astype(BF16).reshape(total, parts, local_len // parts, width)
@@ -1468,6 +1706,7 @@
     )
     rows = [grad_projections[:, k] for k in range(3)]
     rows += [grad_w_output, grad_gain_one[:, None], grad_gain_two[:, None], grad_router.T]
+    table = table.T[:buckets]
     rows, table = lax.psum((jnp.concatenate(rows, axis=1).astype(BF16), table.astype(BF16)), "wide")
     rows = lax.psum_scatter(rows, "seq", scatter_dimension=0, tiled=True).astype(F32)
     table = lax.psum_scatter(table, "seq", scatter_dimension=0, tiled=True).astype(F32)
@@ -1477,6 +1716,7 @@
             me,
             all_rows.reshape(total * own_experts, *received.shape[1:]),
             all_cots.reshape(total * own_experts, *cot_rows.shape[1:]),
+            w_router,
             w_in,
             w_out,
             e,

time: 326 us -> 441 us (1.35)
  Pallas kernels: 247 us -> 399 us
  waiting for transfers between devices: 16.5 us -> 0.02 us
  between operations: 14.5 us -> 1.18 us
  local copies, waits for them, and re-layouts: 21.2 us -> 8.17 us
  starting transfers between devices: 0.25 us -> 12.4 us
    pallas_call x2 -> x3, Pallas kernels: 47.3 us -> 202 us  [the longest x1 147 us: close(): pl.pallas_call(functools.partial(close_kernel, heads), in_specs=[vmem] *...]
    all_gather x2 -> x0, waiting for transfers between devices: 16.5 us -> none  [the longest x1 16.5 us: per_device(): all_rows = lax.all_gather(received, 'seq', axis=0, axis_index_groups=rings)]
    ppermute x0 -> x6, starting transfers between devices: none -> 12.4 us  [line_step(): return [lax.ppermute(before, 'seq', up), lax.ppermute(after, 'seq', down)]]
    pallas_call x1, Pallas kernels: 59.9 us -> 66.9 us  [finish(): pl.pallas_call(functools.partial(finish_kernel, seqs), in_specs=[vmem] *...]
    unnamed x55 -> x33, local copies, waits for them, and re-layouts: 7.55 us -> 2.16 us
    pallas_call x1, Pallas kernels: 45.2 us -> 40 us  [attend(): pl.pallas_call(attend_kernel, in_specs=[vmem, vmem], out_specs=[vmem, vme...]
    dynamic_slice x2 -> x0, local copies, waits for them, and re-layouts: 4.55 us -> none  [per_device(): lax.dynamic_slice(w, (0, part * cols), (width, cols))]
  transfers between devices with their start and end apart: 2 -> 6, of which waited for: 1 -> 0; matrix products, arithmetic and copies ran while one was open for 8% -> 2% of each run, Pallas kernels for 48% -> 23%
where the time goes in v4:
time: 441 us; the launch traced here: 435 us
  Pallas kernels  399 us (90%)
  starting transfers between devices  12.4 us (3%)
  matrix products  10.4 us (2%)
  local copies, waits for them, and re-layouts  8.17 us (2%)
    pallas_call x1, Pallas kernels, close(): pl.pallas_call(functools.partial(close_kernel, heads), in_specs=[vmem] *...  147 us
    pallas_call x1, Pallas kernels, finish(): pl.pallas_call(functools.partial(finish_kernel, seqs), in_specs=[vmem] *...  66.9 us
    pallas_call x1, Pallas kernels, attend_back(): pl.pallas_call(functools.partial(attend_back_kernel, early is not None),...  60 us
    pallas_call x1, Pallas kernels, attend(): pl.pallas_call(attend_kernel, in_specs=[vmem, vmem], out_specs=[vmem, vme...  40 us
    pallas_call x1, Pallas kernels, run_experts(): pl.pallas_call(functools.partial(experts_kernel, block, seqs), in_specs=[...  37.6 us
    pallas_call x1, Pallas kernels, begin(): pl.pallas_call(functools.partial(begin_kernel, capacity), in_specs=[vmem]...  30.3 us
    pallas_call x1, Pallas kernels, exchange(): pl.pallas_call(functools.partial(exchange_kernel, seqs), in_specs=[vmem,...  16.5 us
    ppermute x6, starting transfers between devices, line_step(): return [lax.ppermute(before, 'seq', up), lax.ppermute(after, 'seq', down)]  12.4 us
  transfers between devices with their start and end apart: 6, of which 0 were waited for; matrix products, arithmetic and copies ran while one was open for 2% of the time, Pallas kernels for 23%

profile of v4, /device:TPU:0, one launch (start us, length us, event | category | flops | bytes accessed | tf_op | source)
XLA Modules:
  0.0 435.2 jit_solution(16652760783776124172)
XLA Ops:
  0.7 1.3 reshape.100.gain_ref
  1.9 1.5 copy.29.routes_ref
  3.5 30.3 %begin.1 = (bf16[8,2,64,768]{3,2,1,0:T(8,128)(2,1)}, bf16[3,6,64,1024]{3,2,1,0:T(8,128)(2,1)}, bf16[768,1024]{1,0:T(8,128)(2,1)}, bf16[512,640]{1,0:T(8,128)(2,1...) custom-call(bf16[8,64,768]{2,1,0:T(8,128)(2,1)} %bitcast.53, bf16[768,768]{1,0:T(8,128)(2,1)} %query_ref.1, ...), custom_call_target="tpu_custom_call" | custom-call | flops 4294967296 | bytes 83886080 | tf_op jit(solution)/shard_map/begin/pallas_call | solution.py:981
  33.8 5.2 %collective-permute-start = (bf16[2,320,768]{2,1,0:T(8,128)(2,1)}, bf16[2,320,768]{2,1,0:T(8,128)(2,1)}, u32[]{:S(2)}, u32[]{:S(2)}) collective-permute-start(bf16[2,320,768]{2,1,0:T(8,128)(2,1)} %get-tuple-element.55.cot_ref.refs_5_), channel_id=1, source_target_pairs={{0,8},{4,12},{8,16},{12,20},{16,24},{20,28},{1,9},{5,13},{9,17},{1... | collective-permute-start | bytes 2949128 | tf_op jit(solution)/shard_map/ppermute | solution.py:1527
  39.0 1.5 collective-permute-start.1
  41.5 40.0 %attend.1 = (bf16[8,6,64,128]{3,2,1,0:T(8,128)(2,1)}, bf16[8,6,64,128]{3,2,1,0:T(8,128)(2,1)}, bf16[4,6,1024,256]{3,2,1,0:T(8,128)(2,1)}, f32[4,6,1,256]{3,2,1,0:T(1,128)}) custom-call(bf16[3,6,64,1024]{3,2,1,0:T(8,128)(2,1)} %get-tuple-element.52.qkv_ref.refs_5_, f32[6,1,2048]{2,1,0:T(1,128)} %reshape.90.bias_ref), custom_call_target="tpu_custom_call" | custom-call | flops 1610612736 | bytes 12582912 | tf_op jit(solution)/shard_map/attend/pallas_call | solution.py:160
  81.5 2.4 copy.30
  83.9 2.3 multiply_reduce_fusion.2
  87.2 0.8 copy.31.router_ref
  88.1 1.7 convolution_convert_fusion
  89.8 0.9 fusion.1.refs_6_
  90.7 16.5 %exchange.1 = (bf16[2,320,768]{2,1,0:T(8,128)(2,1)}, bf16[320,768]{1,0:T(8,128)(2,1)}, bf16[320,768]{1,0:T(8,128)(2,1)}) custom-call(bf16[2,320,768]{2,1,0:T(8,128)(2,1)} %bitcast.43, bf16[2,320,768]{2,1,0:T(8,128)(2,1)} %collective-permute-done.before_ref.refs_6_, bf16[2,320,768]{2,1,0:T(8,128)(2,1)} %collective-permute-done.1.after_ref.refs_7_), custom_call_target="tpu_custom_call" | custom-call | tf_op jit(solution)/shard_map/exchange/pallas_call | solution.py:582
  107.3 37.6 %experts.1 = (bf16[2,320,1536]{2,1,0:T(8,128)(2,1)}, bf16[320,768]{1,0:T(8,128)(2,1)}, bf16[320,768]{1,0:T(8,128)(2,1)}, bf16[2,320,768]{2,1,0:T(8,128)(2,1)}, bf16[2,320,768]{2,1,0:T(8,128)(2,1)}) custom-call(bf16[2,320,768]{2,1,0:T(8,128)(2,1)} %get-tuple-element.56.rows_ref.line_ref.refs_0_, bf16[2,320,768]{2,1,0:T(8,128)(2,1)} %get-tuple-element.55.cot_ref.refs_5_, ...), custom_call_target="tpu_custom_call" | custom-call | flops 12079595520 | bytes 18874368 | tf_op jit(solution)/shard_map/experts/pallas_call | solution.py:707
  144.9 3.2 fusion.11
  148.4 0.8 copy-done.3
  150.2 2.1 fusion.8
  152.4 1.8 bitcast_convert_fusion
  154.1 1.5 collective-permute-start.3
  155.6 1.3 collective-permute-start.5
  156.9 1.5 collective-permute-start.2
  158.4 1.5 collective-permute-start.4
  160.6 60.0 %attend_back.1 = (bf16[1024,1152]{1,0:T(8,128)(2,1)}, f32[16,128]{1,0:T(8,128)}, bf16[4,24,768]{2,1,0:T(8,128)(2,1)}, bf16[2,320,768]{2,1,0:T(8,128)(2,1)}, bf16[2,320,768]{2,1,0:T(8,128)(2,1)}) custom-call(bf16[4,6,1024,256]{3,2,1,0:T(8,128)(2,1)} %get-tuple-element.58.refs_0_, f32[4,6,1,256]{3,2,1,0:T(1,128)} %get-tuple-element.59.refs_1_, ...), custom_call_target="tpu_custom_call" | custom-call | flops 3221225472 | bytes 12582912 | tf_op jit(solution)/shard_map/attend_back/pallas_call | solution.py:418
  220.6 66.9 %finish.1 = (bf16[8,64,768]{2,1,0:T(8,128)(2,1)}, bf16[4,2,24,1152]{3,2,1,0:T(8,128)(2,1)}, bf16[4,24,768]{2,1,0:T(8,128)(2,1)}, bf16[32,768]{1,0:T(8,128)(2,1)}...) custom-call(bf16[1024,1152]{1,0:T(8,128)(2,1)} %get-tuple-element.63.three_ref, ...), custom_call_target="tpu_custom_call" | custom-call | flops 17179869184 | bytes 62914560 | tf_op jit(solution)/shard_map/finish/pallas_call | solution.py:1371
  287.5 147.4 %close.1 = (f32[512,768]{1,0:T(8,128)}, f32[96,768]{1,0:T(8,128)}, f32[96,768]{1,0:T(8,128)}, f32[96,768]{1,0:T(8,128)}, f32[96,768]{1,0:T(8,128)}, /*index=5*/f...) custom-call(bf16[8,64,768]{2,1,0:T(8,128)(2,1)} %get-tuple-element.7, ...), custom_call_target="tpu_custom_call" | custom-call | tf_op jit(solution)/shard_map/close/pallas_call | solution.py:1493
  (56 shorter events, 4.1 us)
Async XLA Ops:
  0.6 40.0 %copy-start = (bf16[32,12]{0,1:T(8,128)(2,1)S(1)}, bf16[32,12]{0,1:T(8,128)(2,1)}, u32[]{:S(2)}) copy-start(bf16[32,12]{0,1:T(8,128)(2,1)} %param.23) | copy-start | bytes 2308
  3.5 37.0 %copy-start.10 = (s32[2047]{0:T(1024)S(1)}, s32[2047]{0:T(1024)}, u32[]{:S(2)}) copy-start(s32[2047]{0:T(1024)} %param.17) | copy-start | bytes 24568
  33.8 56.9 %collective-permute-start = (bf16[2,320,768]{2,1,0:T(8,128)(2,1)}, bf16[2,320,768]{2,1,0:T(8,128)(2,1)}, u32[]{:S(2)}, u32[]{:S(2)}) collective-permute-start(bf16[2,320,768]{2,1,0:T(8,128)(2,1)} %get-tuple-element.55.cot_ref.refs_5_), channel_id=1, source_target_pairs={{0,8},{4,12},{8,16},{12,20},{16,24},{20,28},{1,9},{5,13},{9,17},{1... | collective-permute-start | bytes 2949128 | tf_op jit(solution)/shard_map/ppermute | solution.py:1527
  39.0 51.7 %collective-permute-start.1 = (bf16[2,320,768]{2,1,0:T(8,128)(2,1)}, bf16[2,320,768]{2,1,0:T(8,128)(2,1)}, u32[]{:S(2)}, u32[]{:S(2)}) collective-permute-start(bf16[2,320,768]{2,1,0:T(8,128)(2,1)} %get-tuple-element.55.cot_ref.refs_5_), channel_id=1, source_target_pairs={{8,0},{12,4},{16,8},{20,12},{24,16},{28,20},{9,1},{13,5},{17,9},{2... | collective-permute-start | bytes 2949128 | tf_op jit(solution)/shard_map/ppermute | solution.py:1527
  81.5 2.4 copy-start.6
  83.9 2.3 copy-start.11
  86.1 0.7 copy-start.8
  86.2 1.9 copy-start.9
  86.2 2.0 copy-start.15
  86.8 3.0 copy-start.2
  144.9 3.2 copy-start.5
  148.1 1.1 copy-start.3
  150.2 2.1 copy-start.7
  152.3 1.8 copy-start.4
  152.3 1.8 copy-start.14
  152.3 4.6 %copy-start.12 = (bf16[320,768]{1,0:T(8,128)(2,1)S(1)}, bf16[320,768]{1,0:T(8,128)(2,1)}, u32[]{:S(2)}) copy-start(bf16[320,768]{1,0:T(8,128)(2,1)} %get-tuple-element.71.refs_8_) | copy-start | bytes 1474564
  152.3 6.0 %copy-start.13 = (bf16[320,768]{1,0:T(8,128)(2,1)S(1)}, bf16[320,768]{1,0:T(8,128)(2,1)}, u32[]{:S(2)}) copy-start(bf16[320,768]{1,0:T(8,128)(2,1)} %get-tuple-element.73.refs_10_) | copy-start | bytes 1474564
  154.1 66.4 %collective-permute-start.3 = (bf16[320,768]{1,0:T(8,128)(2,1)S(1)}, bf16[320,768]{1,0:T(8,128)(2,1)}, u32[]{:S(2)}, u32[]{:S(2)}) collective-permute-start(bf16[320,768]{1,0:T(8,128)(2,1)S(1)} %copy-done.14), channel_id=1, source_target_pairs={{16,24},{20,28},{17,25},{21,29},{18,26},{22,30},{19,27},{23,31}} | collective-permute-start | bytes 1474568 | tf_op jit(solution)/shard_map/ppermute | solution.py:1527
  155.6 65.0 %collective-permute-start.5 = (bf16[320,768]{1,0:T(8,128)(2,1)}, bf16[320,768]{1,0:T(8,128)(2,1)}, u32[]{:S(2)}, u32[]{:S(2)}) collective-permute-start(bf16[320,768]{1,0:T(8,128)(2,1)} %get-tuple-element.74.refs_11_), channel_id=1, source_target_pairs={{8,0},{12,4},{9,1},{13,5},{10,2},{14,6},{11,3},{15,7}} | collective-permute-start | bytes 1474568 | tf_op jit(solution)/shard_map/ppermute | solution.py:1527
  156.9 63.7 %collective-permute-start.2 = (bf16[320,768]{1,0:T(8,128)(2,1)S(1)}, bf16[320,768]{1,0:T(8,128)(2,1)}, u32[]{:S(2)}, u32[]{:S(2)}) collective-permute-start(bf16[320,768]{1,0:T(8,128)(2,1)S(1)} %copy-done.12), channel_id=1, source_target_pairs={{16,24},{20,28},{17,25},{21,29},{18,26},{22,30},{19,27},{23,31}} | collective-permute-start | bytes 1474568 | tf_op jit(solution)/shard_map/ppermute | solution.py:1527
  158.4 62.2 %collective-permute-start.4 = (bf16[320,768]{1,0:T(8,128)(2,1)S(1)}, bf16[320,768]{1,0:T(8,128)(2,1)}, u32[]{:S(2)}, u32[]{:S(2)}) collective-permute-start(bf16[320,768]{1,0:T(8,128)(2,1)S(1)} %copy-done.13), channel_id=1, source_target_pairs={{8,0},{12,4},{9,1},{13,5},{10,2},{14,6},{11,3},{15,7}} | collective-permute-start | bytes 1474568 | tf_op jit(solution)/shard_map/ppermute | solution.py:1527
  287.5 147.5 %copy-start.1 = (bf16[32,12]{0,1:T(8,128)(2,1)S(1)}, bf16[32,12]{0,1:T(8,128)(2,1)}, u32[]{:S(2)}) copy-start(bf16[32,12]{0,1:T(8,128)(2,1)} %param.23) | copy-start | bytes 2308
